TPU v7x, 32 devices: a whole 2x2x4 slice. The times are simulated.
32 devices in a mesh: tm: 8 (over z, core), space: 4 (over y, x).
Axes of the slice: x: 2, y: 2, z: 4, core: 2. Of those that a mesh axis runs over, the one named last changes fastest.
Arguments:
- spectrum: float32 [2048], P('space'), may hold values from 4 to 64
- coupling: float32 [64, 2048], P('tm', 'space'), may hold values from 0 to 1, as said below
- spatial_basis: bfloat16 [2048, 2048], P(None, 'space'), may hold values from -0.125 to 0.125
- noise_keys: int32 [64], replicated, may hold values from 0 to 16777215
- noise_counters: int32 [64], replicated, may hold values from 0 to 1048575
Outputs:
- samples: float32 [2048, 4096], P('space', 'tm')
Inputs may be any that keep to these rules, and one draw needn't show every extreme that they name: `coupling`: every entry lies strictly between 0 and 1.
All inputs are finite; a program needn't handle non-finite values.
Results may differ from a plain program's by a relative error of at most 0.015.
Values may be sent and summed in bfloat16 or wider, within the bound.
No kernel may reach another device: no remote copies, remote signals or barrier semaphores. Data moves between devices by JAX's collectives and lax.ppermute only.
A program may use at most 64 MiB of HBM per device.

v0:
```python
import functools

import jax
import jax.numpy as jnp
from jax import lax
from jax.experimental import pallas as pl
from jax.experimental.pallas import tpu as pltpu
from jax.sharding import PartitionSpec as P


F32 = jnp.float32
BF16 = jnp.bfloat16
VMEM = pl.BlockSpec(memory_space=pltpu.VMEM)
ANY = pl.BlockSpec(memory_space=pl.ANY)
HBM = pl.BlockSpec(memory_space=pltpu.HBM)
LIMIT = pltpu.CompilerParams(vmem_limit_bytes=24 << 20)
SINE = (6.28318516, -41.34165503, 81.60100406, -76.54978208, 39.53670436)


def partners(count):
    pairs = [(i, i + 1) for i in range(1, count - 2, 2)]
    return pairs, ([count - 1] if count > 1 else [])


def exchange(x, move):
    tm, space = lax.axis_size("tm"), lax.axis_size("space")
    moves = []
    for t in range(tm):
        for s in range(space):
            to = move(t, s)
            if to is not None:
                moves.append((t * space + s, to[0] * space + to[1]))
    return lax.ppermute(x, ("tm", "space"), moves)


def swap(x, axis, offset):
    count = lax.axis_size(axis)
    return lax.ppermute(x, axis, [(i, i ^ offset) for i in range(count)])


def split3(x):
    high = x.astype(BF16).astype(F32)
    rest = x - high
    middle = rest.astype(BF16).astype(F32)
    return high, middle, rest - middle


def mix_bits(state):
    state = state ^ lax.shift_right_logical(state, jnp.int32(16))
    state = state * jnp.int32(-2048144789)
    state = state ^ lax.shift_right_logical(state, jnp.int32(13))
    state = state * jnp.int32(-1028477387)
    return state ^ lax.shift_right_logical(state, jnp.int32(16))


def gaussian(seeded):
    first = mix_bits(seeded)
    second = mix_bits(first + jnp.int32(1013904223))
    unit = (lax.shift_right_logical(first, jnp.int32(8)).astype(F32) + 0.5) * (1.0 / 16777216.0)
    square = -2.0 * jnp.log(unit)
    radius = square * lax.rsqrt(jnp.maximum(square, 1e-30))
    turn = (lax.shift_right_arithmetic(second, jnp.int32(8)).astype(F32) + 0.5) * (1.0 / 16777216.0)
    w = 0.25 - jnp.abs(turn)
    z = w * w
    sine = SINE[4]
    for c in SINE[3::-1]:
        sine = sine * z + c
    return radius * (sine * w)


TAIL = 64


def pick(core, offsets):
    return offsets[0] if offsets[0] == offsets[1] else jnp.where(core == 0, offsets[0], offsets[1])


def pack_kernel(tm_axis, sp_axis, offsets, coup, spec, basis, *rest):
    *outs, coup_out, spec_out, sems = rest
    me, sp = lax.axis_index(tm_axis), lax.axis_index(sp_axis)
    core = lax.rem(me, 2)
    copies = [
        pltpu.make_async_copy(coup, coup_out, sems.at[len(outs)]),
        pltpu.make_async_copy(spec, spec_out, sems.at[len(outs) + 1]),
    ]
    for i, (out, offset) in enumerate(zip(outs, offsets)):
        rows = out.shape[0] - TAIL
        block = sp ^ pick(core, offset)
        if offset[0] == offset[1]:
            block = block * 2 + core
        start = pl.multiple_of(block * rows, rows)
        copies.append(
            pltpu.make_async_copy(basis.at[pl.ds(start, rows), :], out.at[pl.ds(0, rows), :], sems.at[i])
        )
    for copy in copies:
        copy.start()
    for copy in copies:
        copy.wait()


def totals(ref):
    product = square = total = None
    for t in range(ref.shape[0]):
        c = ref[pl.ds(t, 1), :]
        product = c if t == 0 else product * c
        square = c * c if t == 0 else square * (c * c)
        total = square if t == 0 else total + square
    return product, total


def joined(early, late):
    return early[0] * late[0], early[1] + (early[0] * early[0]) * late[1]


def table_rows(shape, rows):
    row = lax.broadcasted_iota(jnp.int32, shape, 0)
    table = jnp.zeros(shape, F32)
    for j, value in enumerate(rows):
        table = jnp.where(row == j, value, table)
    return table


def ordered(first, mine, theirs):
    early = tuple(jnp.where(first, x, y) for x, y in zip(mine, theirs))
    late = tuple(jnp.where(first, y, x) for x, y in zip(mine, theirs))
    return early, late


def table_kernel(tm_axis, count, coup, other, spec, *rest):
    out, *messages, tail, sems = rest[count:]
    first = lax.rem(lax.axis_index(tm_axis), 2) == 0
    (x,), (y,) = ordered(first, (coup[...],), (other[...],))
    parts = split3(x) + split3(y)
    parts = parts + (table_rows(x.shape, split3(spec[...])), jnp.zeros_like(x))
    for j in range(4):
        tail[pl.ds(16 * j, 16), :] = jnp.concatenate(parts[2 * j : 2 * j + 2], 0).astype(BF16)
    copies = []
    for i, message in enumerate(messages):
        rows = message.shape[0] - TAIL
        copies.append(pltpu.make_async_copy(tail, message.at[pl.ds(rows, TAIL), :], sems.at[i]))
        copies[-1].start()
    early, late = ordered(first, totals(coup), totals(other))
    out[...] = table_rows(out.shape, (*joined(early, late), *early, *late))
    for copy in copies:
        copy.wait()


def noise_kernel(tm_axis, sp_axis, blocks, extras, keys, counters, *rest):
    *outs, base = rest[extras:]
    outs = outs[: len(blocks)]
    steps, vecs, modes = outs[0].shape
    me, sp = lax.axis_index(tm_axis), lax.axis_index(sp_axis)
    diagonal = lax.broadcasted_iota(jnp.int32, (vecs, vecs), 0) == lax.broadcasted_iota(
        jnp.int32, (vecs, vecs), 1
    )

    def column(ref):
        row = jnp.broadcast_to(ref[...].astype(F32), (vecs, vecs))
        return jnp.sum(jnp.where(diagonal, row, 0.0), axis=1, keepdims=True).astype(jnp.int32)

    start = column(keys) * jnp.int32(668265261) + column(counters) * jnp.int32(374761393)
    base[...] = jnp.broadcast_to(start, base.shape)
    group = 8
    for out, (block, offset) in zip(outs, blocks):
        ids = (sp ^ pick(lax.rem(me, 2), offset)) * modes + lax.broadcasted_iota(jnp.int32, (1, modes), 1)
        lane = ids * jnp.int32(-1640531535)
        first_step = (me ^ block) * steps

        def step(t, _):
            shifted = lane + (first_step + t) * jnp.int32(374761393)
            for v in range(vecs // group):
                seeded = jnp.tile(base[pl.ds(v * group, group), :], (1, modes // 128)) + shifted
                out[t, pl.ds(v * group, group), :] = gaussian(seeded)
            return 0

        lax.fori_loop(0, steps, step, 0)


def chain(coup, spec, d_start, f_start):
    before, after = [], []
    square, total = None, None
    d_now = d_start
    for t in range(coup.shape[0]):
        c = coup[t : t + 1, :]
        square = c * c if t == 0 else square * (c * c)
        total = square if t == 0 else total + square
        before.append(d_now)
        d_now = d_start + f_start * total
        after.append(d_now)
    ratio = jnp.concatenate(before, 0) / jnp.concatenate(after, 0)
    return jnp.sqrt(ratio / spec), ratio


def after(start, total):
    return start[0] + start[1] * total[1], start[1] * (total[0] * total[0])


def select(flag, x, y):
    return tuple(jnp.where(flag, p, q) for p, q in zip(x, y))


def gain_of(start, total):
    return total[0] * start[0] / (start[0] + start[1] * total[1])


def offset_kernel(tm_axis, noise, coup, spec, table, *rest):
    received, rest = rest[:-7], rest[-7:]
    o_ref, sent, wts, df, tables, alpha, beta = rest
    steps, vecs, modes = noise.shape
    me = lax.axis_index(tm_axis)
    chip = me // 2
    first = lax.rem(me, 2) == 0
    one = jnp.ones((1, modes), F32)
    tables[chip] = table[...]
    for e, ref in enumerate(received):
        tables[chip ^ (e + 1)] = ref[...]
    now, start, weight = (one, one), (one, one), jnp.zeros((1, modes), F32)
    for b in range(tables.shape[0]):
        wts[b] = jnp.broadcast_to(weight, (8, modes))
        total = tables[b, pl.ds(0, 1), :], tables[b, pl.ds(1, 1), :]
        here = chip == b
        start = select(here, now, start)
        weight = jnp.where(here, 1.0, weight * gain_of(now, total))
        now = after(now, total)
    early = table[pl.ds(2, 1), :], table[pl.ds(3, 1), :]
    late = table[pl.ds(4, 1), :], table[pl.ds(5, 1), :]
    second = after(start, early)
    gain_early, gain_late = gain_of(start, early), gain_of(second, late)
    own = select(first, start, second)
    df[...] = table_rows((8, modes), (*own, gain_early, gain_late))
    c = coup[...]
    a, ratio = chain(c, spec[...], *own)
    alpha[...] = c * a
    beta[...] = c * ratio

    def tile(v, _):
        at = pl.ds(pl.multiple_of(v * 16, 16), 16)
        carry = jnp.zeros((16, modes), F32)
        for t in range(steps - 1, -1, -1):
            carry = alpha[pl.ds(t, 1), :] * noise[t, at, :] + beta[pl.ds(t, 1), :] * carry
        o_ref[at, :] = carry
        sent[at, :] = carry.astype(BF16)
        return 0

    lax.fori_loop(0, vecs // 16, tile, 0)


def combine_kernel(tm_axis, own, other, df, out, late):
    first = lax.rem(lax.axis_index(tm_axis), 2) == 0
    x, y = own[...], other[...].astype(F32)
    behind = jnp.where(first, y, x)
    out[...] = (jnp.where(first, x, y) + df[pl.ds(2, 1), :] * behind).astype(BF16)
    late[...] = behind


def carry_kernel(tm_axis, late, wts, df, *rest):
    *received, _, out = rest
    vecs, modes = late.shape
    me = lax.axis_index(tm_axis)
    first = lax.rem(me, 2) == 0
    carry = jnp.zeros(late.shape, F32)
    for e, ref in enumerate(received):
        carry = carry + wts[(me // 2) ^ (e + 1)][0:1, :] * ref[...].astype(F32)
    out[pl.ds(0, vecs), :] = jnp.where(first, late[...] + df[pl.ds(3, 1), :] * carry, carry).astype(BF16)
    out[pl.ds(vecs, 16), :] = table_rows((16, modes), split3(df[pl.ds(0, 1), :]) + split3(df[pl.ds(1, 1), :])).astype(BF16)


def sums_of(block):
    return block[0:1] + block[1:2] + block[2:3], block[3:4] + block[4:5] + block[5:6]


def set_coefs(coefs, c, lam, sums):
    a, ratio = chain(c, lam, *sums)
    coefs[0] = a
    coefs[1] = ratio
    coefs[2] = c


def values(noise, start, coefs, state, rhs, times):
    vecs = noise.shape[1]
    for v in range(0, vecs, 16):
        at = pl.ds(v, 16)
        carry = start(at)
        for n, t in enumerate(times):
            row = pl.ds(t, 1)
            value = coefs[0, row, :] * noise[t, at, :] + coefs[1, row, :] * carry
            if t:
                carry = coefs[2, row, :] * value
            rhs[pl.ds((len(times) - 1 - n) * vecs + v, 16), :] = value.astype(BF16)
        if times[-1]:
            state[at, :] = carry


def product(lhs, rhs):
    return lax.dot_general(lhs, rhs, (((1,), (1,)), ((), ())), preferred_element_type=F32)


def halves_of(steps):
    times = list(range(steps - 1, -1, -1))
    return times[: steps // 2], times[steps // 2 :]


def own_kernel(sp_axis, coup, spec, basis, noise, message, out, lhs, rhs, state, coefs, sem):
    rows = lhs.shape[0]
    steps, vecs, _ = noise.shape
    start = pl.multiple_of(lax.axis_index(sp_axis) * rows, rows)
    copy = pltpu.make_async_copy(basis.at[pl.ds(start, rows), :], lhs, sem)
    copy.start()
    set_coefs(coefs, coup[...], spec[...], sums_of(message[pl.ds(vecs, 16), :].astype(F32)))
    late, early = halves_of(steps)
    width = vecs * len(late)
    values(noise, lambda at: message[at, :].astype(F32), coefs, state, rhs.at[0], late)
    copy.wait()
    values(noise, lambda at: state[at, :], coefs, state, rhs.at[1], early)
    out[:, pl.ds(width, width)] = product(lhs[...], rhs[0])
    out[:, pl.ds(0, width)] = product(lhs[...], rhs[1])


def final_kernel(tm_axis, pairs, single, partial, *rest):
    fetched = len(pairs) + len(single)
    count = 2 * len(pairs) + len(single)
    direct, rest = rest[:fetched], rest[fetched:]
    swapped, rest = rest[:fetched], rest[fetched:]
    noise, rest = rest[:count], rest[count:]
    messages, rest = rest[:count], rest[count:]
    out, lhs, rhs, state, coefs, result, sems = rest
    steps, vecs, _ = noise[0].shape
    core = lax.rem(lax.axis_index(tm_axis), 2)
    first = core == 0
    copies = []
    for i in range(len(single)):
        rows = lhs.shape[1] // 2
        for j, source in enumerate((direct[i], swapped[i])):
            at = pl.multiple_of((core if j == 0 else 1 - core) * rows, rows)
            copies.append(
                pltpu.make_async_copy(
                    source.at[pl.ds(0, rows), :], lhs.at[i, pl.ds(at, rows), :], sems.at[2 * i + j]
                )
            )
            copies[-1].start()

    def chosen(x, y):
        return lambda at: jnp.where(first, messages[x][at, :].astype(F32), messages[y][at, :].astype(F32))

    items = []
    for j, (x, y) in enumerate(pairs):
        i = len(single) + j
        rows = direct[i].shape[0] - TAIL
        near = lambda i=i, rows=rows: direct[i][pl.ds(0, rows), :]
        far = lambda i=i, rows=rows: swapped[i][pl.ds(0, rows), :]
        items.append((near, direct[i], noise[len(single) + j], chosen(x - 1, y - 1)))
        items.append((far, swapped[i], noise[len(single) + len(pairs) + j], chosen(y - 1, x - 1)))
    for i, d in enumerate(single):
        items.append((lambda i=i: lhs[i], direct[i], noise[i], chosen(d - 1, d - 1)))
    for n, (_, source, _, message) in enumerate(items):
        rows = source.shape[0] - TAIL
        x = [source[pl.ds(rows + 16 * j, 16), :].astype(F32) for j in range(4)]
        before = x[0][0:8] + x[0][8:16] + x[1][0:8]
        behind = x[1][8:16] + x[2][0:8] + x[2][8:16]
        lam = x[3][0:1] + x[3][1:2] + x[3][2:3]
        set_coefs(coefs.at[n], jnp.where(first, before, behind), lam, sums_of(message(pl.ds(vecs, 16))))
    late, early = halves_of(steps)
    width = vecs * len(late)
    work = [(h, n) for h in range(2) for n in range(count)]

    def fill(h, n):
        start = items[n][3] if h == 0 else lambda at: state[n, at, :]
        values(items[n][2], start, coefs.at[n], state.at[n], rhs.at[h, n], late if h == 0 else early)

    fill(*work[0])
    outs = []
    for k, (h, n) in enumerate(work):
        if k + 1 < len(work):
            fill(*work[k + 1])
        if h == 0 and n == count - len(single):
            for copy in copies:
                copy.wait()
        term = product(items[n][0](), rhs[h, n])
        at = pl.ds((1 - h) * width, width)
        result[h] = (partial[:, at] if n == 0 else result[h]) + term
        if n == count - 1:
            outs.append(pltpu.make_async_copy(result.at[h], out.at[:, at], sems.at[2 * len(single) + h]))
            outs[-1].start()
    for copy in outs:
        copy.wait()


def kernel_call(body, **options):
    return pl.pallas_call(body, **options)


def local(spectrum, coupling, spatial_basis, noise_keys, noise_counters):
    steps, modes = coupling.shape
    vecs = noise_keys.shape[0]
    tm, space = lax.axis_size("tm"), lax.axis_size("space")
    chips = tm // 2
    nodes_here = spatial_basis.shape[0] // space
    half = nodes_here // 2
    keys, counters = noise_keys.reshape(1, vecs), noise_counters.reshape(1, vecs)
    f32 = lambda *shape: jax.ShapeDtypeStruct(shape, F32)
    bf16 = lambda *shape: jax.ShapeDtypeStruct(shape, BF16)
    fast = dict(compiler_params=LIMIT)
    in_hbm = [
        pltpu.with_memory_space_constraint(x, pltpu.HBM)
        for x in (coupling, spectrum.reshape(1, modes), spatial_basis)
    ]

    pairs, single = partners(space)
    routes = [(d, d) for d in single] + pairs
    sizes = [half + TAIL] * len(single) + [nodes_here + TAIL] * len(pairs)
    other = swap(coupling, "tm", 1)
    *messages, coup, spec = kernel_call(
        functools.partial(pack_kernel, "tm", "space", routes),
        out_shape=[bf16(n, modes) for n in sizes] + [f32(steps, modes), f32(1, modes)],
        in_specs=[HBM] * 3,
        out_specs=[VMEM] * (len(sizes) + 2),
        scratch_shapes=[pltpu.SemaphoreType.DMA((len(sizes) + 2,))],
        **fast,
    )(*in_hbm)
    table, *messages = kernel_call(
        functools.partial(table_kernel, "tm", len(sizes)),
        out_shape=[f32(8, modes)] + [bf16(n, modes) for n in sizes],
        in_specs=[VMEM] * 3 + [ANY] * len(sizes),
        out_specs=[VMEM] + [ANY] * len(sizes),
        scratch_shapes=[pltpu.VMEM((TAIL, modes), BF16), pltpu.SemaphoreType.DMA((len(sizes),))],
        input_output_aliases={3 + i: 1 + i for i in range(len(sizes))},
        **fast,
    )(coup, other, spec, *messages)
    tables = [swap(table, "tm", 2 * e) for e in range(1, chips)]
    direct = [exchange(m, lambda t, s, r=r: (t, s ^ r[t % 2])) for m, r in zip(messages, routes)]

    def noise_of(blocks, after, through=()):
        count = len(blocks) * steps * vecs * modes
        extras = len(after) + len(through)
        return kernel_call(
            functools.partial(noise_kernel, "tm", "space", blocks, extras),
            out_shape=[f32(steps, vecs, modes)] * len(blocks)
            + [jax.ShapeDtypeStruct(x.shape, x.dtype) for x in through],
            in_specs=[VMEM] * 2 + [ANY] * extras,
            out_specs=[VMEM] * len(blocks) + [ANY] * len(through),
            scratch_shapes=[pltpu.VMEM((vecs, 128), jnp.int32)],
            input_output_aliases={2 + len(after) + i: len(blocks) + i for i in range(len(through))},
            cost_estimate=pl.CostEstimate(flops=count * 60, transcendentals=count * 2, bytes_accessed=count * 4),
            **fast,
        )(keys, counters, *after, *through)

    (own,) = noise_of([(0, (0, 0))], (table,))
    state, sent, weights, sums = kernel_call(
        functools.partial(offset_kernel, "tm"),
        out_shape=[f32(vecs, modes), bf16(vecs, modes), f32(chips, 8, modes), f32(8, modes)],
        in_specs=[VMEM] * (4 + len(tables)),
        out_specs=[VMEM] * 4,
        scratch_shapes=[pltpu.VMEM((chips, 8, modes), F32)] + [pltpu.VMEM((steps, modes), F32)] * 2,
        **fast,
    )(own, coup, spec, table, *tables)
    total, late = kernel_call(
        functools.partial(combine_kernel, "tm"),
        out_shape=[bf16(vecs, modes), f32(vecs, modes)],
        in_specs=[VMEM] * 3,
        out_specs=[VMEM] * 2,
        **fast,
    )(state, swap(sent, "tm", 1), sums)
    later = [swap(total, "tm", 2 * e) for e in range(1, chips)]
    noise = list(noise_of([(0, (d, d)) for d in single], (total,)))
    noise += noise_of([(0, r) for r in pairs], (noise[-1],))
    carry = kernel_call(
        functools.partial(carry_kernel, "tm"),
        out_shape=bf16(vecs + 16, modes),
        in_specs=[VMEM] * (3 + len(later)) + [ANY],
        out_specs=VMEM,
        **fast,
    )(late, weights, sums, *later, noise[-1])
    carries = [swap(carry, "space", d) for d in range(1, space)]
    swapped = [swap(m, "tm", 1) for m in direct]
    noise += noise_of([(0, r[::-1]) for r in pairs], (carry,))

    flops = 2 * nodes_here * modes * steps * vecs
    half_cols = steps // 2 * vecs
    result = f32(nodes_here, steps * vecs)
    out = kernel_call(
        functools.partial(own_kernel, "space"),
        out_shape=result,
        in_specs=[VMEM, VMEM, HBM, VMEM, VMEM],
        out_specs=VMEM,
        scratch_shapes=[
            pltpu.VMEM((nodes_here, modes), BF16),
            pltpu.VMEM((2, half_cols, modes), BF16),
            pltpu.VMEM((vecs, modes), F32),
            pltpu.VMEM((3, steps, modes), F32),
            pltpu.SemaphoreType.DMA,
        ],
        cost_estimate=pl.CostEstimate(flops=flops, transcendentals=0, bytes_accessed=4 * steps * vecs * modes),
        **fast,
    )(coup, spec, spatial_basis, own, carry)
    count = space - 1
    return kernel_call(
        functools.partial(final_kernel, "tm", pairs, single),
        out_shape=result,
        in_specs=[VMEM] * (1 + len(direct) + len(swapped) + len(noise) + len(carries)),
        out_specs=HBM,
        scratch_shapes=[
            pltpu.VMEM((len(single), nodes_here, modes), BF16),
            pltpu.VMEM((2, count, half_cols, modes), BF16),
            pltpu.VMEM((count, vecs, modes), F32),
            pltpu.VMEM((count, 3, steps, modes), F32),
            pltpu.VMEM((2, nodes_here, half_cols), F32),
            pltpu.SemaphoreType.DMA((2 * len(single) + 2,)),
        ],
        cost_estimate=pl.CostEstimate(
            flops=flops * count, transcendentals=0, bytes_accessed=4 * steps * vecs * modes * count
        ),
        **fast,
    )(out, *direct, *swapped, *noise, *carries)


def solution(mesh):
    in_specs = (P("space"), P("tm", "space"), P(None, "space"), P(), P())
    out_specs = P("space", "tm")
    return jax.shard_map(local, mesh=mesh, in_specs=in_specs, out_specs=out_specs, check_vma=False)
```

profile of v0, /device:TPU:0, one launch (start us, length us, event | category | flops | bytes accessed | tf_op | source)
XLA Modules:
  0.0 50.1 jit_solution(8761730417944140274)
XLA Ops:
  0.0 0.5 collective-permute-start
  0.5 1.2 %shard_map.55 = (bf16[320,512]{1,0:T(8,128)(2,1)S(1)}, bf16[576,512]{1,0:T(8,128)(2,1)S(1)}, f32[8,512]{1,0:T(8,128)S(1)}, f32[1,512]{1,0:T(1,128)S(1)}) custom-call(f32[8,512]{1,0:T(8,128)} %coup.1, f32[1,512]{1,0:T(1,128)} %bitcast.11, bf16[2048,512]{1,0:T(8,128)(2,1)} %basis.3), custom_call_target="tpu_custom_call" | custom-call | tf_op jit(solution)/shard_map/pallas_call | solution.py:412
  2.0 2.7 %collective-permute-start.9 = (bf16[576,512]{1,0:T(8,128)(2,1)S(1)}, bf16[576,512]{1,0:T(8,128)(2,1)S(1)}, u32[]{:S(2)}, u32[]{:S(2)}) collective-permute-start(bf16[576,512]{1,0:T(8,128)(2,1)S(1)} %get-tuple-element.30), channel_id=1, source_target_pairs={{0,1},{1,0},{2,3},{3,2},{4,6},{5,7},{6,4},{7,5},{8,9},{9,8},{10,11... | collective-permute-start | bytes 1769480 | tf_op jit(solution)/shard_map/ppermute | solution.py:33
  4.7 1.5 %collective-permute-start.8 = (bf16[320,512]{1,0:T(8,128)(2,1)S(1)}, bf16[320,512]{1,0:T(8,128)(2,1)S(1)}, u32[]{:S(2)}, u32[]{:S(2)}) collective-permute-start(bf16[320,512]{1,0:T(8,128)(2,1)S(1)} %get-tuple-element.29), channel_id=1, source_target_pairs={{0,3},{1,2},{2,1},{3,0},{4,7},{5,6},{6,5},{7,4},{8,11},{9,10},{10,... | collective-permute-start | bytes 983048 | tf_op jit(solution)/shard_map/ppermute | solution.py:33
  6.2 9.9 %collective-permute-done.9.rest_1_ = bf16[576,512]{1,0:T(8,128)(2,1)S(1)} collective-permute-done((bf16[576,512]{1,0:T(8,128)(2,1)S(1)}, bf16[576,512]{1,0:T(8,128)(2,1)S(1)}, u32[]{:S(2)}, u32[]{:S(2)}) %collective-permute-start.9) | collective-permute-done | bytes 589856 | tf_op jit(solution)/shard_map/ppermute | solution.py:33
  16.1 5.0 %collective-permute-done.8.rest_0_ = bf16[320,512]{1,0:T(8,128)(2,1)S(1)} collective-permute-done((bf16[320,512]{1,0:T(8,128)(2,1)S(1)}, bf16[320,512]{1,0:T(8,128)(2,1)S(1)}, u32[]{:S(2)}, u32[]{:S(2)}) %collective-permute-start.8) | collective-permute-done | bytes 327712 | tf_op jit(solution)/shard_map/ppermute | solution.py:33
  21.0 3.6 %collective-permute-start.3 = (f32[8,512]{1,0:T(8,128)S(1)}, f32[8,512]{1,0:T(8,128)S(1)}, u32[]{:S(2)}, u32[]{:S(2)}) collective-permute-start(f32[8,512]{1,0:T(8,128)S(1)} %get-tuple-element.22.rest_0_.table), channel_id=1, source_target_pairs={{0,24},{4,28},{8,16},{12,20},{16,8},{20,12},{24,0},{28,4},{1,25},{... | collective-permute-start | bytes 49160 | tf_op jit(solution)/shard_map/ppermute | solution.py:38
  24.7 0.8 %collective-permute-start.1 = (f32[8,512]{1,0:T(8,128)S(1)}, f32[8,512]{1,0:T(8,128)S(1)}, u32[]{:S(2)}, u32[]{:S(2)}) collective-permute-start(f32[8,512]{1,0:T(8,128)S(1)} %get-tuple-element.22.rest_0_.table), channel_id=1, source_target_pairs={{0,8},{4,12},{8,0},{12,4},{16,24},{20,28},{24,16},{28,20},{1,9},{5... | collective-permute-start | bytes 49160 | tf_op jit(solution)/shard_map/ppermute | solution.py:38
  25.4 1.7 %shard_map.57.noise = f32[8,64,512]{2,1,0:T(8,128)S(1)} custom-call(s32[1,64]{1,0:T(1,128)S(1)} %bitcast.3, s32[1,64]{1,0:T(1,128)S(1)} %bitcast.7, f32[8,512]{1,0:T(8,128)S(1)} %get-tuple-element.22.rest_0_.table), custom_call_target="tpu_custom_call" | custom-call | flops 15728640 | bytes 1048576 | tf_op jit(solution)/shard_map/pallas_call | solution.py:435
  27.2 2.1 %collective-permute-done.2.rest_1_ = f32[8,512]{1,0:T(8,128)S(1)} collective-permute-done((f32[8,512]{1,0:T(8,128)S(1)}, f32[8,512]{1,0:T(8,128)S(1)}, u32[]{:S(2)}, u32[]{:S(2)}) %collective-permute-start.2) | collective-permute-done | bytes 16416 | tf_op jit(solution)/shard_map/ppermute | solution.py:38
  29.7 1.2 %collective-permute-done.4.other = bf16[64,512]{1,0:T(8,128)(2,1)S(1)} collective-permute-done((bf16[64,512]{1,0:T(8,128)(2,1)S(1)}, bf16[64,512]{1,0:T(8,128)(2,1)S(1)}, u32[]{:S(2)}, u32[]{:S(2)}) %collective-permute-start.4) | collective-permute-done | bytes 65568 | tf_op jit(solution)/shard_map/ppermute | solution.py:38
  30.9 1.6 %collective-permute-start.7 = (bf16[64,512]{1,0:T(8,128)(2,1)S(1)}, bf16[64,512]{1,0:T(8,128)(2,1)S(1)}, u32[]{:S(2)}, u32[]{:S(2)}) collective-permute-start(bf16[64,512]{1,0:T(8,128)(2,1)S(1)} %get-tuple-element.28.rest_0_), channel_id=1, source_target_pairs={{0,24},{4,28},{8,16},{12,20},{16,8},{20,12},{24,0},{28,4},{1,25},{... | collective-permute-start | bytes 196616 | tf_op jit(solution)/shard_map/ppermute | solution.py:38
  32.5 0.6 %collective-permute-start.6 = (bf16[64,512]{1,0:T(8,128)(2,1)S(1)}, bf16[64,512]{1,0:T(8,128)(2,1)S(1)}, u32[]{:S(2)}, u32[]{:S(2)}) collective-permute-start(bf16[64,512]{1,0:T(8,128)(2,1)S(1)} %get-tuple-element.28.rest_0_), channel_id=1, source_target_pairs={{0,16},{4,20},{8,24},{12,28},{16,0},{20,4},{24,8},{28,12},{1,17},{... | collective-permute-start | bytes 196616 | tf_op jit(solution)/shard_map/ppermute | solution.py:38
  33.1 2.3 %collective-permute-start.5 = (bf16[64,512]{1,0:T(8,128)(2,1)S(1)}, bf16[64,512]{1,0:T(8,128)(2,1)S(1)}, u32[]{:S(2)}, u32[]{:S(2)}) collective-permute-start(bf16[64,512]{1,0:T(8,128)(2,1)S(1)} %get-tuple-element.28.rest_0_), channel_id=1, source_target_pairs={{0,8},{4,12},{8,0},{12,4},{16,24},{20,28},{24,16},{28,20},{1,9},{5... | collective-permute-start | bytes 196616 | tf_op jit(solution)/shard_map/ppermute | solution.py:38
  35.4 1.7 %shard_map.60.rest_0_.rest_4_ = f32[8,64,512]{2,1,0:T(8,128)S(1)} custom-call(s32[1,64]{1,0:T(1,128)S(1)} %bitcast.4, s32[1,64]{1,0:T(1,128)S(1)} %bitcast.8, bf16[64,512]{1,0:T(8,128)(2,1)S(1)} %get-tuple-element.28.rest_0_), custom_call_target="tpu_custom_call" | custom-call | flops 15728640 | bytes 1048576 | tf_op jit(solution)/shard_map/pallas_call | solution.py:435
  37.1 1.7 %shard_map.61.rest_3_.rest_5_ = f32[8,64,512]{2,1,0:T(8,128)S(1)} custom-call(s32[1,64]{1,0:T(1,128)S(1)} %bitcast.5, s32[1,64]{1,0:T(1,128)S(1)} %bitcast.9, f32[8,64,512]{2,1,0:T(8,128)S(1)} %shard_map.60.rest_0_.rest_4_), custom_call_target="tpu_custom_call" | custom-call | flops 15728640 | bytes 1048576 | tf_op jit(solution)/shard_map/pallas_call | solution.py:435
  38.9 0.9 %collective-permute-done.6.rest_1_ = bf16[64,512]{1,0:T(8,128)(2,1)S(1)} collective-permute-done((bf16[64,512]{1,0:T(8,128)(2,1)S(1)}, bf16[64,512]{1,0:T(8,128)(2,1)S(1)}, u32[]{:S(2)}, u32[]{:S(2)}) %collective-permute-start.6) | collective-permute-done | bytes 65568 | tf_op jit(solution)/shard_map/ppermute | solution.py:38
  39.9 1.5 %collective-permute-start.14 = (bf16[80,512]{1,0:T(8,128)(2,1)S(1)}, bf16[80,512]{1,0:T(8,128)(2,1)S(1)}, u32[]{:S(2)}, u32[]{:S(2)}) collective-permute-start(bf16[80,512]{1,0:T(8,128)(2,1)S(1)} %shard_map.62.message.rest_0_), channel_id=1, source_target_pairs={{0,3},{1,2},{2,1},{3,0},{4,7},{5,6},{6,5},{7,4},{8,11},{9,10},{10,... | collective-permute-start | bytes 245768 | tf_op jit(solution)/shard_map/ppermute | solution.py:38
  41.4 1.5 %collective-permute-start.13 = (bf16[80,512]{1,0:T(8,128)(2,1)S(1)}, bf16[80,512]{1,0:T(8,128)(2,1)S(1)}, u32[]{:S(2)}, u32[]{:S(2)}) collective-permute-start(bf16[80,512]{1,0:T(8,128)(2,1)S(1)} %shard_map.62.message.rest_0_), channel_id=1, source_target_pairs={{0,2},{1,3},{2,0},{3,1},{4,6},{5,7},{6,4},{7,5},{8,10},{9,11},{10,... | collective-permute-start | bytes 245768 | tf_op jit(solution)/shard_map/ppermute | solution.py:38
  42.9 0.5 %collective-permute-start.12 = (bf16[80,512]{1,0:T(8,128)(2,1)S(1)}, bf16[80,512]{1,0:T(8,128)(2,1)S(1)}, u32[]{:S(2)}, u32[]{:S(2)}) collective-permute-start(bf16[80,512]{1,0:T(8,128)(2,1)S(1)} %shard_map.62.message.rest_0_), channel_id=1, source_target_pairs={{0,1},{1,0},{2,3},{3,2},{4,5},{5,4},{6,7},{7,6},{8,9},{9,8},{10,11... | collective-permute-start | bytes 245768 | tf_op jit(solution)/shard_map/ppermute | solution.py:38
  43.4 1.7 %shard_map.64.rest_6_ = f32[8,64,512]{2,1,0:T(8,128)S(1)} custom-call(s32[1,64]{1,0:T(1,128)S(1)} %bitcast.6, s32[1,64]{1,0:T(1,128)S(1)} %bitcast.10, bf16[80,512]{1,0:T(8,128)(2,1)S(1)} %shard_map.62.message.rest_0_), custom_call_target="tpu_custom_call" | custom-call | flops 15728640 | bytes 1048576 | tf_op jit(solution)/shard_map/pallas_call | solution.py:435
  45.2 0.8 %shard_map.63.partial = f32[512,512]{1,0:T(8,128)S(1)} custom-call(f32[8,512]{1,0:T(8,128)S(1)} %get-tuple-element.18.coup, f32[1,512]{1,0:T(1,128)S(1)} %get-tuple-element.19.spec, bf16[2048,512]{1,0:T(8,128)(2,1)S(1)} %copy-done, f32[8,64,512]{2,1,0:T(8,128)S(1)} %shard_map.57.noise, bf16[80,512]{1,0:T(8,128)(2,1)S(1)} %shard_map.62.message.rest_0_), custom_call_target="tpu_custom_call" | custom-call | flops 268435456 | bytes 1048576 | tf_op jit(solution)/shard_map/pallas_call | solution.py:480
  45.9 1.0 %collective-permute-done.13.rest_8_ = bf16[80,512]{1,0:T(8,128)(2,1)S(1)} collective-permute-done((bf16[80,512]{1,0:T(8,128)(2,1)S(1)}, bf16[80,512]{1,0:T(8,128)(2,1)S(1)}, u32[]{:S(2)}, u32[]{:S(2)}) %collective-permute-start.13) | collective-permute-done | bytes 81952 | tf_op jit(solution)/shard_map/ppermute | solution.py:38
  47.3 2.8 %shard_map.65 = f32[512,512]{1,0:T(8,128)} custom-call(f32[512,512]{1,0:T(8,128)S(1)} %shard_map.63.partial, bf16[320,512]{1,0:T(8,128)(2,1)S(1)} %collective-permute-done.8.rest_0_, bf16[576,512]{1,0:T(8,128)(2,1)S(1)} %collective-permute-done.9.rest_1_, bf16[320,512]{1,0:T(8,128)(2,1)S(1)} %collective-permute-done.10.rest_2_, ...), custom_call_target="tpu_custom_call" | custom-call | flops 805306368 | bytes 3145728 | tf_op jit(solution)/shard_map/pallas_call | solution.py:496
  (23 shorter events, 1.1 us)
Async XLA Ops:
  0.0 25.4 %copy-start.2 = (s32[64]{0:T(128)S(1)}, s32[64]{0:T(128)}, u32[]{:S(2)}) copy-start(s32[64]{0:T(128)} %param.9) | copy-start | bytes 772
  0.0 25.4 %copy-start.1 = (s32[64]{0:T(128)S(1)}, s32[64]{0:T(128)}, u32[]{:S(2)}) copy-start(s32[64]{0:T(128)} %param.8) | copy-start | bytes 772
  0.0 1.7 %collective-permute-start = (f32[8,512]{1,0:T(8,128)}, f32[8,512]{1,0:T(8,128)S(1)}, u32[]{:S(2)}, u32[]{:S(2)}) collective-permute-start(f32[8,512]{1,0:T(8,128)} %coup.1), channel_id=1, source_target_pairs={{0,4},{4,0},{8,12},{12,8},{16,20},{20,16},{24,28},{28,24},{1,5},{5... | collective-permute-start | bytes 49160 | tf_op jit(solution)/shard_map/ppermute | solution.py:38
  2.0 14.1 %collective-permute-start.9 = (bf16[576,512]{1,0:T(8,128)(2,1)S(1)}, bf16[576,512]{1,0:T(8,128)(2,1)S(1)}, u32[]{:S(2)}, u32[]{:S(2)}) collective-permute-start(bf16[576,512]{1,0:T(8,128)(2,1)S(1)} %get-tuple-element.30), channel_id=1, source_target_pairs={{0,1},{1,0},{2,3},{3,2},{4,6},{5,7},{6,4},{7,5},{8,9},{9,8},{10,11... | collective-permute-start | bytes 1769480 | tf_op jit(solution)/shard_map/ppermute | solution.py:33
  4.7 16.4 %collective-permute-start.8 = (bf16[320,512]{1,0:T(8,128)(2,1)S(1)}, bf16[320,512]{1,0:T(8,128)(2,1)S(1)}, u32[]{:S(2)}, u32[]{:S(2)}) collective-permute-start(bf16[320,512]{1,0:T(8,128)(2,1)S(1)} %get-tuple-element.29), channel_id=1, source_target_pairs={{0,3},{1,2},{2,1},{3,0},{4,7},{5,6},{6,5},{7,4},{8,11},{9,10},{10,... | collective-permute-start | bytes 983048 | tf_op jit(solution)/shard_map/ppermute | solution.py:33
  16.0 31.3 %collective-permute-start.11 = (bf16[576,512]{1,0:T(8,128)(2,1)S(1)}, bf16[576,512]{1,0:T(8,128)(2,1)S(1)}, u32[]{:S(2)}, u32[]{:S(2)}) collective-permute-start(bf16[576,512]{1,0:T(8,128)(2,1)S(1)} %collective-permute-done.9.rest_1_), channel_id=1, source_target_pairs={{0,4},{4,0},{8,12},{12,8},{16,20},{20,16},{24,28},{28,24},{1,5},{5... | collective-permute-start | bytes 1769480 | tf_op jit(solution)/shard_map/ppermute | solution.py:38
  21.0 26.3 %collective-permute-start.10 = (bf16[320,512]{1,0:T(8,128)(2,1)S(1)}, bf16[320,512]{1,0:T(8,128)(2,1)S(1)}, u32[]{:S(2)}, u32[]{:S(2)}) collective-permute-start(bf16[320,512]{1,0:T(8,128)(2,1)S(1)} %collective-permute-done.8.rest_0_), channel_id=1, source_target_pairs={{0,4},{4,0},{8,12},{12,8},{16,20},{20,16},{24,28},{28,24},{1,5},{5... | collective-permute-start | bytes 983048 | tf_op jit(solution)/shard_map/ppermute | solution.py:38
  21.0 6.1 %collective-permute-start.3 = (f32[8,512]{1,0:T(8,128)S(1)}, f32[8,512]{1,0:T(8,128)S(1)}, u32[]{:S(2)}, u32[]{:S(2)}) collective-permute-start(f32[8,512]{1,0:T(8,128)S(1)} %get-tuple-element.22.rest_0_.table), channel_id=1, source_target_pairs={{0,24},{4,28},{8,16},{12,20},{16,8},{20,12},{24,0},{28,4},{1,25},{... | collective-permute-start | bytes 49160 | tf_op jit(solution)/shard_map/ppermute | solution.py:38
  24.7 4.6 %collective-permute-start.2 = (f32[8,512]{1,0:T(8,128)S(1)}, f32[8,512]{1,0:T(8,128)S(1)}, u32[]{:S(2)}, u32[]{:S(2)}) collective-permute-start(f32[8,512]{1,0:T(8,128)S(1)} %get-tuple-element.22.rest_0_.table), channel_id=1, source_target_pairs={{0,16},{4,20},{8,24},{12,28},{16,0},{20,4},{24,8},{28,12},{1,17},{... | collective-permute-start | bytes 49160 | tf_op jit(solution)/shard_map/ppermute | solution.py:38
  24.7 4.6 %collective-permute-start.1 = (f32[8,512]{1,0:T(8,128)S(1)}, f32[8,512]{1,0:T(8,128)S(1)}, u32[]{:S(2)}, u32[]{:S(2)}) collective-permute-start(f32[8,512]{1,0:T(8,128)S(1)} %get-tuple-element.22.rest_0_.table), channel_id=1, source_target_pairs={{0,8},{4,12},{8,0},{12,4},{16,24},{20,28},{24,16},{28,20},{1,9},{5... | collective-permute-start | bytes 49160 | tf_op jit(solution)/shard_map/ppermute | solution.py:38
  29.6 1.3 %collective-permute-start.4 = (bf16[64,512]{1,0:T(8,128)(2,1)S(1)}, bf16[64,512]{1,0:T(8,128)(2,1)S(1)}, u32[]{:S(2)}, u32[]{:S(2)}) collective-permute-start(bf16[64,512]{1,0:T(8,128)(2,1)S(1)} %get-tuple-element.24), channel_id=1, source_target_pairs={{0,4},{4,0},{8,12},{12,8},{16,20},{20,16},{24,28},{28,24},{1,5},{5... | collective-permute-start | bytes 196616 | tf_op jit(solution)/shard_map/ppermute | solution.py:38
  30.9 8.0 %collective-permute-start.7 = (bf16[64,512]{1,0:T(8,128)(2,1)S(1)}, bf16[64,512]{1,0:T(8,128)(2,1)S(1)}, u32[]{:S(2)}, u32[]{:S(2)}) collective-permute-start(bf16[64,512]{1,0:T(8,128)(2,1)S(1)} %get-tuple-element.28.rest_0_), channel_id=1, source_target_pairs={{0,24},{4,28},{8,16},{12,20},{16,8},{20,12},{24,0},{28,4},{1,25},{... | collective-permute-start | bytes 196616 | tf_op jit(solution)/shard_map/ppermute | solution.py:38
  32.5 7.2 %collective-permute-start.6 = (bf16[64,512]{1,0:T(8,128)(2,1)S(1)}, bf16[64,512]{1,0:T(8,128)(2,1)S(1)}, u32[]{:S(2)}, u32[]{:S(2)}) collective-permute-start(bf16[64,512]{1,0:T(8,128)(2,1)S(1)} %get-tuple-element.28.rest_0_), channel_id=1, source_target_pairs={{0,16},{4,20},{8,24},{12,28},{16,0},{20,4},{24,8},{28,12},{1,17},{... | collective-permute-start | bytes 196616 | tf_op jit(solution)/shard_map/ppermute | solution.py:38
  33.1 6.7 %collective-permute-start.5 = (bf16[64,512]{1,0:T(8,128)(2,1)S(1)}, bf16[64,512]{1,0:T(8,128)(2,1)S(1)}, u32[]{:S(2)}, u32[]{:S(2)}) collective-permute-start(bf16[64,512]{1,0:T(8,128)(2,1)S(1)} %get-tuple-element.28.rest_0_), channel_id=1, source_target_pairs={{0,8},{4,12},{8,0},{12,4},{16,24},{20,28},{24,16},{28,20},{1,9},{5... | collective-permute-start | bytes 196616 | tf_op jit(solution)/shard_map/ppermute | solution.py:38
  37.1 8.0 %copy-start = (bf16[2048,512]{1,0:T(8,128)(2,1)S(1)}, bf16[2048,512]{1,0:T(8,128)(2,1)}, u32[]{:S(2)}) copy-start(bf16[2048,512]{1,0:T(8,128)(2,1)} %basis.3) | copy-start | bytes 6291460
  39.9 6.1 %collective-permute-start.14 = (bf16[80,512]{1,0:T(8,128)(2,1)S(1)}, bf16[80,512]{1,0:T(8,128)(2,1)S(1)}, u32[]{:S(2)}, u32[]{:S(2)}) collective-permute-start(bf16[80,512]{1,0:T(8,128)(2,1)S(1)} %shard_map.62.message.rest_0_), channel_id=1, source_target_pairs={{0,3},{1,2},{2,1},{3,0},{4,7},{5,6},{6,5},{7,4},{8,11},{9,10},{10,... | collective-permute-start | bytes 245768 | tf_op jit(solution)/shard_map/ppermute | solution.py:38
  41.4 5.6 %collective-permute-start.13 = (bf16[80,512]{1,0:T(8,128)(2,1)S(1)}, bf16[80,512]{1,0:T(8,128)(2,1)S(1)}, u32[]{:S(2)}, u32[]{:S(2)}) collective-permute-start(bf16[80,512]{1,0:T(8,128)(2,1)S(1)} %shard_map.62.message.rest_0_), channel_id=1, source_target_pairs={{0,2},{1,3},{2,0},{3,1},{4,6},{5,7},{6,4},{7,5},{8,10},{9,11},{10,... | collective-permute-start | bytes 245768 | tf_op jit(solution)/shard_map/ppermute | solution.py:38
  42.9 4.4 %collective-permute-start.12 = (bf16[80,512]{1,0:T(8,128)(2,1)S(1)}, bf16[80,512]{1,0:T(8,128)(2,1)S(1)}, u32[]{:S(2)}, u32[]{:S(2)}) collective-permute-start(bf16[80,512]{1,0:T(8,128)(2,1)S(1)} %shard_map.62.message.rest_0_), channel_id=1, source_target_pairs={{0,1},{1,0},{2,3},{3,2},{4,5},{5,4},{6,7},{7,6},{8,9},{9,8},{10,11... | collective-permute-start | bytes 245768 | tf_op jit(solution)/shard_map/ppermute | solution.py:38
where the time goes:
time: 50.3 us; the launch traced here: 50.1 us
  waiting for transfers between devices  20.5 us (41%)
  starting transfers between devices  17.2 us (34%)
  Pallas kernels  12.4 us (25%)
    ppermute x2, waiting for transfers between devices, exchange(): return lax.ppermute(x, ('tm', 'space'), moves)  14.9 us
    ppermute x13, starting transfers between devices, swap(): return lax.ppermute(x, axis, [(i, i ^ offset) for i in range(count)])  13 us
    pallas_call x4, Pallas kernels, noise_of(): kernel_call(functools.partial(noise_kernel, 'tm', 'space', blocks, extras...  6.97 us
    ppermute x13, waiting for transfers between devices, swap(): return lax.ppermute(x, axis, [(i, i ^ offset) for i in range(count)])  5.58 us
    ppermute x2, starting transfers between devices, exchange(): return lax.ppermute(x, ('tm', 'space'), moves)  4.21 us
    pallas_call x1, Pallas kernels, local(): kernel_call(functools.partial(final_kernel, 'tm', pairs, single), out_sha...  2.83 us
    pallas_call x1, Pallas kernels, local(): kernel_call(functools.partial(pack_kernel, 'tm', 'space', routes), out_sh...  1.19 us
  transfers between devices with their start and end apart: 15, of which 7 were waited for; matrix products, arithmetic and copies ran while one was open for 0% of the time, Pallas kernels for 19%

commit v1 on v0

--- a/solution.py
+++ b/solution.py
@@ -75,13 +75,17 @@
     return offsets[0] if offsets[0] == offsets[1] else jnp.where(core == 0, offsets[0], offsets[1])
 
 
-def pack_kernel(tm_axis, sp_axis, offsets, coup, spec, basis, *rest):
-    *outs, coup_out, spec_out, sems = rest
+def pack_kernel(tm_axis, sp_axis, offsets, coup, spec, basis, keys, counters, *rest):
+    *outs, coup_out, spec_out, base, key_row, counter_row, sems = rest
     me, sp = lax.axis_index(tm_axis), lax.axis_index(sp_axis)
     core = lax.rem(me, 2)
     copies = [
         pltpu.make_async_copy(coup, coup_out, sems.at[len(outs)]),
         pltpu.make_async_copy(spec, spec_out, sems.at[len(outs) + 1]),
+    ]
+    rows_in = [
+        pltpu.make_async_copy(keys, key_row, sems.at[len(outs) + 2]),
+        pltpu.make_async_copy(counters, counter_row, sems.at[len(outs) + 3]),
     ]
     for i, (out, offset) in enumerate(zip(outs, offsets)):
         rows = out.shape[0] - TAIL
@@ -92,8 +96,11 @@
         copies.append(
             pltpu.make_async_copy(basis.at[pl.ds(start, rows), :], out.at[pl.ds(0, rows), :], sems.at[i])
         )
-    for copy in copies:
+    for copy in rows_in + copies:
         copy.start()
+    for copy in rows_in:
+        copy.wait()
+    base_columns(key_row, counter_row, base)
     for copy in copies:
         copy.wait()
 
@@ -145,11 +152,8 @@
         copy.wait()
 
 
-def noise_kernel(tm_axis, sp_axis, blocks, extras, keys, counters, *rest):
-    *outs, base = rest[extras:]
-    outs = outs[: len(blocks)]
-    steps, vecs, modes = outs[0].shape
-    me, sp = lax.axis_index(tm_axis), lax.axis_index(sp_axis)
+def base_columns(keys, counters, base):
+    vecs = base.shape[0]
     diagonal = lax.broadcasted_iota(jnp.int32, (vecs, vecs), 0) == lax.broadcasted_iota(
         jnp.int32, (vecs, vecs), 1
     )
@@ -160,11 +164,17 @@
 
     start = column(keys) * jnp.int32(668265261) + column(counters) * jnp.int32(374761393)
     base[...] = jnp.broadcast_to(start, base.shape)
+
+
+def noise_kernel(tm_axis, sp_axis, offsets, extras, base, *rest):
+    outs = rest[extras:]
+    steps, vecs, modes = outs[0].shape
+    me, sp = lax.axis_index(tm_axis), lax.axis_index(sp_axis)
     group = 8
-    for out, (block, offset) in zip(outs, blocks):
+    for out, offset in zip(outs, offsets):
         ids = (sp ^ pick(lax.rem(me, 2), offset)) * modes + lax.broadcasted_iota(jnp.int32, (1, modes), 1)
         lane = ids * jnp.int32(-1640531535)
-        first_step = (me ^ block) * steps
+        first_step = me * steps
 
         def step(t, _):
             shifted = lane + (first_step + t) * jnp.int32(374761393)
@@ -176,18 +186,20 @@
         lax.fori_loop(0, steps, step, 0)
 
 
-def chain(coup, spec, d_start, f_start):
-    before, after = [], []
-    square, total = None, None
-    d_now = d_start
-    for t in range(coup.shape[0]):
-        c = coup[t : t + 1, :]
-        square = c * c if t == 0 else square * (c * c)
-        total = square if t == 0 else total + square
-        before.append(d_now)
-        d_now = d_start + f_start * total
-        after.append(d_now)
-    ratio = jnp.concatenate(before, 0) / jnp.concatenate(after, 0)
+def running(x, combine, identity):
+    row = lax.broadcasted_iota(jnp.int32, x.shape, 0)
+    shift = 1
+    while shift < x.shape[0]:
+        x = combine(x, jnp.where(row < shift, identity, pltpu.roll(x, shift, 0)))
+        shift *= 2
+    return x
+
+
+def chain(c, spec, d_start, f_start):
+    total = running(running(c * c, jnp.multiply, 1.0), jnp.add, 0.0)
+    behind = d_start + f_start * total
+    row = lax.broadcasted_iota(jnp.int32, c.shape, 0)
+    ratio = jnp.where(row == 0, d_start, pltpu.roll(behind, 1, 0)) / behind
     return jnp.sqrt(ratio / spec), ratio
 
 
@@ -271,24 +283,24 @@
 
 def set_coefs(coefs, c, lam, sums):
     a, ratio = chain(c, lam, *sums)
+    row = lax.broadcasted_iota(jnp.int32, c.shape, 0)
+    steps = c.shape[0]
     coefs[0] = a
-    coefs[1] = ratio
-    coefs[2] = c
-
-
-def values(noise, start, coefs, state, rhs, times):
+    coefs[1] = ratio * jnp.where(row == steps - 1, 1.0, pltpu.roll(c, steps - 1, 0))
+
+
+def values(noise, start, coefs, state, rhs, times, part=(0, 1)):
     vecs = noise.shape[1]
-    for v in range(0, vecs, 16):
+    share = vecs // part[1]
+    for v in range(part[0] * share, (part[0] + 1) * share, 16):
         at = pl.ds(v, 16)
-        carry = start(at)
+        value = start(at)
         for n, t in enumerate(times):
             row = pl.ds(t, 1)
-            value = coefs[0, row, :] * noise[t, at, :] + coefs[1, row, :] * carry
-            if t:
-                carry = coefs[2, row, :] * value
+            value = coefs[0, row, :] * noise[t, at, :] + coefs[1, row, :] * value
             rhs[pl.ds((len(times) - 1 - n) * vecs + v, 16), :] = value.astype(BF16)
         if times[-1]:
-            state[at, :] = carry
+            state[at, :] = value
 
 
 def product(lhs, rhs):
@@ -298,6 +310,10 @@
 def halves_of(steps):
     times = list(range(steps - 1, -1, -1))
     return times[: steps // 2], times[steps // 2 :]
+
+
+def region(position, n):
+    return pl.when(position >= -n)
 
 
 def own_kernel(sp_axis, coup, spec, basis, noise, message, out, lhs, rhs, state, coefs, sem):
@@ -311,9 +327,15 @@
     width = vecs * len(late)
     values(noise, lambda at: message[at, :].astype(F32), coefs, state, rhs.at[0], late)
     copy.wait()
-    values(noise, lambda at: state[at, :], coefs, state, rhs.at[1], early)
-    out[:, pl.ds(width, width)] = product(lhs[...], rhs[0])
-    out[:, pl.ds(0, width)] = product(lhs[...], rhs[1])
+
+    @region(start, 0)
+    def _():
+        out[:, pl.ds(width, width)] = product(lhs[...], rhs[0])
+        values(noise, lambda at: state[at, :], coefs, state, rhs.at[1], early)
+
+    @region(start, 1)
+    def _():
+        out[:, pl.ds(0, width)] = product(lhs[...], rhs[1])
 
 
 def final_kernel(tm_axis, pairs, single, partial, *rest):
@@ -346,43 +368,65 @@
     for j, (x, y) in enumerate(pairs):
         i = len(single) + j
         rows = direct[i].shape[0] - TAIL
-        near = lambda i=i, rows=rows: direct[i][pl.ds(0, rows), :]
-        far = lambda i=i, rows=rows: swapped[i][pl.ds(0, rows), :]
+        near = lambda at=pl.ds(0, rows), i=i: direct[i][at, :]
+        far = lambda at=pl.ds(0, rows), i=i: swapped[i][at, :]
         items.append((near, direct[i], noise[len(single) + j], chosen(x - 1, y - 1)))
         items.append((far, swapped[i], noise[len(single) + len(pairs) + j], chosen(y - 1, x - 1)))
     for i, d in enumerate(single):
-        items.append((lambda i=i: lhs[i], direct[i], noise[i], chosen(d - 1, d - 1)))
-    for n, (_, source, _, message) in enumerate(items):
+        items.append((lambda at=slice(None), i=i: lhs[i, at, :], direct[i], noise[i], chosen(d - 1, d - 1)))
+
+    def prepare(n):
+        _, source, _, message = items[n]
         rows = source.shape[0] - TAIL
         x = [source[pl.ds(rows + 16 * j, 16), :].astype(F32) for j in range(4)]
         before = x[0][0:8] + x[0][8:16] + x[1][0:8]
         behind = x[1][8:16] + x[2][0:8] + x[2][8:16]
         lam = x[3][0:1] + x[3][1:2] + x[3][2:3]
         set_coefs(coefs.at[n], jnp.where(first, before, behind), lam, sums_of(message(pl.ds(vecs, 16))))
+
     late, early = halves_of(steps)
     width = vecs * len(late)
     work = [(h, n) for h in range(2) for n in range(count)]
 
-    def fill(h, n):
+    def fill(h, n, part=(0, 1)):
         start = items[n][3] if h == 0 else lambda at: state[n, at, :]
-        values(items[n][2], start, coefs.at[n], state.at[n], rhs.at[h, n], late if h == 0 else early)
-
+        values(items[n][2], start, coefs.at[n], state.at[n], rhs.at[h, n], late if h == 0 else early, part)
+
+    def output(h, part=None):
+        rows = result.shape[1]
+        take = pl.ds(0, rows) if part is None else pl.ds(part * (rows // 2), rows // 2)
+        at = pl.ds((1 - h) * width, width)
+        slot = 2 * len(single) + h + (part or 0)
+        return pltpu.make_async_copy(result.at[h, take, :], out.at[take, at], sems.at[slot])
+
+    prepare(0)
     fill(*work[0])
-    outs = []
     for k, (h, n) in enumerate(work):
-        if k + 1 < len(work):
-            fill(*work[k + 1])
-        if h == 0 and n == count - len(single):
+        if h == 0 and n == 2 * len(pairs):
             for copy in copies:
                 copy.wait()
-        term = product(items[n][0](), rhs[h, n])
         at = pl.ds((1 - h) * width, width)
-        result[h] = (partial[:, at] if n == 0 else result[h]) + term
-        if n == count - 1:
-            outs.append(pltpu.make_async_copy(result.at[h], out.at[:, at], sems.at[2 * len(single) + h]))
-            outs[-1].start()
-    for copy in outs:
-        copy.wait()
+        last = k + 1 == len(work)
+
+        @region(core, k)
+        def _():
+            rows = result.shape[1] // 2
+            if not last and work[k + 1][0] == 0:
+                prepare(work[k + 1][1])
+            for part in range(2):
+                take = pl.ds(part * rows, rows)
+                term = product(items[n][0](take), rhs[h, n])
+                result[h, take, :] = (partial[take, at] if n == 0 else result[h, take, :]) + term
+                if last:
+                    output(h, part).start()
+                else:
+                    fill(*work[k + 1], (part, 2))
+
+        if h == 0 and n == count - 1:
+            output(0).start()
+    output(0).wait()
+    output(1, 0).wait()
+    output(1, 1).wait()
 
 
 def kernel_call(body, **options):
@@ -402,19 +446,20 @@
     fast = dict(compiler_params=LIMIT)
     in_hbm = [
         pltpu.with_memory_space_constraint(x, pltpu.HBM)
-        for x in (coupling, spectrum.reshape(1, modes), spatial_basis)
+        for x in (coupling, spectrum.reshape(1, modes), spatial_basis, keys, counters)
     ]
 
     pairs, single = partners(space)
     routes = [(d, d) for d in single] + pairs
     sizes = [half + TAIL] * len(single) + [nodes_here + TAIL] * len(pairs)
     other = swap(coupling, "tm", 1)
-    *messages, coup, spec = kernel_call(
+    *messages, coup, spec, base = kernel_call(
         functools.partial(pack_kernel, "tm", "space", routes),
-        out_shape=[bf16(n, modes) for n in sizes] + [f32(steps, modes), f32(1, modes)],
-        in_specs=[HBM] * 3,
-        out_specs=[VMEM] * (len(sizes) + 2),
-        scratch_shapes=[pltpu.SemaphoreType.DMA((len(sizes) + 2,))],
+        out_shape=[bf16(n, modes) for n in sizes]
+        + [f32(steps, modes), f32(1, modes), jax.ShapeDtypeStruct((vecs, 128), jnp.int32)],
+        in_specs=[HBM] * 5,
+        out_specs=[VMEM] * (len(sizes) + 3),
+        scratch_shapes=[pltpu.VMEM((1, vecs), jnp.int32)] * 2 + [pltpu.SemaphoreType.DMA((len(sizes) + 4,))],
         **fast,
     )(*in_hbm)
     table, *messages = kernel_call(
@@ -429,22 +474,18 @@
     tables = [swap(table, "tm", 2 * e) for e in range(1, chips)]
     direct = [exchange(m, lambda t, s, r=r: (t, s ^ r[t % 2])) for m, r in zip(messages, routes)]
 
-    def noise_of(blocks, after, through=()):
-        count = len(blocks) * steps * vecs * modes
-        extras = len(after) + len(through)
+    def noise_of(offsets, after):
+        count = len(offsets) * steps * vecs * modes
         return kernel_call(
-            functools.partial(noise_kernel, "tm", "space", blocks, extras),
-            out_shape=[f32(steps, vecs, modes)] * len(blocks)
-            + [jax.ShapeDtypeStruct(x.shape, x.dtype) for x in through],
-            in_specs=[VMEM] * 2 + [ANY] * extras,
-            out_specs=[VMEM] * len(blocks) + [ANY] * len(through),
-            scratch_shapes=[pltpu.VMEM((vecs, 128), jnp.int32)],
-            input_output_aliases={2 + len(after) + i: len(blocks) + i for i in range(len(through))},
+            functools.partial(noise_kernel, "tm", "space", offsets, len(after)),
+            out_shape=[f32(steps, vecs, modes)] * len(offsets),
+            in_specs=[VMEM] + [ANY] * len(after),
+            out_specs=[VMEM] * len(offsets),
             cost_estimate=pl.CostEstimate(flops=count * 60, transcendentals=count * 2, bytes_accessed=count * 4),
             **fast,
-        )(keys, counters, *after, *through)
-
-    (own,) = noise_of([(0, (0, 0))], (table,))
+        )(base, *after)
+
+    (own,) = noise_of([(0, 0)], (table,))
     state, sent, weights, sums = kernel_call(
         functools.partial(offset_kernel, "tm"),
         out_shape=[f32(vecs, modes), bf16(vecs, modes), f32(chips, 8, modes), f32(8, modes)],
@@ -461,8 +502,8 @@
         **fast,
     )(state, swap(sent, "tm", 1), sums)
     later = [swap(total, "tm", 2 * e) for e in range(1, chips)]
-    noise = list(noise_of([(0, (d, d)) for d in single], (total,)))
-    noise += noise_of([(0, r) for r in pairs], (noise[-1],))
+    noise = list(noise_of([(d, d) for d in single], (total,)))
+    noise += noise_of(pairs, (noise[-1],))
     carry = kernel_call(
         functools.partial(carry_kernel, "tm"),
         out_shape=bf16(vecs + 16, modes),
@@ -472,7 +513,7 @@
     )(late, weights, sums, *later, noise[-1])
     carries = [swap(carry, "space", d) for d in range(1, space)]
     swapped = [swap(m, "tm", 1) for m in direct]
-    noise += noise_of([(0, r[::-1]) for r in pairs], (carry,))
+    noise += noise_of([r[::-1] for r in pairs], (carry,))
 
     flops = 2 * nodes_here * modes * steps * vecs
     half_cols = steps // 2 * vecs
@@ -486,7 +527,7 @@
             pltpu.VMEM((nodes_here, modes), BF16),
             pltpu.VMEM((2, half_cols, modes), BF16),
             pltpu.VMEM((vecs, modes), F32),
-            pltpu.VMEM((3, steps, modes), F32),
+            pltpu.VMEM((2, steps, modes), F32),
             pltpu.SemaphoreType.DMA,
         ],
         cost_estimate=pl.CostEstimate(flops=flops, transcendentals=0, bytes_accessed=4 * steps * vecs * modes),
@@ -502,9 +543,9 @@
             pltpu.VMEM((len(single), nodes_here, modes), BF16),
             pltpu.VMEM((2, count, half_cols, modes), BF16),
             pltpu.VMEM((count, vecs, modes), F32),
-            pltpu.VMEM((count, 3, steps, modes), F32),
+            pltpu.VMEM((count, 2, steps, modes), F32),
             pltpu.VMEM((2, nodes_here, half_cols), F32),
-            pltpu.SemaphoreType.DMA((2 * len(single) + 2,)),
+            pltpu.SemaphoreType.DMA((2 * len(single) + 3,)),
         ],
         cost_estimate=pl.CostEstimate(
             flops=flops * count, transcendentals=0, bytes_accessed=4 * steps * vecs * modes * count

time: 50.3 us -> 50.5 us (level)
  transfers between devices with their start and end apart: 15 -> 15, of which waited for: 7 -> 7; matrix products, arithmetic and copies ran while one was open for 0% -> 0% of each run, Pallas kernels for 19% -> 18%
where the time goes in v1:
time: 50.5 us; the launch traced here: 50.4 us
  waiting for transfers between devices  20.7 us (41%)
  starting transfers between devices  17.1 us (34%)
  Pallas kernels  12.4 us (25%)
    ppermute x2, waiting for transfers between devices, exchange(): return lax.ppermute(x, ('tm', 'space'), moves)  14.9 us
    ppermute x13, starting transfers between devices, swap(): return lax.ppermute(x, axis, [(i, i ^ offset) for i in range(count)])  13 us
    pallas_call x4, Pallas kernels, noise_of(): kernel_call(functools.partial(noise_kernel, 'tm', 'space', offsets, len(a...  6.62 us
    ppermute x13, waiting for transfers between devices, swap(): return lax.ppermute(x, axis, [(i, i ^ offset) for i in range(count)])  5.85 us
    ppermute x2, starting transfers between devices, exchange(): return lax.ppermute(x, ('tm', 'space'), moves)  4.16 us
    pallas_call x1, Pallas kernels, local(): kernel_call(functools.partial(final_kernel, 'tm', pairs, single), out_sha...  3.09 us
    pallas_call x1, Pallas kernels, local(): kernel_call(functools.partial(pack_kernel, 'tm', 'space', routes), out_sh...  1.24 us
  transfers between devices with their start and end apart: 15, of which 7 were waited for; matrix products, arithmetic and copies ran while one was open for 0% of the time, Pallas kernels for 18%

profile of v1, /device:TPU:0, one launch (start us, length us, event | category | flops | bytes accessed | tf_op | source)
XLA Modules:
  0.0 50.4 jit_solution(10303919567544645855)
XLA Ops:
  0.0 0.5 collective-permute-start
  0.5 1.2 %shard_map.55 = (bf16[320,512]{1,0:T(8,128)(2,1)S(1)}, bf16[576,512]{1,0:T(8,128)(2,1)S(1)}, f32[8,512]{1,0:T(8,128)S(1)}, f32[1,512]{1,0:T(1,128)S(1)}, s32[64,128]{1,0:T(8,128)S(1)}) custom-call(f32[8,512]{1,0:T(8,128)} %coup.1, f32[1,512]{1,0:T(1,128)} %bitcast.3, bf16[2048,512]{1,0:T(8,128)(2,1)} %basis.3, s32[1,64]{1,0:T(1,128)} %bitcast.4, s32[1,64]{1,0:T(1,128)} %bitcast.5), custom_call_target="tpu_custom_call" | custom-call | tf_op jit(solution)/shard_map/pallas_call | solution.py:456
  2.0 2.7 %collective-permute-start.9 = (bf16[576,512]{1,0:T(8,128)(2,1)S(1)}, bf16[576,512]{1,0:T(8,128)(2,1)S(1)}, u32[]{:S(2)}, u32[]{:S(2)}) collective-permute-start(bf16[576,512]{1,0:T(8,128)(2,1)S(1)} %get-tuple-element.32), channel_id=1, source_target_pairs={{0,1},{1,0},{2,3},{3,2},{4,6},{5,7},{6,4},{7,5},{8,9},{9,8},{10,11... | collective-permute-start | bytes 1769480 | tf_op jit(solution)/shard_map/ppermute | solution.py:33
  4.7 1.5 %collective-permute-start.8 = (bf16[320,512]{1,0:T(8,128)(2,1)S(1)}, bf16[320,512]{1,0:T(8,128)(2,1)S(1)}, u32[]{:S(2)}, u32[]{:S(2)}) collective-permute-start(bf16[320,512]{1,0:T(8,128)(2,1)S(1)} %get-tuple-element.31), channel_id=1, source_target_pairs={{0,3},{1,2},{2,1},{3,0},{4,7},{5,6},{6,5},{7,4},{8,11},{9,10},{10,... | collective-permute-start | bytes 983048 | tf_op jit(solution)/shard_map/ppermute | solution.py:33
  6.2 9.9 %collective-permute-done.9.rest_1_ = bf16[576,512]{1,0:T(8,128)(2,1)S(1)} collective-permute-done((bf16[576,512]{1,0:T(8,128)(2,1)S(1)}, bf16[576,512]{1,0:T(8,128)(2,1)S(1)}, u32[]{:S(2)}, u32[]{:S(2)}) %collective-permute-start.9) | collective-permute-done | bytes 589856 | tf_op jit(solution)/shard_map/ppermute | solution.py:33
  16.0 5.0 %collective-permute-done.8.rest_0_ = bf16[320,512]{1,0:T(8,128)(2,1)S(1)} collective-permute-done((bf16[320,512]{1,0:T(8,128)(2,1)S(1)}, bf16[320,512]{1,0:T(8,128)(2,1)S(1)}, u32[]{:S(2)}, u32[]{:S(2)}) %collective-permute-start.8) | collective-permute-done | bytes 327712 | tf_op jit(solution)/shard_map/ppermute | solution.py:33
  21.0 3.6 %collective-permute-start.3 = (f32[8,512]{1,0:T(8,128)S(1)}, f32[8,512]{1,0:T(8,128)S(1)}, u32[]{:S(2)}, u32[]{:S(2)}) collective-permute-start(f32[8,512]{1,0:T(8,128)S(1)} %get-tuple-element.24.rest_0_.table), channel_id=1, source_target_pairs={{0,24},{4,28},{8,16},{12,20},{16,8},{20,12},{24,0},{28,4},{1,25},{... | collective-permute-start | bytes 49160 | tf_op jit(solution)/shard_map/ppermute | solution.py:38
  24.6 0.8 %collective-permute-start.1 = (f32[8,512]{1,0:T(8,128)S(1)}, f32[8,512]{1,0:T(8,128)S(1)}, u32[]{:S(2)}, u32[]{:S(2)}) collective-permute-start(f32[8,512]{1,0:T(8,128)S(1)} %get-tuple-element.24.rest_0_.table), channel_id=1, source_target_pairs={{0,8},{4,12},{8,0},{12,4},{16,24},{20,28},{24,16},{28,20},{1,9},{5... | collective-permute-start | bytes 49160 | tf_op jit(solution)/shard_map/ppermute | solution.py:38
  25.4 1.7 %shard_map.57.noise = f32[8,64,512]{2,1,0:T(8,128)S(1)} custom-call(s32[64,128]{1,0:T(8,128)S(1)} %get-tuple-element.21.base, f32[8,512]{1,0:T(8,128)S(1)} %get-tuple-element.24.rest_0_.table), custom_call_target="tpu_custom_call" | custom-call | flops 15728640 | bytes 1048576 | tf_op jit(solution)/shard_map/pallas_call | solution.py:479
  27.1 2.2 %collective-permute-done.2.rest_1_ = f32[8,512]{1,0:T(8,128)S(1)} collective-permute-done((f32[8,512]{1,0:T(8,128)S(1)}, f32[8,512]{1,0:T(8,128)S(1)}, u32[]{:S(2)}, u32[]{:S(2)}) %collective-permute-start.2) | collective-permute-done | bytes 16416 | tf_op jit(solution)/shard_map/ppermute | solution.py:38
  29.6 1.2 %collective-permute-done.4.other = bf16[64,512]{1,0:T(8,128)(2,1)S(1)} collective-permute-done((bf16[64,512]{1,0:T(8,128)(2,1)S(1)}, bf16[64,512]{1,0:T(8,128)(2,1)S(1)}, u32[]{:S(2)}, u32[]{:S(2)}) %collective-permute-start.4) | collective-permute-done | bytes 65568 | tf_op jit(solution)/shard_map/ppermute | solution.py:38
  30.9 1.5 %collective-permute-start.7 = (bf16[64,512]{1,0:T(8,128)(2,1)S(1)}, bf16[64,512]{1,0:T(8,128)(2,1)S(1)}, u32[]{:S(2)}, u32[]{:S(2)}) collective-permute-start(bf16[64,512]{1,0:T(8,128)(2,1)S(1)} %get-tuple-element.30.rest_0_), channel_id=1, source_target_pairs={{0,24},{4,28},{8,16},{12,20},{16,8},{20,12},{24,0},{28,4},{1,25},{... | collective-permute-start | bytes 196616 | tf_op jit(solution)/shard_map/ppermute | solution.py:38
  32.4 0.6 %collective-permute-start.6 = (bf16[64,512]{1,0:T(8,128)(2,1)S(1)}, bf16[64,512]{1,0:T(8,128)(2,1)S(1)}, u32[]{:S(2)}, u32[]{:S(2)}) collective-permute-start(bf16[64,512]{1,0:T(8,128)(2,1)S(1)} %get-tuple-element.30.rest_0_), channel_id=1, source_target_pairs={{0,16},{4,20},{8,24},{12,28},{16,0},{20,4},{24,8},{28,12},{1,17},{... | collective-permute-start | bytes 196616 | tf_op jit(solution)/shard_map/ppermute | solution.py:38
  33.1 2.3 %collective-permute-start.5 = (bf16[64,512]{1,0:T(8,128)(2,1)S(1)}, bf16[64,512]{1,0:T(8,128)(2,1)S(1)}, u32[]{:S(2)}, u32[]{:S(2)}) collective-permute-start(bf16[64,512]{1,0:T(8,128)(2,1)S(1)} %get-tuple-element.30.rest_0_), channel_id=1, source_target_pairs={{0,8},{4,12},{8,0},{12,4},{16,24},{20,28},{24,16},{28,20},{1,9},{5... | collective-permute-start | bytes 196616 | tf_op jit(solution)/shard_map/ppermute | solution.py:38
  35.4 1.7 %shard_map.60.rest_0_.rest_4_ = f32[8,64,512]{2,1,0:T(8,128)S(1)} custom-call(s32[64,128]{1,0:T(8,128)S(1)} %get-tuple-element.21.base, bf16[64,512]{1,0:T(8,128)(2,1)S(1)} %get-tuple-element.30.rest_0_), custom_call_target="tpu_custom_call" | custom-call | flops 15728640 | bytes 1048576 | tf_op jit(solution)/shard_map/pallas_call | solution.py:479
  37.0 1.7 %shard_map.61.rest_3_.rest_5_ = f32[8,64,512]{2,1,0:T(8,128)S(1)} custom-call(s32[64,128]{1,0:T(8,128)S(1)} %get-tuple-element.21.base, f32[8,64,512]{2,1,0:T(8,128)S(1)} %shard_map.60.rest_0_.rest_4_), custom_call_target="tpu_custom_call" | custom-call | flops 15728640 | bytes 1048576 | tf_op jit(solution)/shard_map/pallas_call | solution.py:479
  38.7 1.0 %collective-permute-done.6.rest_1_ = bf16[64,512]{1,0:T(8,128)(2,1)S(1)} collective-permute-done((bf16[64,512]{1,0:T(8,128)(2,1)S(1)}, bf16[64,512]{1,0:T(8,128)(2,1)S(1)}, u32[]{:S(2)}, u32[]{:S(2)}) %collective-permute-start.6) | collective-permute-done | bytes 65568 | tf_op jit(solution)/shard_map/ppermute | solution.py:38
  39.8 1.5 %collective-permute-start.14 = (bf16[80,512]{1,0:T(8,128)(2,1)S(1)}, bf16[80,512]{1,0:T(8,128)(2,1)S(1)}, u32[]{:S(2)}, u32[]{:S(2)}) collective-permute-start(bf16[80,512]{1,0:T(8,128)(2,1)S(1)} %shard_map.62.message.rest_0_), channel_id=1, source_target_pairs={{0,3},{1,2},{2,1},{3,0},{4,7},{5,6},{6,5},{7,4},{8,11},{9,10},{10,... | collective-permute-start | bytes 245768 | tf_op jit(solution)/shard_map/ppermute | solution.py:38
  41.3 1.5 %collective-permute-start.13 = (bf16[80,512]{1,0:T(8,128)(2,1)S(1)}, bf16[80,512]{1,0:T(8,128)(2,1)S(1)}, u32[]{:S(2)}, u32[]{:S(2)}) collective-permute-start(bf16[80,512]{1,0:T(8,128)(2,1)S(1)} %shard_map.62.message.rest_0_), channel_id=1, source_target_pairs={{0,2},{1,3},{2,0},{3,1},{4,6},{5,7},{6,4},{7,5},{8,10},{9,11},{10,... | collective-permute-start | bytes 245768 | tf_op jit(solution)/shard_map/ppermute | solution.py:38
  42.9 0.5 %collective-permute-start.12 = (bf16[80,512]{1,0:T(8,128)(2,1)S(1)}, bf16[80,512]{1,0:T(8,128)(2,1)S(1)}, u32[]{:S(2)}, u32[]{:S(2)}) collective-permute-start(bf16[80,512]{1,0:T(8,128)(2,1)S(1)} %shard_map.62.message.rest_0_), channel_id=1, source_target_pairs={{0,1},{1,0},{2,3},{3,2},{4,5},{5,4},{6,7},{7,6},{8,9},{9,8},{10,11... | collective-permute-start | bytes 245768 | tf_op jit(solution)/shard_map/ppermute | solution.py:38
  43.4 1.7 %shard_map.64.rest_6_ = f32[8,64,512]{2,1,0:T(8,128)S(1)} custom-call(s32[64,128]{1,0:T(8,128)S(1)} %get-tuple-element.21.base, bf16[80,512]{1,0:T(8,128)(2,1)S(1)} %shard_map.62.message.rest_0_), custom_call_target="tpu_custom_call" | custom-call | flops 15728640 | bytes 1048576 | tf_op jit(solution)/shard_map/pallas_call | solution.py:479
  45.0 0.8 %shard_map.63.partial = f32[512,512]{1,0:T(8,128)S(1)} custom-call(f32[8,512]{1,0:T(8,128)S(1)} %get-tuple-element.19.coup, f32[1,512]{1,0:T(1,128)S(1)} %get-tuple-element.20.spec, bf16[2048,512]{1,0:T(8,128)(2,1)S(1)} %copy-done, f32[8,64,512]{2,1,0:T(8,128)S(1)} %shard_map.57.noise, bf16[80,512]{1,0:T(8,128)(2,1)S(1)} %shard_map.62.message.rest_0_), custom_call_target="tpu_custom_call" | custom-call | flops 268435456 | bytes 1048576 | tf_op jit(solution)/shard_map/pallas_call | solution.py:521
  45.9 1.0 %collective-permute-done.13.rest_8_ = bf16[80,512]{1,0:T(8,128)(2,1)S(1)} collective-permute-done((bf16[80,512]{1,0:T(8,128)(2,1)S(1)}, bf16[80,512]{1,0:T(8,128)(2,1)S(1)}, u32[]{:S(2)}, u32[]{:S(2)}) %collective-permute-start.13) | collective-permute-done | bytes 81952 | tf_op jit(solution)/shard_map/ppermute | solution.py:38
  47.3 3.1 %shard_map.65 = f32[512,512]{1,0:T(8,128)} custom-call(f32[512,512]{1,0:T(8,128)S(1)} %shard_map.63.partial, bf16[320,512]{1,0:T(8,128)(2,1)S(1)} %collective-permute-done.8.rest_0_, bf16[576,512]{1,0:T(8,128)(2,1)S(1)} %collective-permute-done.9.rest_1_, bf16[320,512]{1,0:T(8,128)(2,1)S(1)} %collective-permute-done.10.rest_2_, ...), custom_call_target="tpu_custom_call" | custom-call | flops 805306368 | bytes 3145728 | tf_op jit(solution)/shard_map/pallas_call | solution.py:537
  (19 shorter events, 1.1 us)
Async XLA Ops:
  0.0 1.7 %collective-permute-start = (f32[8,512]{1,0:T(8,128)}, f32[8,512]{1,0:T(8,128)S(1)}, u32[]{:S(2)}, u32[]{:S(2)}) collective-permute-start(f32[8,512]{1,0:T(8,128)} %coup.1), channel_id=1, source_target_pairs={{0,4},{4,0},{8,12},{12,8},{16,20},{20,16},{24,28},{28,24},{1,5},{5... | collective-permute-start | bytes 49160 | tf_op jit(solution)/shard_map/ppermute | solution.py:38
  2.0 14.0 %collective-permute-start.9 = (bf16[576,512]{1,0:T(8,128)(2,1)S(1)}, bf16[576,512]{1,0:T(8,128)(2,1)S(1)}, u32[]{:S(2)}, u32[]{:S(2)}) collective-permute-start(bf16[576,512]{1,0:T(8,128)(2,1)S(1)} %get-tuple-element.32), channel_id=1, source_target_pairs={{0,1},{1,0},{2,3},{3,2},{4,6},{5,7},{6,4},{7,5},{8,9},{9,8},{10,11... | collective-permute-start | bytes 1769480 | tf_op jit(solution)/shard_map/ppermute | solution.py:33
  4.7 16.4 %collective-permute-start.8 = (bf16[320,512]{1,0:T(8,128)(2,1)S(1)}, bf16[320,512]{1,0:T(8,128)(2,1)S(1)}, u32[]{:S(2)}, u32[]{:S(2)}) collective-permute-start(bf16[320,512]{1,0:T(8,128)(2,1)S(1)} %get-tuple-element.31), channel_id=1, source_target_pairs={{0,3},{1,2},{2,1},{3,0},{4,7},{5,6},{6,5},{7,4},{8,11},{9,10},{10,... | collective-permute-start | bytes 983048 | tf_op jit(solution)/shard_map/ppermute | solution.py:33
  16.0 31.3 %collective-permute-start.11 = (bf16[576,512]{1,0:T(8,128)(2,1)S(1)}, bf16[576,512]{1,0:T(8,128)(2,1)S(1)}, u32[]{:S(2)}, u32[]{:S(2)}) collective-permute-start(bf16[576,512]{1,0:T(8,128)(2,1)S(1)} %collective-permute-done.9.rest_1_), channel_id=1, source_target_pairs={{0,4},{4,0},{8,12},{12,8},{16,20},{20,16},{24,28},{28,24},{1,5},{5... | collective-permute-start | bytes 1769480 | tf_op jit(solution)/shard_map/ppermute | solution.py:38
  21.0 26.3 %collective-permute-start.10 = (bf16[320,512]{1,0:T(8,128)(2,1)S(1)}, bf16[320,512]{1,0:T(8,128)(2,1)S(1)}, u32[]{:S(2)}, u32[]{:S(2)}) collective-permute-start(bf16[320,512]{1,0:T(8,128)(2,1)S(1)} %collective-permute-done.8.rest_0_), channel_id=1, source_target_pairs={{0,4},{4,0},{8,12},{12,8},{16,20},{20,16},{24,28},{28,24},{1,5},{5... | collective-permute-start | bytes 983048 | tf_op jit(solution)/shard_map/ppermute | solution.py:38
  21.0 6.0 %collective-permute-start.3 = (f32[8,512]{1,0:T(8,128)S(1)}, f32[8,512]{1,0:T(8,128)S(1)}, u32[]{:S(2)}, u32[]{:S(2)}) collective-permute-start(f32[8,512]{1,0:T(8,128)S(1)} %get-tuple-element.24.rest_0_.table), channel_id=1, source_target_pairs={{0,24},{4,28},{8,16},{12,20},{16,8},{20,12},{24,0},{28,4},{1,25},{... | collective-permute-start | bytes 49160 | tf_op jit(solution)/shard_map/ppermute | solution.py:38
  24.6 4.6 %collective-permute-start.2 = (f32[8,512]{1,0:T(8,128)S(1)}, f32[8,512]{1,0:T(8,128)S(1)}, u32[]{:S(2)}, u32[]{:S(2)}) collective-permute-start(f32[8,512]{1,0:T(8,128)S(1)} %get-tuple-element.24.rest_0_.table), channel_id=1, source_target_pairs={{0,16},{4,20},{8,24},{12,28},{16,0},{20,4},{24,8},{28,12},{1,17},{... | collective-permute-start | bytes 49160 | tf_op jit(solution)/shard_map/ppermute | solution.py:38
  24.6 4.6 %collective-permute-start.1 = (f32[8,512]{1,0:T(8,128)S(1)}, f32[8,512]{1,0:T(8,128)S(1)}, u32[]{:S(2)}, u32[]{:S(2)}) collective-permute-start(f32[8,512]{1,0:T(8,128)S(1)} %get-tuple-element.24.rest_0_.table), channel_id=1, source_target_pairs={{0,8},{4,12},{8,0},{12,4},{16,24},{20,28},{24,16},{28,20},{1,9},{5... | collective-permute-start | bytes 49160 | tf_op jit(solution)/shard_map/ppermute | solution.py:38
  29.6 1.3 %collective-permute-start.4 = (bf16[64,512]{1,0:T(8,128)(2,1)S(1)}, bf16[64,512]{1,0:T(8,128)(2,1)S(1)}, u32[]{:S(2)}, u32[]{:S(2)}) collective-permute-start(bf16[64,512]{1,0:T(8,128)(2,1)S(1)} %get-tuple-element.26), channel_id=1, source_target_pairs={{0,4},{4,0},{8,12},{12,8},{16,20},{20,16},{24,28},{28,24},{1,5},{5... | collective-permute-start | bytes 196616 | tf_op jit(solution)/shard_map/ppermute | solution.py:38
  30.9 7.8 %collective-permute-start.7 = (bf16[64,512]{1,0:T(8,128)(2,1)S(1)}, bf16[64,512]{1,0:T(8,128)(2,1)S(1)}, u32[]{:S(2)}, u32[]{:S(2)}) collective-permute-start(bf16[64,512]{1,0:T(8,128)(2,1)S(1)} %get-tuple-element.30.rest_0_), channel_id=1, source_target_pairs={{0,24},{4,28},{8,16},{12,20},{16,8},{20,12},{24,0},{28,4},{1,25},{... | collective-permute-start | bytes 196616 | tf_op jit(solution)/shard_map/ppermute | solution.py:38
  32.4 7.3 %collective-permute-start.6 = (bf16[64,512]{1,0:T(8,128)(2,1)S(1)}, bf16[64,512]{1,0:T(8,128)(2,1)S(1)}, u32[]{:S(2)}, u32[]{:S(2)}) collective-permute-start(bf16[64,512]{1,0:T(8,128)(2,1)S(1)} %get-tuple-element.30.rest_0_), channel_id=1, source_target_pairs={{0,16},{4,20},{8,24},{12,28},{16,0},{20,4},{24,8},{28,12},{1,17},{... | collective-permute-start | bytes 196616 | tf_op jit(solution)/shard_map/ppermute | solution.py:38
  33.1 6.7 %collective-permute-start.5 = (bf16[64,512]{1,0:T(8,128)(2,1)S(1)}, bf16[64,512]{1,0:T(8,128)(2,1)S(1)}, u32[]{:S(2)}, u32[]{:S(2)}) collective-permute-start(bf16[64,512]{1,0:T(8,128)(2,1)S(1)} %get-tuple-element.30.rest_0_), channel_id=1, source_target_pairs={{0,8},{4,12},{8,0},{12,4},{16,24},{20,28},{24,16},{28,20},{1,9},{5... | collective-permute-start | bytes 196616 | tf_op jit(solution)/shard_map/ppermute | solution.py:38
  37.0 8.0 %copy-start = (bf16[2048,512]{1,0:T(8,128)(2,1)S(1)}, bf16[2048,512]{1,0:T(8,128)(2,1)}, u32[]{:S(2)}) copy-start(bf16[2048,512]{1,0:T(8,128)(2,1)} %basis.3) | copy-start | bytes 6291460
  39.8 6.1 %collective-permute-start.14 = (bf16[80,512]{1,0:T(8,128)(2,1)S(1)}, bf16[80,512]{1,0:T(8,128)(2,1)S(1)}, u32[]{:S(2)}, u32[]{:S(2)}) collective-permute-start(bf16[80,512]{1,0:T(8,128)(2,1)S(1)} %shard_map.62.message.rest_0_), channel_id=1, source_target_pairs={{0,3},{1,2},{2,1},{3,0},{4,7},{5,6},{6,5},{7,4},{8,11},{9,10},{10,... | collective-permute-start | bytes 245768 | tf_op jit(solution)/shard_map/ppermute | solution.py:38
  41.3 5.6 %collective-permute-start.13 = (bf16[80,512]{1,0:T(8,128)(2,1)S(1)}, bf16[80,512]{1,0:T(8,128)(2,1)S(1)}, u32[]{:S(2)}, u32[]{:S(2)}) collective-permute-start(bf16[80,512]{1,0:T(8,128)(2,1)S(1)} %shard_map.62.message.rest_0_), channel_id=1, source_target_pairs={{0,2},{1,3},{2,0},{3,1},{4,6},{5,7},{6,4},{7,5},{8,10},{9,11},{10,... | collective-permute-start | bytes 245768 | tf_op jit(solution)/shard_map/ppermute | solution.py:38
  42.9 4.4 %collective-permute-start.12 = (bf16[80,512]{1,0:T(8,128)(2,1)S(1)}, bf16[80,512]{1,0:T(8,128)(2,1)S(1)}, u32[]{:S(2)}, u32[]{:S(2)}) collective-permute-start(bf16[80,512]{1,0:T(8,128)(2,1)S(1)} %shard_map.62.message.rest_0_), channel_id=1, source_target_pairs={{0,1},{1,0},{2,3},{3,2},{4,5},{5,4},{6,7},{7,6},{8,9},{9,8},{10,11... | collective-permute-start | bytes 245768 | tf_op jit(solution)/shard_map/ppermute | solution.py:38

commit v2 on v1

--- a/solution.py
+++ b/solution.py
@@ -258,23 +258,35 @@
 
 
 def combine_kernel(tm_axis, own, other, df, out, late):
-    first = lax.rem(lax.axis_index(tm_axis), 2) == 0
-    x, y = own[...], other[...].astype(F32)
-    behind = jnp.where(first, y, x)
-    out[...] = (jnp.where(first, x, y) + df[pl.ds(2, 1), :] * behind).astype(BF16)
-    late[...] = behind
-
-
-def carry_kernel(tm_axis, late, wts, df, *rest):
-    *received, _, out = rest
-    vecs, modes = late.shape
-    me = lax.axis_index(tm_axis)
-    first = lax.rem(me, 2) == 0
-    carry = jnp.zeros(late.shape, F32)
+    core = lax.rem(lax.axis_index(tm_axis), 2)
+    first = core == 0
+    half = out.shape[0]
+    late[...] = jnp.where(first, other[...].astype(F32), own[...])
+    at = pl.ds(pl.multiple_of(core * half, half), half)
+    x, y = own[at, :], other[at, :].astype(F32)
+    out[...] = (jnp.where(first, x, y) + df[pl.ds(2, 1), :] * jnp.where(first, y, x)).astype(BF16)
+
+
+def half_kernel(tm_axis, wts, *rest):
+    *received, _, out, sent = rest
+    chip = lax.axis_index(tm_axis) // 2
+    carry = jnp.zeros(out.shape, F32)
     for e, ref in enumerate(received):
-        carry = carry + wts[(me // 2) ^ (e + 1)][0:1, :] * ref[...].astype(F32)
-    out[pl.ds(0, vecs), :] = jnp.where(first, late[...] + df[pl.ds(3, 1), :] * carry, carry).astype(BF16)
-    out[pl.ds(vecs, 16), :] = table_rows((16, modes), split3(df[pl.ds(0, 1), :]) + split3(df[pl.ds(1, 1), :])).astype(BF16)
+        carry = carry + wts[chip ^ (e + 1)][0:1, :] * ref[...].astype(F32)
+    out[...] = carry
+    sent[...] = carry.astype(BF16)
+
+
+def carry_kernel(tm_axis, mine, theirs, late, df, _, out):
+    half, modes = mine.shape
+    core = lax.rem(lax.axis_index(tm_axis), 2)
+    gain = df[pl.ds(3, 1), :]
+    for j in range(2):
+        at = pl.ds(j * half, half)
+        carry = jnp.where(core == j, mine[...], theirs[...].astype(F32))
+        out[at, :] = jnp.where(core == 0, late[at, :] + gain * carry, carry).astype(BF16)
+    parts = split3(df[pl.ds(0, 1), :]) + split3(df[pl.ds(1, 1), :])
+    out[pl.ds(2 * half, 16), :] = table_rows((16, modes), parts).astype(BF16)
 
 
 def sums_of(block):
@@ -312,10 +324,6 @@
     return times[: steps // 2], times[steps // 2 :]
 
 
-def region(position, n):
-    return pl.when(position >= -n)
-
-
 def own_kernel(sp_axis, coup, spec, basis, noise, message, out, lhs, rhs, state, coefs, sem):
     rows = lhs.shape[0]
     steps, vecs, _ = noise.shape
@@ -327,15 +335,9 @@
     width = vecs * len(late)
     values(noise, lambda at: message[at, :].astype(F32), coefs, state, rhs.at[0], late)
     copy.wait()
-
-    @region(start, 0)
-    def _():
-        out[:, pl.ds(width, width)] = product(lhs[...], rhs[0])
-        values(noise, lambda at: state[at, :], coefs, state, rhs.at[1], early)
-
-    @region(start, 1)
-    def _():
-        out[:, pl.ds(0, width)] = product(lhs[...], rhs[1])
+    values(noise, lambda at: state[at, :], coefs, state, rhs.at[1], early)
+    out[:, pl.ds(width, width)] = product(lhs[...], rhs[0])
+    out[:, pl.ds(0, width)] = product(lhs[...], rhs[1])
 
 
 def final_kernel(tm_axis, pairs, single, partial, *rest):
@@ -368,65 +370,43 @@
     for j, (x, y) in enumerate(pairs):
         i = len(single) + j
         rows = direct[i].shape[0] - TAIL
-        near = lambda at=pl.ds(0, rows), i=i: direct[i][at, :]
-        far = lambda at=pl.ds(0, rows), i=i: swapped[i][at, :]
+        near = lambda i=i, rows=rows: direct[i][pl.ds(0, rows), :]
+        far = lambda i=i, rows=rows: swapped[i][pl.ds(0, rows), :]
         items.append((near, direct[i], noise[len(single) + j], chosen(x - 1, y - 1)))
         items.append((far, swapped[i], noise[len(single) + len(pairs) + j], chosen(y - 1, x - 1)))
     for i, d in enumerate(single):
-        items.append((lambda at=slice(None), i=i: lhs[i, at, :], direct[i], noise[i], chosen(d - 1, d - 1)))
-
-    def prepare(n):
-        _, source, _, message = items[n]
+        items.append((lambda i=i: lhs[i], direct[i], noise[i], chosen(d - 1, d - 1)))
+    for n, (_, source, _, message) in enumerate(items):
         rows = source.shape[0] - TAIL
         x = [source[pl.ds(rows + 16 * j, 16), :].astype(F32) for j in range(4)]
         before = x[0][0:8] + x[0][8:16] + x[1][0:8]
         behind = x[1][8:16] + x[2][0:8] + x[2][8:16]
         lam = x[3][0:1] + x[3][1:2] + x[3][2:3]
         set_coefs(coefs.at[n], jnp.where(first, before, behind), lam, sums_of(message(pl.ds(vecs, 16))))
-
     late, early = halves_of(steps)
     width = vecs * len(late)
     work = [(h, n) for h in range(2) for n in range(count)]
 
-    def fill(h, n, part=(0, 1)):
+    def fill(h, n):
         start = items[n][3] if h == 0 else lambda at: state[n, at, :]
-        values(items[n][2], start, coefs.at[n], state.at[n], rhs.at[h, n], late if h == 0 else early, part)
-
-    def output(h, part=None):
-        rows = result.shape[1]
-        take = pl.ds(0, rows) if part is None else pl.ds(part * (rows // 2), rows // 2)
-        at = pl.ds((1 - h) * width, width)
-        slot = 2 * len(single) + h + (part or 0)
-        return pltpu.make_async_copy(result.at[h, take, :], out.at[take, at], sems.at[slot])
-
-    prepare(0)
+        values(items[n][2], start, coefs.at[n], state.at[n], rhs.at[h, n], late if h == 0 else early)
+
     fill(*work[0])
+    outs = []
     for k, (h, n) in enumerate(work):
-        if h == 0 and n == 2 * len(pairs):
+        if k + 1 < len(work):
+            fill(*work[k + 1])
+        if h == 0 and n == count - len(single):
             for copy in copies:
                 copy.wait()
+        term = product(items[n][0](), rhs[h, n])
         at = pl.ds((1 - h) * width, width)
-        last = k + 1 == len(work)
-
-        @region(core, k)
-        def _():
-            rows = result.shape[1] // 2
-            if not last and work[k + 1][0] == 0:
-                prepare(work[k + 1][1])
-            for part in range(2):
-                take = pl.ds(part * rows, rows)
-                term = product(items[n][0](take), rhs[h, n])
-                result[h, take, :] = (partial[take, at] if n == 0 else result[h, take, :]) + term
-                if last:
-                    output(h, part).start()
-                else:
-                    fill(*work[k + 1], (part, 2))
-
-        if h == 0 and n == count - 1:
-            output(0).start()
-    output(0).wait()
-    output(1, 0).wait()
-    output(1, 1).wait()
+        result[h] = (partial[:, at] if n == 0 else result[h]) + term
+        if n == count - 1:
+            outs.append(pltpu.make_async_copy(result.at[h], out.at[:, at], sems.at[2 * len(single) + h]))
+            outs[-1].start()
+    for copy in outs:
+        copy.wait()
 
 
 def kernel_call(body, **options):
@@ -496,21 +476,29 @@
     )(own, coup, spec, table, *tables)
     total, late = kernel_call(
         functools.partial(combine_kernel, "tm"),
-        out_shape=[bf16(vecs, modes), f32(vecs, modes)],
+        out_shape=[bf16(vecs // 2, modes), f32(vecs, modes)],
         in_specs=[VMEM] * 3,
         out_specs=[VMEM] * 2,
         **fast,
     )(state, swap(sent, "tm", 1), sums)
     later = [swap(total, "tm", 2 * e) for e in range(1, chips)]
     noise = list(noise_of([(d, d) for d in single], (total,)))
-    noise += noise_of(pairs, (noise[-1],))
+    mine, sent = kernel_call(
+        functools.partial(half_kernel, "tm"),
+        out_shape=[f32(vecs // 2, modes), bf16(vecs // 2, modes)],
+        in_specs=[VMEM] * (1 + len(later)) + [ANY],
+        out_specs=[VMEM] * 2,
+        **fast,
+    )(weights, *later, noise[-1])
+    theirs = swap(sent, "tm", 1)
+    noise += noise_of(pairs, (sent,))
     carry = kernel_call(
         functools.partial(carry_kernel, "tm"),
         out_shape=bf16(vecs + 16, modes),
-        in_specs=[VMEM] * (3 + len(later)) + [ANY],
+        in_specs=[VMEM] * 4 + [ANY],
         out_specs=VMEM,
         **fast,
-    )(late, weights, sums, *later, noise[-1])
+    )(mine, theirs, late, sums, noise[-1])
     carries = [swap(carry, "space", d) for d in range(1, space)]
     swapped = [swap(m, "tm", 1) for m in direct]
     noise += noise_of([r[::-1] for r in pairs], (carry,))
@@ -545,7 +533,7 @@
             pltpu.VMEM((count, vecs, modes), F32),
             pltpu.VMEM((count, 2, steps, modes), F32),
             pltpu.VMEM((2, nodes_here, half_cols), F32),
-            pltpu.SemaphoreType.DMA((2 * len(single) + 3,)),
+            pltpu.SemaphoreType.DMA((2 * len(single) + 2,)),
         ],
         cost_estimate=pl.CostEstimate(
             flops=flops * count, transcendentals=0, bytes_accessed=4 * steps * vecs * modes * count

time: 50.5 us -> 50 us (0.990)
    ppermute x13 -> x14, waiting for transfers between devices: 5.85 us -> 5.74 us  [swap(): return lax.ppermute(x, axis, [(i, i ^ offset) for i in range(count)])]
    ppermute x13 -> x14, starting transfers between devices: 13 us -> 13 us  [swap(): return lax.ppermute(x, axis, [(i, i ^ offset) for i in range(count)])]
  transfers between devices with their start and end apart: 15 -> 16, of which waited for: 7 -> 8; matrix products, arithmetic and copies ran while one was open for 0% -> 0% of each run, Pallas kernels for 18% -> 18%
where the time goes in v2:
time: 50 us; the launch traced here: 49.8 us
  waiting for transfers between devices  20.6 us (41%)
  starting transfers between devices  17.2 us (34%)
  Pallas kernels  11.9 us (24%)
    ppermute x2, waiting for transfers between devices, exchange(): return lax.ppermute(x, ('tm', 'space'), moves)  14.9 us
    ppermute x14, starting transfers between devices, swap(): return lax.ppermute(x, axis, [(i, i ^ offset) for i in range(count)])  13 us
    pallas_call x4, Pallas kernels, noise_of(): kernel_call(functools.partial(noise_kernel, 'tm', 'space', offsets, len(a...  6.62 us
    ppermute x14, waiting for transfers between devices, swap(): return lax.ppermute(x, axis, [(i, i ^ offset) for i in range(count)])  5.74 us
    ppermute x2, starting transfers between devices, exchange(): return lax.ppermute(x, ('tm', 'space'), moves)  4.16 us
    pallas_call x1, Pallas kernels, local(): kernel_call(functools.partial(final_kernel, 'tm', pairs, single), out_sha...  2.75 us
    pallas_call x1, Pallas kernels, local(): kernel_call(functools.partial(pack_kernel, 'tm', 'space', routes), out_sh...  1.24 us
  transfers between devices with their start and end apart: 16, of which 8 were waited for; matrix products, arithmetic and copies ran while one was open for 0% of the time, Pallas kernels for 18%

profile of v2, /device:TPU:0, one launch (start us, length us, event | category | flops | bytes accessed | tf_op | source)
XLA Modules:
  0.0 49.8 jit_solution(7083781373701078209)
XLA Ops:
  0.0 0.5 collective-permute-start
  0.5 1.2 %shard_map.55 = (bf16[320,512]{1,0:T(8,128)(2,1)S(1)}, bf16[576,512]{1,0:T(8,128)(2,1)S(1)}, f32[8,512]{1,0:T(8,128)S(1)}, f32[1,512]{1,0:T(1,128)S(1)}, s32[64,128]{1,0:T(8,128)S(1)}) custom-call(f32[8,512]{1,0:T(8,128)} %coup.1, f32[1,512]{1,0:T(1,128)} %bitcast.3, bf16[2048,512]{1,0:T(8,128)(2,1)} %basis.3, s32[1,64]{1,0:T(1,128)} %bitcast.4, s32[1,64]{1,0:T(1,128)} %bitcast.5), custom_call_target="tpu_custom_call" | custom-call | tf_op jit(solution)/shard_map/pallas_call | solution.py:436
  2.0 2.7 %collective-permute-start.10 = (bf16[576,512]{1,0:T(8,128)(2,1)S(1)}, bf16[576,512]{1,0:T(8,128)(2,1)S(1)}, u32[]{:S(2)}, u32[]{:S(2)}) collective-permute-start(bf16[576,512]{1,0:T(8,128)(2,1)S(1)} %get-tuple-element.36), channel_id=1, source_target_pairs={{0,1},{1,0},{2,3},{3,2},{4,6},{5,7},{6,4},{7,5},{8,9},{9,8},{10,11... | collective-permute-start | bytes 1769480 | tf_op jit(solution)/shard_map/ppermute | solution.py:33
  4.7 1.5 %collective-permute-start.9 = (bf16[320,512]{1,0:T(8,128)(2,1)S(1)}, bf16[320,512]{1,0:T(8,128)(2,1)S(1)}, u32[]{:S(2)}, u32[]{:S(2)}) collective-permute-start(bf16[320,512]{1,0:T(8,128)(2,1)S(1)} %get-tuple-element.35), channel_id=1, source_target_pairs={{0,3},{1,2},{2,1},{3,0},{4,7},{5,6},{6,5},{7,4},{8,11},{9,10},{10,... | collective-permute-start | bytes 983048 | tf_op jit(solution)/shard_map/ppermute | solution.py:33
  6.2 9.9 %collective-permute-done.10.rest_1_ = bf16[576,512]{1,0:T(8,128)(2,1)S(1)} collective-permute-done((bf16[576,512]{1,0:T(8,128)(2,1)S(1)}, bf16[576,512]{1,0:T(8,128)(2,1)S(1)}, u32[]{:S(2)}, u32[]{:S(2)}) %collective-permute-start.10) | collective-permute-done | bytes 589856 | tf_op jit(solution)/shard_map/ppermute | solution.py:33
  16.0 5.0 %collective-permute-done.9.rest_0_ = bf16[320,512]{1,0:T(8,128)(2,1)S(1)} collective-permute-done((bf16[320,512]{1,0:T(8,128)(2,1)S(1)}, bf16[320,512]{1,0:T(8,128)(2,1)S(1)}, u32[]{:S(2)}, u32[]{:S(2)}) %collective-permute-start.9) | collective-permute-done | bytes 327712 | tf_op jit(solution)/shard_map/ppermute | solution.py:33
  21.0 3.6 %collective-permute-start.3 = (f32[8,512]{1,0:T(8,128)S(1)}, f32[8,512]{1,0:T(8,128)S(1)}, u32[]{:S(2)}, u32[]{:S(2)}) collective-permute-start(f32[8,512]{1,0:T(8,128)S(1)} %get-tuple-element.26.rest_0_.table), channel_id=1, source_target_pairs={{0,24},{4,28},{8,16},{12,20},{16,8},{20,12},{24,0},{28,4},{1,25},{... | collective-permute-start | bytes 49160 | tf_op jit(solution)/shard_map/ppermute | solution.py:38
  24.6 0.8 %collective-permute-start.1 = (f32[8,512]{1,0:T(8,128)S(1)}, f32[8,512]{1,0:T(8,128)S(1)}, u32[]{:S(2)}, u32[]{:S(2)}) collective-permute-start(f32[8,512]{1,0:T(8,128)S(1)} %get-tuple-element.26.rest_0_.table), channel_id=1, source_target_pairs={{0,8},{4,12},{8,0},{12,4},{16,24},{20,28},{24,16},{28,20},{1,9},{5... | collective-permute-start | bytes 49160 | tf_op jit(solution)/shard_map/ppermute | solution.py:38
  25.4 1.7 %shard_map.57.noise = f32[8,64,512]{2,1,0:T(8,128)S(1)} custom-call(s32[64,128]{1,0:T(8,128)S(1)} %get-tuple-element.23.base, f32[8,512]{1,0:T(8,128)S(1)} %get-tuple-element.26.rest_0_.table), custom_call_target="tpu_custom_call" | custom-call | flops 15728640 | bytes 1048576 | tf_op jit(solution)/shard_map/pallas_call | solution.py:459
  27.1 2.2 %collective-permute-done.2.rest_1_ = f32[8,512]{1,0:T(8,128)S(1)} collective-permute-done((f32[8,512]{1,0:T(8,128)S(1)}, f32[8,512]{1,0:T(8,128)S(1)}, u32[]{:S(2)}, u32[]{:S(2)}) %collective-permute-start.2) | collective-permute-done | bytes 16416 | tf_op jit(solution)/shard_map/ppermute | solution.py:38
  29.6 1.2 %collective-permute-done.4.other = bf16[64,512]{1,0:T(8,128)(2,1)S(1)} collective-permute-done((bf16[64,512]{1,0:T(8,128)(2,1)S(1)}, bf16[64,512]{1,0:T(8,128)(2,1)S(1)}, u32[]{:S(2)}, u32[]{:S(2)}) %collective-permute-start.4) | collective-permute-done | bytes 65568 | tf_op jit(solution)/shard_map/ppermute | solution.py:38
  30.9 1.5 %collective-permute-start.7 = (bf16[32,512]{1,0:T(8,128)(2,1)S(1)}, bf16[32,512]{1,0:T(8,128)(2,1)S(1)}, u32[]{:S(2)}, u32[]{:S(2)}) collective-permute-start(bf16[32,512]{1,0:T(8,128)(2,1)S(1)} %get-tuple-element.31.rest_0_), channel_id=1, source_target_pairs={{0,24},{4,28},{8,16},{12,20},{16,8},{20,12},{24,0},{28,4},{1,25},{... | collective-permute-start | bytes 98312 | tf_op jit(solution)/shard_map/ppermute | solution.py:38
  32.4 0.6 %collective-permute-start.6 = (bf16[32,512]{1,0:T(8,128)(2,1)S(1)}, bf16[32,512]{1,0:T(8,128)(2,1)S(1)}, u32[]{:S(2)}, u32[]{:S(2)}) collective-permute-start(bf16[32,512]{1,0:T(8,128)(2,1)S(1)} %get-tuple-element.31.rest_0_), channel_id=1, source_target_pairs={{0,16},{4,20},{8,24},{12,28},{16,0},{20,4},{24,8},{28,12},{1,17},{... | collective-permute-start | bytes 98312 | tf_op jit(solution)/shard_map/ppermute | solution.py:38
  33.1 2.3 %collective-permute-start.5 = (bf16[32,512]{1,0:T(8,128)(2,1)S(1)}, bf16[32,512]{1,0:T(8,128)(2,1)S(1)}, u32[]{:S(2)}, u32[]{:S(2)}) collective-permute-start(bf16[32,512]{1,0:T(8,128)(2,1)S(1)} %get-tuple-element.31.rest_0_), channel_id=1, source_target_pairs={{0,8},{4,12},{8,0},{12,4},{16,24},{20,28},{24,16},{28,20},{1,9},{5... | collective-permute-start | bytes 98312 | tf_op jit(solution)/shard_map/ppermute | solution.py:38
  35.4 1.7 %shard_map.60.rest_3_.rest_4_ = f32[8,64,512]{2,1,0:T(8,128)S(1)} custom-call(s32[64,128]{1,0:T(8,128)S(1)} %get-tuple-element.23.base, bf16[32,512]{1,0:T(8,128)(2,1)S(1)} %get-tuple-element.31.rest_0_), custom_call_target="tpu_custom_call" | custom-call | flops 15728640 | bytes 1048576 | tf_op jit(solution)/shard_map/pallas_call | solution.py:459
  37.0 0.4 collective-permute-done.6.rest_1_
  37.8 1.7 %shard_map.62._.rest_5_ = f32[8,64,512]{2,1,0:T(8,128)S(1)} custom-call(s32[64,128]{1,0:T(8,128)S(1)} %get-tuple-element.23.base, bf16[32,512]{1,0:T(8,128)(2,1)S(1)} %get-tuple-element.33.rest_0_), custom_call_target="tpu_custom_call" | custom-call | flops 15728640 | bytes 1048576 | tf_op jit(solution)/shard_map/pallas_call | solution.py:459
  39.5 1.5 %collective-permute-start.15 = (bf16[80,512]{1,0:T(8,128)(2,1)S(1)}, bf16[80,512]{1,0:T(8,128)(2,1)S(1)}, u32[]{:S(2)}, u32[]{:S(2)}) collective-permute-start(bf16[80,512]{1,0:T(8,128)(2,1)S(1)} %shard_map.63.message.rest_0_), channel_id=1, source_target_pairs={{0,3},{1,2},{2,1},{3,0},{4,7},{5,6},{6,5},{7,4},{8,11},{9,10},{10,... | collective-permute-start | bytes 245768 | tf_op jit(solution)/shard_map/ppermute | solution.py:38
  41.0 1.5 %collective-permute-start.14 = (bf16[80,512]{1,0:T(8,128)(2,1)S(1)}, bf16[80,512]{1,0:T(8,128)(2,1)S(1)}, u32[]{:S(2)}, u32[]{:S(2)}) collective-permute-start(bf16[80,512]{1,0:T(8,128)(2,1)S(1)} %shard_map.63.message.rest_0_), channel_id=1, source_target_pairs={{0,2},{1,3},{2,0},{3,1},{4,6},{5,7},{6,4},{7,5},{8,10},{9,11},{10,... | collective-permute-start | bytes 245768 | tf_op jit(solution)/shard_map/ppermute | solution.py:38
  42.5 0.5 %collective-permute-start.13 = (bf16[80,512]{1,0:T(8,128)(2,1)S(1)}, bf16[80,512]{1,0:T(8,128)(2,1)S(1)}, u32[]{:S(2)}, u32[]{:S(2)}) collective-permute-start(bf16[80,512]{1,0:T(8,128)(2,1)S(1)} %shard_map.63.message.rest_0_), channel_id=1, source_target_pairs={{0,1},{1,0},{2,3},{3,2},{4,5},{5,4},{6,7},{7,6},{8,9},{9,8},{10,11... | collective-permute-start | bytes 245768 | tf_op jit(solution)/shard_map/ppermute | solution.py:38
  43.1 1.7 %shard_map.65.rest_6_ = f32[8,64,512]{2,1,0:T(8,128)S(1)} custom-call(s32[64,128]{1,0:T(8,128)S(1)} %get-tuple-element.23.base, bf16[80,512]{1,0:T(8,128)(2,1)S(1)} %shard_map.63.message.rest_0_), custom_call_target="tpu_custom_call" | custom-call | flops 15728640 | bytes 1048576 | tf_op jit(solution)/shard_map/pallas_call | solution.py:459
  44.7 0.7 %shard_map.64.partial = f32[512,512]{1,0:T(8,128)S(1)} custom-call(f32[8,512]{1,0:T(8,128)S(1)} %get-tuple-element.21.coup, f32[1,512]{1,0:T(1,128)S(1)} %get-tuple-element.22.spec, bf16[2048,512]{1,0:T(8,128)(2,1)S(1)} %copy-done, f32[8,64,512]{2,1,0:T(8,128)S(1)} %shard_map.57.noise, bf16[80,512]{1,0:T(8,128)(2,1)S(1)} %shard_map.63.message.rest_0_), custom_call_target="tpu_custom_call" | custom-call | flops 268435456 | bytes 1048576 | tf_op jit(solution)/shard_map/pallas_call | solution.py:509
  45.6 1.4 %collective-permute-done.14.rest_8_ = bf16[80,512]{1,0:T(8,128)(2,1)S(1)} collective-permute-done((bf16[80,512]{1,0:T(8,128)(2,1)S(1)}, bf16[80,512]{1,0:T(8,128)(2,1)S(1)}, u32[]{:S(2)}, u32[]{:S(2)}) %collective-permute-start.14) | collective-permute-done | bytes 81952 | tf_op jit(solution)/shard_map/ppermute | solution.py:38
  47.1 2.8 %shard_map.66 = f32[512,512]{1,0:T(8,128)} custom-call(f32[512,512]{1,0:T(8,128)S(1)} %shard_map.64.partial, bf16[320,512]{1,0:T(8,128)(2,1)S(1)} %collective-permute-done.9.rest_0_, bf16[576,512]{1,0:T(8,128)(2,1)S(1)} %collective-permute-done.10.rest_1_, bf16[320,512]{1,0:T(8,128)(2,1)S(1)} %collective-permute-done.11.rest_2_, ...), custom_call_target="tpu_custom_call" | custom-call | flops 805306368 | bytes 3145728 | tf_op jit(solution)/shard_map/pallas_call | solution.py:525
  (22 shorter events, 1.3 us)
Async XLA Ops:
  0.0 1.7 %collective-permute-start = (f32[8,512]{1,0:T(8,128)}, f32[8,512]{1,0:T(8,128)S(1)}, u32[]{:S(2)}, u32[]{:S(2)}) collective-permute-start(f32[8,512]{1,0:T(8,128)} %coup.1), channel_id=1, source_target_pairs={{0,4},{4,0},{8,12},{12,8},{16,20},{20,16},{24,28},{28,24},{1,5},{5... | collective-permute-start | bytes 49160 | tf_op jit(solution)/shard_map/ppermute | solution.py:38
  2.0 14.0 %collective-permute-start.10 = (bf16[576,512]{1,0:T(8,128)(2,1)S(1)}, bf16[576,512]{1,0:T(8,128)(2,1)S(1)}, u32[]{:S(2)}, u32[]{:S(2)}) collective-permute-start(bf16[576,512]{1,0:T(8,128)(2,1)S(1)} %get-tuple-element.36), channel_id=1, source_target_pairs={{0,1},{1,0},{2,3},{3,2},{4,6},{5,7},{6,4},{7,5},{8,9},{9,8},{10,11... | collective-permute-start | bytes 1769480 | tf_op jit(solution)/shard_map/ppermute | solution.py:33
  4.7 16.4 %collective-permute-start.9 = (bf16[320,512]{1,0:T(8,128)(2,1)S(1)}, bf16[320,512]{1,0:T(8,128)(2,1)S(1)}, u32[]{:S(2)}, u32[]{:S(2)}) collective-permute-start(bf16[320,512]{1,0:T(8,128)(2,1)S(1)} %get-tuple-element.35), channel_id=1, source_target_pairs={{0,3},{1,2},{2,1},{3,0},{4,7},{5,6},{6,5},{7,4},{8,11},{9,10},{10,... | collective-permute-start | bytes 983048 | tf_op jit(solution)/shard_map/ppermute | solution.py:33
  16.0 31.0 %collective-permute-start.12 = (bf16[576,512]{1,0:T(8,128)(2,1)S(1)}, bf16[576,512]{1,0:T(8,128)(2,1)S(1)}, u32[]{:S(2)}, u32[]{:S(2)}) collective-permute-start(bf16[576,512]{1,0:T(8,128)(2,1)S(1)} %collective-permute-done.10.rest_1_), channel_id=1, source_target_pairs={{0,4},{4,0},{8,12},{12,8},{16,20},{20,16},{24,28},{28,24},{1,5},{5... | collective-permute-start | bytes 1769480 | tf_op jit(solution)/shard_map/ppermute | solution.py:38
  21.0 26.0 %collective-permute-start.11 = (bf16[320,512]{1,0:T(8,128)(2,1)S(1)}, bf16[320,512]{1,0:T(8,128)(2,1)S(1)}, u32[]{:S(2)}, u32[]{:S(2)}) collective-permute-start(bf16[320,512]{1,0:T(8,128)(2,1)S(1)} %collective-permute-done.9.rest_0_), channel_id=1, source_target_pairs={{0,4},{4,0},{8,12},{12,8},{16,20},{20,16},{24,28},{28,24},{1,5},{5... | collective-permute-start | bytes 983048 | tf_op jit(solution)/shard_map/ppermute | solution.py:38
  21.0 6.0 %collective-permute-start.3 = (f32[8,512]{1,0:T(8,128)S(1)}, f32[8,512]{1,0:T(8,128)S(1)}, u32[]{:S(2)}, u32[]{:S(2)}) collective-permute-start(f32[8,512]{1,0:T(8,128)S(1)} %get-tuple-element.26.rest_0_.table), channel_id=1, source_target_pairs={{0,24},{4,28},{8,16},{12,20},{16,8},{20,12},{24,0},{28,4},{1,25},{... | collective-permute-start | bytes 49160 | tf_op jit(solution)/shard_map/ppermute | solution.py:38
  24.6 4.6 %collective-permute-start.2 = (f32[8,512]{1,0:T(8,128)S(1)}, f32[8,512]{1,0:T(8,128)S(1)}, u32[]{:S(2)}, u32[]{:S(2)}) collective-permute-start(f32[8,512]{1,0:T(8,128)S(1)} %get-tuple-element.26.rest_0_.table), channel_id=1, source_target_pairs={{0,16},{4,20},{8,24},{12,28},{16,0},{20,4},{24,8},{28,12},{1,17},{... | collective-permute-start | bytes 49160 | tf_op jit(solution)/shard_map/ppermute | solution.py:38
  24.6 4.6 %collective-permute-start.1 = (f32[8,512]{1,0:T(8,128)S(1)}, f32[8,512]{1,0:T(8,128)S(1)}, u32[]{:S(2)}, u32[]{:S(2)}) collective-permute-start(f32[8,512]{1,0:T(8,128)S(1)} %get-tuple-element.26.rest_0_.table), channel_id=1, source_target_pairs={{0,8},{4,12},{8,0},{12,4},{16,24},{20,28},{24,16},{28,20},{1,9},{5... | collective-permute-start | bytes 49160 | tf_op jit(solution)/shard_map/ppermute | solution.py:38
  29.6 1.3 %collective-permute-start.4 = (bf16[64,512]{1,0:T(8,128)(2,1)S(1)}, bf16[64,512]{1,0:T(8,128)(2,1)S(1)}, u32[]{:S(2)}, u32[]{:S(2)}) collective-permute-start(bf16[64,512]{1,0:T(8,128)(2,1)S(1)} %get-tuple-element.29), channel_id=1, source_target_pairs={{0,4},{4,0},{8,12},{12,8},{16,20},{20,16},{24,28},{28,24},{1,5},{5... | collective-permute-start | bytes 196616 | tf_op jit(solution)/shard_map/ppermute | solution.py:38
  30.9 6.1 %collective-permute-start.7 = (bf16[32,512]{1,0:T(8,128)(2,1)S(1)}, bf16[32,512]{1,0:T(8,128)(2,1)S(1)}, u32[]{:S(2)}, u32[]{:S(2)}) collective-permute-start(bf16[32,512]{1,0:T(8,128)(2,1)S(1)} %get-tuple-element.31.rest_0_), channel_id=1, source_target_pairs={{0,24},{4,28},{8,16},{12,20},{16,8},{20,12},{24,0},{28,4},{1,25},{... | collective-permute-start | bytes 98312 | tf_op jit(solution)/shard_map/ppermute | solution.py:38
  32.4 5.0 %collective-permute-start.6 = (bf16[32,512]{1,0:T(8,128)(2,1)S(1)}, bf16[32,512]{1,0:T(8,128)(2,1)S(1)}, u32[]{:S(2)}, u32[]{:S(2)}) collective-permute-start(bf16[32,512]{1,0:T(8,128)(2,1)S(1)} %get-tuple-element.31.rest_0_), channel_id=1, source_target_pairs={{0,16},{4,20},{8,24},{12,28},{16,0},{20,4},{24,8},{28,12},{1,17},{... | collective-permute-start | bytes 98312 | tf_op jit(solution)/shard_map/ppermute | solution.py:38
  33.1 4.6 %collective-permute-start.5 = (bf16[32,512]{1,0:T(8,128)(2,1)S(1)}, bf16[32,512]{1,0:T(8,128)(2,1)S(1)}, u32[]{:S(2)}, u32[]{:S(2)}) collective-permute-start(bf16[32,512]{1,0:T(8,128)(2,1)S(1)} %get-tuple-element.31.rest_0_), channel_id=1, source_target_pairs={{0,8},{4,12},{8,0},{12,4},{16,24},{20,28},{24,16},{28,20},{1,9},{5... | collective-permute-start | bytes 98312 | tf_op jit(solution)/shard_map/ppermute | solution.py:38
  37.7 7.0 %copy-start = (bf16[2048,512]{1,0:T(8,128)(2,1)S(1)}, bf16[2048,512]{1,0:T(8,128)(2,1)}, u32[]{:S(2)}) copy-start(bf16[2048,512]{1,0:T(8,128)(2,1)} %basis.3) | copy-start | bytes 6291460
  37.7 1.7 %collective-permute-start.8 = (bf16[32,512]{1,0:T(8,128)(2,1)S(1)}, bf16[32,512]{1,0:T(8,128)(2,1)S(1)}, u32[]{:S(2)}, u32[]{:S(2)}) collective-permute-start(bf16[32,512]{1,0:T(8,128)(2,1)S(1)} %get-tuple-element.33.rest_0_), channel_id=1, source_target_pairs={{0,4},{4,0},{8,12},{12,8},{16,20},{20,16},{24,28},{28,24},{1,5},{5... | collective-permute-start | bytes 98312 | tf_op jit(solution)/shard_map/ppermute | solution.py:38
  39.5 6.1 %collective-permute-start.15 = (bf16[80,512]{1,0:T(8,128)(2,1)S(1)}, bf16[80,512]{1,0:T(8,128)(2,1)S(1)}, u32[]{:S(2)}, u32[]{:S(2)}) collective-permute-start(bf16[80,512]{1,0:T(8,128)(2,1)S(1)} %shard_map.63.message.rest_0_), channel_id=1, source_target_pairs={{0,3},{1,2},{2,1},{3,0},{4,7},{5,6},{6,5},{7,4},{8,11},{9,10},{10,... | collective-permute-start | bytes 245768 | tf_op jit(solution)/shard_map/ppermute | solution.py:38
  41.0 6.1 %collective-permute-start.14 = (bf16[80,512]{1,0:T(8,128)(2,1)S(1)}, bf16[80,512]{1,0:T(8,128)(2,1)S(1)}, u32[]{:S(2)}, u32[]{:S(2)}) collective-permute-start(bf16[80,512]{1,0:T(8,128)(2,1)S(1)} %shard_map.63.message.rest_0_), channel_id=1, source_target_pairs={{0,2},{1,3},{2,0},{3,1},{4,6},{5,7},{6,4},{7,5},{8,10},{9,11},{10,... | collective-permute-start | bytes 245768 | tf_op jit(solution)/shard_map/ppermute | solution.py:38
  42.5 4.5 %collective-permute-start.13 = (bf16[80,512]{1,0:T(8,128)(2,1)S(1)}, bf16[80,512]{1,0:T(8,128)(2,1)S(1)}, u32[]{:S(2)}, u32[]{:S(2)}) collective-permute-start(bf16[80,512]{1,0:T(8,128)(2,1)S(1)} %shard_map.63.message.rest_0_), channel_id=1, source_target_pairs={{0,1},{1,0},{2,3},{3,2},{4,5},{5,4},{6,7},{7,6},{8,9},{9,8},{10,11... | collective-permute-start | bytes 245768 | tf_op jit(solution)/shard_map/ppermute | solution.py:38

commit v3 on v2

--- a/solution.py
+++ b/solution.py
@@ -277,7 +277,7 @@
     sent[...] = carry.astype(BF16)
 
 
-def carry_kernel(tm_axis, mine, theirs, late, df, _, out):
+def carry_kernel(tm_axis, mine, theirs, late, df, out):
     half, modes = mine.shape
     core = lax.rem(lax.axis_index(tm_axis), 2)
     gain = df[pl.ds(3, 1), :]
@@ -491,17 +491,17 @@
         **fast,
     )(weights, *later, noise[-1])
     theirs = swap(sent, "tm", 1)
-    noise += noise_of(pairs, (sent,))
     carry = kernel_call(
         functools.partial(carry_kernel, "tm"),
         out_shape=bf16(vecs + 16, modes),
-        in_specs=[VMEM] * 4 + [ANY],
+        in_specs=[VMEM] * 4,
         out_specs=VMEM,
         **fast,
-    )(mine, theirs, late, sums, noise[-1])
+    )(mine, theirs, late, sums)
     carries = [swap(carry, "space", d) for d in range(1, space)]
     swapped = [swap(m, "tm", 1) for m in direct]
-    noise += noise_of([r[::-1] for r in pairs], (carry,))
+    noise += noise_of(pairs, (carry,))
+    noise += noise_of([r[::-1] for r in pairs], (noise[-1],))
 
     flops = 2 * nodes_here * modes * steps * vecs
     half_cols = steps // 2 * vecs

time: 50 us -> 49.5 us (0.990)
  transfers between devices with their start and end apart: 16 -> 16, of which waited for: 8 -> 7; matrix products, arithmetic and copies ran while one was open for 0% -> 0% of each run, Pallas kernels for 18% -> 18%
where the time goes in v3:
time: 49.5 us; the launch traced here: 49.4 us
  waiting for transfers between devices  20.2 us (41%)
  starting transfers between devices  17.2 us (35%)
  Pallas kernels  11.9 us (24%)
    ppermute x2, waiting for transfers between devices, exchange(): return lax.ppermute(x, ('tm', 'space'), moves)  14.9 us
    ppermute x14, starting transfers between devices, swap(): return lax.ppermute(x, axis, [(i, i ^ offset) for i in range(count)])  13 us
    pallas_call x4, Pallas kernels, noise_of(): kernel_call(functools.partial(noise_kernel, 'tm', 'space', offsets, len(a...  6.62 us
    ppermute x14, waiting for transfers between devices, swap(): return lax.ppermute(x, axis, [(i, i ^ offset) for i in range(count)])  5.28 us
    ppermute x2, starting transfers between devices, exchange(): return lax.ppermute(x, ('tm', 'space'), moves)  4.16 us
    pallas_call x1, Pallas kernels, local(): kernel_call(functools.partial(final_kernel, 'tm', pairs, single), out_sha...  2.75 us
    pallas_call x1, Pallas kernels, local(): kernel_call(functools.partial(pack_kernel, 'tm', 'space', routes), out_sh...  1.24 us
  transfers between devices with their start and end apart: 16, of which 7 were waited for; matrix products, arithmetic and copies ran while one was open for 0% of the time, Pallas kernels for 18%

profile of v3, /device:TPU:0, one launch (start us, length us, event | category | flops | bytes accessed | tf_op | source)
XLA Modules:
  0.0 49.4 jit_solution(5361632310446961320)
XLA Ops:
  0.0 0.5 collective-permute-start
  0.5 1.2 %shard_map.55 = (bf16[320,512]{1,0:T(8,128)(2,1)S(1)}, bf16[576,512]{1,0:T(8,128)(2,1)S(1)}, f32[8,512]{1,0:T(8,128)S(1)}, f32[1,512]{1,0:T(1,128)S(1)}, s32[64,128]{1,0:T(8,128)S(1)}) custom-call(f32[8,512]{1,0:T(8,128)} %coup.1, f32[1,512]{1,0:T(1,128)} %bitcast.3, bf16[2048,512]{1,0:T(8,128)(2,1)} %basis.3, s32[1,64]{1,0:T(1,128)} %bitcast.4, s32[1,64]{1,0:T(1,128)} %bitcast.5), custom_call_target="tpu_custom_call" | custom-call | tf_op jit(solution)/shard_map/pallas_call | solution.py:436
  2.0 2.7 %collective-permute-start.10 = (bf16[576,512]{1,0:T(8,128)(2,1)S(1)}, bf16[576,512]{1,0:T(8,128)(2,1)S(1)}, u32[]{:S(2)}, u32[]{:S(2)}) collective-permute-start(bf16[576,512]{1,0:T(8,128)(2,1)S(1)} %get-tuple-element.36), channel_id=1, source_target_pairs={{0,1},{1,0},{2,3},{3,2},{4,6},{5,7},{6,4},{7,5},{8,9},{9,8},{10,11... | collective-permute-start | bytes 1769480 | tf_op jit(solution)/shard_map/ppermute | solution.py:33
  4.7 1.5 %collective-permute-start.9 = (bf16[320,512]{1,0:T(8,128)(2,1)S(1)}, bf16[320,512]{1,0:T(8,128)(2,1)S(1)}, u32[]{:S(2)}, u32[]{:S(2)}) collective-permute-start(bf16[320,512]{1,0:T(8,128)(2,1)S(1)} %get-tuple-element.35), channel_id=1, source_target_pairs={{0,3},{1,2},{2,1},{3,0},{4,7},{5,6},{6,5},{7,4},{8,11},{9,10},{10,... | collective-permute-start | bytes 983048 | tf_op jit(solution)/shard_map/ppermute | solution.py:33
  6.2 9.9 %collective-permute-done.10.rest_1_ = bf16[576,512]{1,0:T(8,128)(2,1)S(1)} collective-permute-done((bf16[576,512]{1,0:T(8,128)(2,1)S(1)}, bf16[576,512]{1,0:T(8,128)(2,1)S(1)}, u32[]{:S(2)}, u32[]{:S(2)}) %collective-permute-start.10) | collective-permute-done | bytes 589856 | tf_op jit(solution)/shard_map/ppermute | solution.py:33
  16.0 5.0 %collective-permute-done.9.rest_0_ = bf16[320,512]{1,0:T(8,128)(2,1)S(1)} collective-permute-done((bf16[320,512]{1,0:T(8,128)(2,1)S(1)}, bf16[320,512]{1,0:T(8,128)(2,1)S(1)}, u32[]{:S(2)}, u32[]{:S(2)}) %collective-permute-start.9) | collective-permute-done | bytes 327712 | tf_op jit(solution)/shard_map/ppermute | solution.py:33
  21.0 3.6 %collective-permute-start.3 = (f32[8,512]{1,0:T(8,128)S(1)}, f32[8,512]{1,0:T(8,128)S(1)}, u32[]{:S(2)}, u32[]{:S(2)}) collective-permute-start(f32[8,512]{1,0:T(8,128)S(1)} %get-tuple-element.26.rest_0_.table), channel_id=1, source_target_pairs={{0,24},{4,28},{8,16},{12,20},{16,8},{20,12},{24,0},{28,4},{1,25},{... | collective-permute-start | bytes 49160 | tf_op jit(solution)/shard_map/ppermute | solution.py:38
  24.6 0.8 %collective-permute-start.1 = (f32[8,512]{1,0:T(8,128)S(1)}, f32[8,512]{1,0:T(8,128)S(1)}, u32[]{:S(2)}, u32[]{:S(2)}) collective-permute-start(f32[8,512]{1,0:T(8,128)S(1)} %get-tuple-element.26.rest_0_.table), channel_id=1, source_target_pairs={{0,8},{4,12},{8,0},{12,4},{16,24},{20,28},{24,16},{28,20},{1,9},{5... | collective-permute-start | bytes 49160 | tf_op jit(solution)/shard_map/ppermute | solution.py:38
  25.4 1.7 %shard_map.57.noise = f32[8,64,512]{2,1,0:T(8,128)S(1)} custom-call(s32[64,128]{1,0:T(8,128)S(1)} %get-tuple-element.23.base, f32[8,512]{1,0:T(8,128)S(1)} %get-tuple-element.26.rest_0_.table), custom_call_target="tpu_custom_call" | custom-call | flops 15728640 | bytes 1048576 | tf_op jit(solution)/shard_map/pallas_call | solution.py:459
  27.1 2.2 %collective-permute-done.2.rest_1_ = f32[8,512]{1,0:T(8,128)S(1)} collective-permute-done((f32[8,512]{1,0:T(8,128)S(1)}, f32[8,512]{1,0:T(8,128)S(1)}, u32[]{:S(2)}, u32[]{:S(2)}) %collective-permute-start.2) | collective-permute-done | bytes 16416 | tf_op jit(solution)/shard_map/ppermute | solution.py:38
  29.6 1.2 %collective-permute-done.4.other = bf16[64,512]{1,0:T(8,128)(2,1)S(1)} collective-permute-done((bf16[64,512]{1,0:T(8,128)(2,1)S(1)}, bf16[64,512]{1,0:T(8,128)(2,1)S(1)}, u32[]{:S(2)}, u32[]{:S(2)}) %collective-permute-start.4) | collective-permute-done | bytes 65568 | tf_op jit(solution)/shard_map/ppermute | solution.py:38
  30.9 1.5 %collective-permute-start.7 = (bf16[32,512]{1,0:T(8,128)(2,1)S(1)}, bf16[32,512]{1,0:T(8,128)(2,1)S(1)}, u32[]{:S(2)}, u32[]{:S(2)}) collective-permute-start(bf16[32,512]{1,0:T(8,128)(2,1)S(1)} %get-tuple-element.31.rest_0_), channel_id=1, source_target_pairs={{0,24},{4,28},{8,16},{12,20},{16,8},{20,12},{24,0},{28,4},{1,25},{... | collective-permute-start | bytes 98312 | tf_op jit(solution)/shard_map/ppermute | solution.py:38
  32.4 0.6 %collective-permute-start.6 = (bf16[32,512]{1,0:T(8,128)(2,1)S(1)}, bf16[32,512]{1,0:T(8,128)(2,1)S(1)}, u32[]{:S(2)}, u32[]{:S(2)}) collective-permute-start(bf16[32,512]{1,0:T(8,128)(2,1)S(1)} %get-tuple-element.31.rest_0_), channel_id=1, source_target_pairs={{0,16},{4,20},{8,24},{12,28},{16,0},{20,4},{24,8},{28,12},{1,17},{... | collective-permute-start | bytes 98312 | tf_op jit(solution)/shard_map/ppermute | solution.py:38
  33.1 2.3 %collective-permute-start.5 = (bf16[32,512]{1,0:T(8,128)(2,1)S(1)}, bf16[32,512]{1,0:T(8,128)(2,1)S(1)}, u32[]{:S(2)}, u32[]{:S(2)}) collective-permute-start(bf16[32,512]{1,0:T(8,128)(2,1)S(1)} %get-tuple-element.31.rest_0_), channel_id=1, source_target_pairs={{0,8},{4,12},{8,0},{12,4},{16,24},{20,28},{24,16},{28,20},{1,9},{5... | collective-permute-start | bytes 98312 | tf_op jit(solution)/shard_map/ppermute | solution.py:38
  35.4 1.7 %shard_map.60.rest_3_.rest_4_ = f32[8,64,512]{2,1,0:T(8,128)S(1)} custom-call(s32[64,128]{1,0:T(8,128)S(1)} %get-tuple-element.23.base, bf16[32,512]{1,0:T(8,128)(2,1)S(1)} %get-tuple-element.31.rest_0_), custom_call_target="tpu_custom_call" | custom-call | flops 15728640 | bytes 1048576 | tf_op jit(solution)/shard_map/pallas_call | solution.py:459
  37.0 0.4 collective-permute-done.6.rest_1_
  37.8 1.2 %collective-permute-done.8.theirs = bf16[32,512]{1,0:T(8,128)(2,1)S(1)} collective-permute-done((bf16[32,512]{1,0:T(8,128)(2,1)S(1)}, bf16[32,512]{1,0:T(8,128)(2,1)S(1)}, u32[]{:S(2)}, u32[]{:S(2)}) %collective-permute-start.8) | collective-permute-done | bytes 32800 | tf_op jit(solution)/shard_map/ppermute | solution.py:38
  39.0 1.5 %collective-permute-start.15 = (bf16[80,512]{1,0:T(8,128)(2,1)S(1)}, bf16[80,512]{1,0:T(8,128)(2,1)S(1)}, u32[]{:S(2)}, u32[]{:S(2)}) collective-permute-start(bf16[80,512]{1,0:T(8,128)(2,1)S(1)} %shard_map.62.message.rest_0_), channel_id=1, source_target_pairs={{0,3},{1,2},{2,1},{3,0},{4,7},{5,6},{6,5},{7,4},{8,11},{9,10},{10,... | collective-permute-start | bytes 245768 | tf_op jit(solution)/shard_map/ppermute | solution.py:38
  40.5 1.5 %collective-permute-start.14 = (bf16[80,512]{1,0:T(8,128)(2,1)S(1)}, bf16[80,512]{1,0:T(8,128)(2,1)S(1)}, u32[]{:S(2)}, u32[]{:S(2)}) collective-permute-start(bf16[80,512]{1,0:T(8,128)(2,1)S(1)} %shard_map.62.message.rest_0_), channel_id=1, source_target_pairs={{0,2},{1,3},{2,0},{3,1},{4,6},{5,7},{6,4},{7,5},{8,10},{9,11},{10,... | collective-permute-start | bytes 245768 | tf_op jit(solution)/shard_map/ppermute | solution.py:38
  42.0 0.5 %collective-permute-start.13 = (bf16[80,512]{1,0:T(8,128)(2,1)S(1)}, bf16[80,512]{1,0:T(8,128)(2,1)S(1)}, u32[]{:S(2)}, u32[]{:S(2)}) collective-permute-start(bf16[80,512]{1,0:T(8,128)(2,1)S(1)} %shard_map.62.message.rest_0_), channel_id=1, source_target_pairs={{0,1},{1,0},{2,3},{3,2},{4,5},{5,4},{6,7},{7,6},{8,9},{9,8},{10,11... | collective-permute-start | bytes 245768 | tf_op jit(solution)/shard_map/ppermute | solution.py:38
  42.6 1.7 %shard_map.64.rest_0_.rest_5_ = f32[8,64,512]{2,1,0:T(8,128)S(1)} custom-call(s32[64,128]{1,0:T(8,128)S(1)} %get-tuple-element.23.base, bf16[80,512]{1,0:T(8,128)(2,1)S(1)} %shard_map.62.message.rest_0_), custom_call_target="tpu_custom_call" | custom-call | flops 15728640 | bytes 1048576 | tf_op jit(solution)/shard_map/pallas_call | solution.py:459
  44.2 1.7 %shard_map.65.rest_6_ = f32[8,64,512]{2,1,0:T(8,128)S(1)} custom-call(s32[64,128]{1,0:T(8,128)S(1)} %get-tuple-element.23.base, f32[8,64,512]{2,1,0:T(8,128)S(1)} %shard_map.64.rest_0_.rest_5_), custom_call_target="tpu_custom_call" | custom-call | flops 15728640 | bytes 1048576 | tf_op jit(solution)/shard_map/pallas_call | solution.py:459
  45.9 0.7 %shard_map.63.partial = f32[512,512]{1,0:T(8,128)S(1)} custom-call(f32[8,512]{1,0:T(8,128)S(1)} %get-tuple-element.21.coup, f32[1,512]{1,0:T(1,128)S(1)} %get-tuple-element.22.spec, bf16[2048,512]{1,0:T(8,128)(2,1)S(1)} %copy-done, f32[8,64,512]{2,1,0:T(8,128)S(1)} %shard_map.57.noise, bf16[80,512]{1,0:T(8,128)(2,1)S(1)} %shard_map.62.message.rest_0_), custom_call_target="tpu_custom_call" | custom-call | flops 268435456 | bytes 1048576 | tf_op jit(solution)/shard_map/pallas_call | solution.py:509
  46.6 2.8 %shard_map.66 = f32[512,512]{1,0:T(8,128)} custom-call(f32[512,512]{1,0:T(8,128)S(1)} %shard_map.63.partial, bf16[320,512]{1,0:T(8,128)(2,1)S(1)} %collective-permute-done.9.rest_0_, bf16[576,512]{1,0:T(8,128)(2,1)S(1)} %collective-permute-done.10.rest_1_, bf16[320,512]{1,0:T(8,128)(2,1)S(1)} %collective-permute-done.11.rest_2_, ...), custom_call_target="tpu_custom_call" | custom-call | flops 805306368 | bytes 3145728 | tf_op jit(solution)/shard_map/pallas_call | solution.py:525
  (22 shorter events, 1.1 us)
Async XLA Ops:
  0.0 1.7 %collective-permute-start = (f32[8,512]{1,0:T(8,128)}, f32[8,512]{1,0:T(8,128)S(1)}, u32[]{:S(2)}, u32[]{:S(2)}) collective-permute-start(f32[8,512]{1,0:T(8,128)} %coup.1), channel_id=1, source_target_pairs={{0,4},{4,0},{8,12},{12,8},{16,20},{20,16},{24,28},{28,24},{1,5},{5... | collective-permute-start | bytes 49160 | tf_op jit(solution)/shard_map/ppermute | solution.py:38
  2.0 14.0 %collective-permute-start.10 = (bf16[576,512]{1,0:T(8,128)(2,1)S(1)}, bf16[576,512]{1,0:T(8,128)(2,1)S(1)}, u32[]{:S(2)}, u32[]{:S(2)}) collective-permute-start(bf16[576,512]{1,0:T(8,128)(2,1)S(1)} %get-tuple-element.36), channel_id=1, source_target_pairs={{0,1},{1,0},{2,3},{3,2},{4,6},{5,7},{6,4},{7,5},{8,9},{9,8},{10,11... | collective-permute-start | bytes 1769480 | tf_op jit(solution)/shard_map/ppermute | solution.py:33
  4.7 16.4 %collective-permute-start.9 = (bf16[320,512]{1,0:T(8,128)(2,1)S(1)}, bf16[320,512]{1,0:T(8,128)(2,1)S(1)}, u32[]{:S(2)}, u32[]{:S(2)}) collective-permute-start(bf16[320,512]{1,0:T(8,128)(2,1)S(1)} %get-tuple-element.35), channel_id=1, source_target_pairs={{0,3},{1,2},{2,1},{3,0},{4,7},{5,6},{6,5},{7,4},{8,11},{9,10},{10,... | collective-permute-start | bytes 983048 | tf_op jit(solution)/shard_map/ppermute | solution.py:33
  16.0 30.6 %collective-permute-start.12 = (bf16[576,512]{1,0:T(8,128)(2,1)S(1)}, bf16[576,512]{1,0:T(8,128)(2,1)S(1)}, u32[]{:S(2)}, u32[]{:S(2)}) collective-permute-start(bf16[576,512]{1,0:T(8,128)(2,1)S(1)} %collective-permute-done.10.rest_1_), channel_id=1, source_target_pairs={{0,4},{4,0},{8,12},{12,8},{16,20},{20,16},{24,28},{28,24},{1,5},{5... | collective-permute-start | bytes 1769480 | tf_op jit(solution)/shard_map/ppermute | solution.py:38
  21.0 25.6 %collective-permute-start.11 = (bf16[320,512]{1,0:T(8,128)(2,1)S(1)}, bf16[320,512]{1,0:T(8,128)(2,1)S(1)}, u32[]{:S(2)}, u32[]{:S(2)}) collective-permute-start(bf16[320,512]{1,0:T(8,128)(2,1)S(1)} %collective-permute-done.9.rest_0_), channel_id=1, source_target_pairs={{0,4},{4,0},{8,12},{12,8},{16,20},{20,16},{24,28},{28,24},{1,5},{5... | collective-permute-start | bytes 983048 | tf_op jit(solution)/shard_map/ppermute | solution.py:38
  21.0 6.0 %collective-permute-start.3 = (f32[8,512]{1,0:T(8,128)S(1)}, f32[8,512]{1,0:T(8,128)S(1)}, u32[]{:S(2)}, u32[]{:S(2)}) collective-permute-start(f32[8,512]{1,0:T(8,128)S(1)} %get-tuple-element.26.rest_0_.table), channel_id=1, source_target_pairs={{0,24},{4,28},{8,16},{12,20},{16,8},{20,12},{24,0},{28,4},{1,25},{... | collective-permute-start | bytes 49160 | tf_op jit(solution)/shard_map/ppermute | solution.py:38
  24.6 4.6 %collective-permute-start.2 = (f32[8,512]{1,0:T(8,128)S(1)}, f32[8,512]{1,0:T(8,128)S(1)}, u32[]{:S(2)}, u32[]{:S(2)}) collective-permute-start(f32[8,512]{1,0:T(8,128)S(1)} %get-tuple-element.26.rest_0_.table), channel_id=1, source_target_pairs={{0,16},{4,20},{8,24},{12,28},{16,0},{20,4},{24,8},{28,12},{1,17},{... | collective-permute-start | bytes 49160 | tf_op jit(solution)/shard_map/ppermute | solution.py:38
  24.6 4.6 %collective-permute-start.1 = (f32[8,512]{1,0:T(8,128)S(1)}, f32[8,512]{1,0:T(8,128)S(1)}, u32[]{:S(2)}, u32[]{:S(2)}) collective-permute-start(f32[8,512]{1,0:T(8,128)S(1)} %get-tuple-element.26.rest_0_.table), channel_id=1, source_target_pairs={{0,8},{4,12},{8,0},{12,4},{16,24},{20,28},{24,16},{28,20},{1,9},{5... | collective-permute-start | bytes 49160 | tf_op jit(solution)/shard_map/ppermute | solution.py:38
  29.6 1.3 %collective-permute-start.4 = (bf16[64,512]{1,0:T(8,128)(2,1)S(1)}, bf16[64,512]{1,0:T(8,128)(2,1)S(1)}, u32[]{:S(2)}, u32[]{:S(2)}) collective-permute-start(bf16[64,512]{1,0:T(8,128)(2,1)S(1)} %get-tuple-element.29), channel_id=1, source_target_pairs={{0,4},{4,0},{8,12},{12,8},{16,20},{20,16},{24,28},{28,24},{1,5},{5... | collective-permute-start | bytes 196616 | tf_op jit(solution)/shard_map/ppermute | solution.py:38
  30.9 6.1 %collective-permute-start.7 = (bf16[32,512]{1,0:T(8,128)(2,1)S(1)}, bf16[32,512]{1,0:T(8,128)(2,1)S(1)}, u32[]{:S(2)}, u32[]{:S(2)}) collective-permute-start(bf16[32,512]{1,0:T(8,128)(2,1)S(1)} %get-tuple-element.31.rest_0_), channel_id=1, source_target_pairs={{0,24},{4,28},{8,16},{12,20},{16,8},{20,12},{24,0},{28,4},{1,25},{... | collective-permute-start | bytes 98312 | tf_op jit(solution)/shard_map/ppermute | solution.py:38
  32.4 5.0 %collective-permute-start.6 = (bf16[32,512]{1,0:T(8,128)(2,1)S(1)}, bf16[32,512]{1,0:T(8,128)(2,1)S(1)}, u32[]{:S(2)}, u32[]{:S(2)}) collective-permute-start(bf16[32,512]{1,0:T(8,128)(2,1)S(1)} %get-tuple-element.31.rest_0_), channel_id=1, source_target_pairs={{0,16},{4,20},{8,24},{12,28},{16,0},{20,4},{24,8},{28,12},{1,17},{... | collective-permute-start | bytes 98312 | tf_op jit(solution)/shard_map/ppermute | solution.py:38
  33.1 4.6 %collective-permute-start.5 = (bf16[32,512]{1,0:T(8,128)(2,1)S(1)}, bf16[32,512]{1,0:T(8,128)(2,1)S(1)}, u32[]{:S(2)}, u32[]{:S(2)}) collective-permute-start(bf16[32,512]{1,0:T(8,128)(2,1)S(1)} %get-tuple-element.31.rest_0_), channel_id=1, source_target_pairs={{0,8},{4,12},{8,0},{12,4},{16,24},{20,28},{24,16},{28,20},{1,9},{5... | collective-permute-start | bytes 98312 | tf_op jit(solution)/shard_map/ppermute | solution.py:38
  37.7 8.2 %copy-start = (bf16[2048,512]{1,0:T(8,128)(2,1)S(1)}, bf16[2048,512]{1,0:T(8,128)(2,1)}, u32[]{:S(2)}) copy-start(bf16[2048,512]{1,0:T(8,128)(2,1)} %basis.3) | copy-start | bytes 6291460
  37.7 1.3 %collective-permute-start.8 = (bf16[32,512]{1,0:T(8,128)(2,1)S(1)}, bf16[32,512]{1,0:T(8,128)(2,1)S(1)}, u32[]{:S(2)}, u32[]{:S(2)}) collective-permute-start(bf16[32,512]{1,0:T(8,128)(2,1)S(1)} %get-tuple-element.33), channel_id=1, source_target_pairs={{0,4},{4,0},{8,12},{12,8},{16,20},{20,16},{24,28},{28,24},{1,5},{5... | collective-permute-start | bytes 98312 | tf_op jit(solution)/shard_map/ppermute | solution.py:38
  39.0 7.6 %collective-permute-start.15 = (bf16[80,512]{1,0:T(8,128)(2,1)S(1)}, bf16[80,512]{1,0:T(8,128)(2,1)S(1)}, u32[]{:S(2)}, u32[]{:S(2)}) collective-permute-start(bf16[80,512]{1,0:T(8,128)(2,1)S(1)} %shard_map.62.message.rest_0_), channel_id=1, source_target_pairs={{0,3},{1,2},{2,1},{3,0},{4,7},{5,6},{6,5},{7,4},{8,11},{9,10},{10,... | collective-permute-start | bytes 245768 | tf_op jit(solution)/shard_map/ppermute | solution.py:38
  40.5 6.1 %collective-permute-start.14 = (bf16[80,512]{1,0:T(8,128)(2,1)S(1)}, bf16[80,512]{1,0:T(8,128)(2,1)S(1)}, u32[]{:S(2)}, u32[]{:S(2)}) collective-permute-start(bf16[80,512]{1,0:T(8,128)(2,1)S(1)} %shard_map.62.message.rest_0_), channel_id=1, source_target_pairs={{0,2},{1,3},{2,0},{3,1},{4,6},{5,7},{6,4},{7,5},{8,10},{9,11},{10,... | collective-permute-start | bytes 245768 | tf_op jit(solution)/shard_map/ppermute | solution.py:38
  42.0 4.6 %collective-permute-start.13 = (bf16[80,512]{1,0:T(8,128)(2,1)S(1)}, bf16[80,512]{1,0:T(8,128)(2,1)S(1)}, u32[]{:S(2)}, u32[]{:S(2)}) collective-permute-start(bf16[80,512]{1,0:T(8,128)(2,1)S(1)} %shard_map.62.message.rest_0_), channel_id=1, source_target_pairs={{0,1},{1,0},{2,3},{3,2},{4,5},{5,4},{6,7},{7,6},{8,9},{9,8},{10,11... | collective-permute-start | bytes 245768 | tf_op jit(solution)/shard_map/ppermute | solution.py:38

commit v4 on v2

--- a/solution.py
+++ b/solution.py
@@ -166,15 +166,15 @@
     base[...] = jnp.broadcast_to(start, base.shape)
 
 
-def noise_kernel(tm_axis, sp_axis, offsets, extras, base, *rest):
+def noise_kernel(tm_axis, sp_axis, parts, total_steps, extras, base, *rest):
     outs = rest[extras:]
-    steps, vecs, modes = outs[0].shape
     me, sp = lax.axis_index(tm_axis), lax.axis_index(sp_axis)
     group = 8
-    for out, offset in zip(outs, offsets):
+    for out, (offset, begin) in zip(outs, parts):
+        steps, vecs, modes = out.shape
         ids = (sp ^ pick(lax.rem(me, 2), offset)) * modes + lax.broadcasted_iota(jnp.int32, (1, modes), 1)
         lane = ids * jnp.int32(-1640531535)
-        first_step = me * steps
+        first_step = me * total_steps + begin
 
         def step(t, _):
             shifted = lane + (first_step + t) * jnp.int32(374761393)
@@ -257,7 +257,7 @@
     lax.fori_loop(0, vecs // 16, tile, 0)
 
 
-def combine_kernel(tm_axis, own, other, df, out, late):
+def combine_kernel(tm_axis, own, other, df, _, out, late):
     core = lax.rem(lax.axis_index(tm_axis), 2)
     first = core == 0
     half = out.shape[0]
@@ -301,15 +301,14 @@
     coefs[1] = ratio * jnp.where(row == steps - 1, 1.0, pltpu.roll(c, steps - 1, 0))
 
 
-def values(noise, start, coefs, state, rhs, times, part=(0, 1)):
-    vecs = noise.shape[1]
-    share = vecs // part[1]
-    for v in range(part[0] * share, (part[0] + 1) * share, 16):
+def values(noise, start, coefs, state, rhs, times):
+    span, vecs, _ = noise[0].shape
+    for v in range(0, vecs, 16):
         at = pl.ds(v, 16)
         value = start(at)
         for n, t in enumerate(times):
             row = pl.ds(t, 1)
-            value = coefs[0, row, :] * noise[t, at, :] + coefs[1, row, :] * value
+            value = coefs[0, row, :] * noise[t // span][t % span, at, :] + coefs[1, row, :] * value
             rhs[pl.ds((len(times) - 1 - n) * vecs + v, 16), :] = value.astype(BF16)
         if times[-1]:
             state[at, :] = value
@@ -333,9 +332,9 @@
     set_coefs(coefs, coup[...], spec[...], sums_of(message[pl.ds(vecs, 16), :].astype(F32)))
     late, early = halves_of(steps)
     width = vecs * len(late)
-    values(noise, lambda at: message[at, :].astype(F32), coefs, state, rhs.at[0], late)
+    values((noise,), lambda at: message[at, :].astype(F32), coefs, state, rhs.at[0], late)
     copy.wait()
-    values(noise, lambda at: state[at, :], coefs, state, rhs.at[1], early)
+    values((noise,), lambda at: state[at, :], coefs, state, rhs.at[1], early)
     out[:, pl.ds(width, width)] = product(lhs[...], rhs[0])
     out[:, pl.ds(0, width)] = product(lhs[...], rhs[1])
 
@@ -345,10 +344,10 @@
     count = 2 * len(pairs) + len(single)
     direct, rest = rest[:fetched], rest[fetched:]
     swapped, rest = rest[:fetched], rest[fetched:]
-    noise, rest = rest[:count], rest[count:]
+    noise, rest = [rest[2 * n : 2 * n + 2] for n in range(count)], rest[2 * count :]
     messages, rest = rest[:count], rest[count:]
     out, lhs, rhs, state, coefs, result, sems = rest
-    steps, vecs, _ = noise[0].shape
+    steps, vecs = 2 * noise[0][0].shape[0], noise[0][0].shape[1]
     core = lax.rem(lax.axis_index(tm_axis), 2)
     first = core == 0
     copies = []
@@ -454,18 +453,21 @@
     tables = [swap(table, "tm", 2 * e) for e in range(1, chips)]
     direct = [exchange(m, lambda t, s, r=r: (t, s ^ r[t % 2])) for m, r in zip(messages, routes)]
 
-    def noise_of(offsets, after):
-        count = len(offsets) * steps * vecs * modes
+    def noise_of(parts, span, after):
+        count = len(parts) * span * vecs * modes
         return kernel_call(
-            functools.partial(noise_kernel, "tm", "space", offsets, len(after)),
-            out_shape=[f32(steps, vecs, modes)] * len(offsets),
+            functools.partial(noise_kernel, "tm", "space", parts, steps, len(after)),
+            out_shape=[f32(span, vecs, modes)] * len(parts),
             in_specs=[VMEM] + [ANY] * len(after),
-            out_specs=[VMEM] * len(offsets),
+            out_specs=[VMEM] * len(parts),
             cost_estimate=pl.CostEstimate(flops=count * 60, transcendentals=count * 2, bytes_accessed=count * 4),
             **fast,
         )(base, *after)
 
-    (own,) = noise_of([(0, 0)], (table,))
+    span = steps // 2
+    alone = [(d, d) for d in single]
+    half_of = lambda routes, part, after: noise_of([(r, part * span) for r in routes], span, after)
+    (own,) = noise_of([((0, 0), 0)], steps, (table,))
     state, sent, weights, sums = kernel_call(
         functools.partial(offset_kernel, "tm"),
         out_shape=[f32(vecs, modes), bf16(vecs, modes), f32(chips, 8, modes), f32(8, modes)],
@@ -474,34 +476,39 @@
         scratch_shapes=[pltpu.VMEM((chips, 8, modes), F32)] + [pltpu.VMEM((steps, modes), F32)] * 2,
         **fast,
     )(own, coup, spec, table, *tables)
+    alone_0 = half_of(alone, 0, (sent,))
     total, late = kernel_call(
         functools.partial(combine_kernel, "tm"),
         out_shape=[bf16(vecs // 2, modes), f32(vecs, modes)],
-        in_specs=[VMEM] * 3,
+        in_specs=[VMEM] * 3 + [ANY],
         out_specs=[VMEM] * 2,
         **fast,
-    )(state, swap(sent, "tm", 1), sums)
+    )(state, swap(sent, "tm", 1), sums, alone_0[0])
     later = [swap(total, "tm", 2 * e) for e in range(1, chips)]
-    noise = list(noise_of([(d, d) for d in single], (total,)))
+    alone_1 = half_of(alone, 1, (total,))
     mine, sent = kernel_call(
         functools.partial(half_kernel, "tm"),
         out_shape=[f32(vecs // 2, modes), bf16(vecs // 2, modes)],
         in_specs=[VMEM] * (1 + len(later)) + [ANY],
         out_specs=[VMEM] * 2,
         **fast,
-    )(weights, *later, noise[-1])
+    )(weights, *later, alone_1[0])
     theirs = swap(sent, "tm", 1)
-    noise += noise_of(pairs, (sent,))
+    near_0 = half_of(pairs, 0, (sent,)) if pairs else [sent]
     carry = kernel_call(
         functools.partial(carry_kernel, "tm"),
         out_shape=bf16(vecs + 16, modes),
         in_specs=[VMEM] * 4 + [ANY],
         out_specs=VMEM,
         **fast,
-    )(mine, theirs, late, sums, noise[-1])
+    )(mine, theirs, late, sums, near_0[0])
     carries = [swap(carry, "space", d) for d in range(1, space)]
     swapped = [swap(m, "tm", 1) for m in direct]
-    noise += noise_of([r[::-1] for r in pairs], (carry,))
+    noise = [x for both in zip(alone_0, alone_1) for x in both]
+    if pairs:
+        near_1 = half_of(pairs, 1, (carry,))
+        far = noise_of([(r[::-1], n * span) for r in pairs for n in range(2)], span, (near_1[-1],))
+        noise += [x for both in zip(near_0, near_1) for x in both] + list(far)
 
     flops = 2 * nodes_here * modes * steps * vecs
     half_cols = steps // 2 * vecs

time: 50 us -> 49.4 us (0.988)
  waiting for transfers between devices: 20.6 us -> 20 us
    ppermute x14, waiting for transfers between devices: 5.74 us -> 5.13 us  [swap(): return lax.ppermute(x, axis, [(i, i ^ offset) for i in range(count)])]
    pallas_call x4 -> x6, Pallas kernels: 6.62 us -> 6.66 us  [noise_of(): kernel_call(functools.partial(noise_kernel, 'tm', 'space', parts, steps,...]
  transfers between devices with their start and end apart: 16 -> 16, of which waited for: 8 -> 10; matrix products, arithmetic and copies ran while one was open for 0% -> 0% of each run, Pallas kernels for 18% -> 18%
where the time goes in v4:
time: 49.4 us; the launch traced here: 49.3 us
  waiting for transfers between devices  20 us (40%)
  starting transfers between devices  17.2 us (35%)
  Pallas kernels  11.9 us (24%)
    ppermute x2, waiting for transfers between devices, exchange(): return lax.ppermute(x, ('tm', 'space'), moves)  14.9 us
    ppermute x14, starting transfers between devices, swap(): return lax.ppermute(x, axis, [(i, i ^ offset) for i in range(count)])  13 us
    pallas_call x6, Pallas kernels, noise_of(): kernel_call(functools.partial(noise_kernel, 'tm', 'space', parts, steps,...  6.66 us
    ppermute x14, waiting for transfers between devices, swap(): return lax.ppermute(x, axis, [(i, i ^ offset) for i in range(count)])  5.13 us
    ppermute x2, starting transfers between devices, exchange(): return lax.ppermute(x, ('tm', 'space'), moves)  4.16 us
    pallas_call x1, Pallas kernels, local(): kernel_call(functools.partial(final_kernel, 'tm', pairs, single), out_sha...  2.77 us
    pallas_call x1, Pallas kernels, local(): kernel_call(functools.partial(pack_kernel, 'tm', 'space', routes), out_sh...  1.24 us
  transfers between devices with their start and end apart: 16, of which 10 were waited for; matrix products, arithmetic and copies ran while one was open for 0% of the time, Pallas kernels for 18%

profile of v4, /device:TPU:0, one launch (start us, length us, event | category | flops | bytes accessed | tf_op | source)
XLA Modules:
  0.0 49.3 jit_solution(10302081738492258008)
XLA Ops:
  0.0 0.5 %collective-permute-start = (f32[8,512]{1,0:T(8,128)}, f32[8,512]{1,0:T(8,128)S(1)}, u32[]{:S(2)}, u32[]{:S(2)}) collective-permute-start(f32[8,512]{1,0:T(8,128)} %coup.1), channel_id=1, source_target_pairs={{0,4},{4,0},{8,12},{12,8},{16,20},{20,16},{24,28},{28,24},{1,5},{5... | collective-permute-start | bytes 49160 | tf_op jit(solution)/shard_map/ppermute | solution.py:38
  0.5 1.2 %shard_map.55 = (bf16[320,512]{1,0:T(8,128)(2,1)S(1)}, bf16[576,512]{1,0:T(8,128)(2,1)S(1)}, f32[8,512]{1,0:T(8,128)S(1)}, f32[1,512]{1,0:T(1,128)S(1)}, s32[64,128]{1,0:T(8,128)S(1)}) custom-call(f32[8,512]{1,0:T(8,128)} %coup.1, f32[1,512]{1,0:T(1,128)} %bitcast.3, bf16[2048,512]{1,0:T(8,128)(2,1)} %basis.3, s32[1,64]{1,0:T(1,128)} %bitcast.4, s32[1,64]{1,0:T(1,128)} %bitcast.5), custom_call_target="tpu_custom_call" | custom-call | tf_op jit(solution)/shard_map/pallas_call | solution.py:435
  2.0 2.7 %collective-permute-start.10 = (bf16[576,512]{1,0:T(8,128)(2,1)S(1)}, bf16[576,512]{1,0:T(8,128)(2,1)S(1)}, u32[]{:S(2)}, u32[]{:S(2)}) collective-permute-start(bf16[576,512]{1,0:T(8,128)(2,1)S(1)} %get-tuple-element.38), channel_id=1, source_target_pairs={{0,1},{1,0},{2,3},{3,2},{4,6},{5,7},{6,4},{7,5},{8,9},{9,8},{10,11... | collective-permute-start | bytes 1769480 | tf_op jit(solution)/shard_map/ppermute | solution.py:33
  4.7 1.5 %collective-permute-start.9 = (bf16[320,512]{1,0:T(8,128)(2,1)S(1)}, bf16[320,512]{1,0:T(8,128)(2,1)S(1)}, u32[]{:S(2)}, u32[]{:S(2)}) collective-permute-start(bf16[320,512]{1,0:T(8,128)(2,1)S(1)} %get-tuple-element.37), channel_id=1, source_target_pairs={{0,3},{1,2},{2,1},{3,0},{4,7},{5,6},{6,5},{7,4},{8,11},{9,10},{10,... | collective-permute-start | bytes 983048 | tf_op jit(solution)/shard_map/ppermute | solution.py:33
  6.2 9.9 %collective-permute-done.10.rest_1_ = bf16[576,512]{1,0:T(8,128)(2,1)S(1)} collective-permute-done((bf16[576,512]{1,0:T(8,128)(2,1)S(1)}, bf16[576,512]{1,0:T(8,128)(2,1)S(1)}, u32[]{:S(2)}, u32[]{:S(2)}) %collective-permute-start.10) | collective-permute-done | bytes 589856 | tf_op jit(solution)/shard_map/ppermute | solution.py:33
  16.0 5.0 %collective-permute-done.9.rest_0_ = bf16[320,512]{1,0:T(8,128)(2,1)S(1)} collective-permute-done((bf16[320,512]{1,0:T(8,128)(2,1)S(1)}, bf16[320,512]{1,0:T(8,128)(2,1)S(1)}, u32[]{:S(2)}, u32[]{:S(2)}) %collective-permute-start.9) | collective-permute-done | bytes 327712 | tf_op jit(solution)/shard_map/ppermute | solution.py:33
  21.0 3.6 %collective-permute-start.3 = (f32[8,512]{1,0:T(8,128)S(1)}, f32[8,512]{1,0:T(8,128)S(1)}, u32[]{:S(2)}, u32[]{:S(2)}) collective-permute-start(f32[8,512]{1,0:T(8,128)S(1)} %get-tuple-element.28.rest_0_.table), channel_id=1, source_target_pairs={{0,24},{4,28},{8,16},{12,20},{16,8},{20,12},{24,0},{28,4},{1,25},{... | collective-permute-start | bytes 49160 | tf_op jit(solution)/shard_map/ppermute | solution.py:38
  24.6 0.8 %collective-permute-start.1 = (f32[8,512]{1,0:T(8,128)S(1)}, f32[8,512]{1,0:T(8,128)S(1)}, u32[]{:S(2)}, u32[]{:S(2)}) collective-permute-start(f32[8,512]{1,0:T(8,128)S(1)} %get-tuple-element.28.rest_0_.table), channel_id=1, source_target_pairs={{0,8},{4,12},{8,0},{12,4},{16,24},{20,28},{24,16},{28,20},{1,9},{5... | collective-permute-start | bytes 49160 | tf_op jit(solution)/shard_map/ppermute | solution.py:38
  25.4 1.7 %shard_map.57.noise = f32[8,64,512]{2,1,0:T(8,128)S(1)} custom-call(s32[64,128]{1,0:T(8,128)S(1)} %get-tuple-element.25.base, f32[8,512]{1,0:T(8,128)S(1)} %get-tuple-element.28.rest_0_.table), custom_call_target="tpu_custom_call" | custom-call | flops 15728640 | bytes 1048576 | tf_op jit(solution)/shard_map/pallas_call | solution.py:458
  27.1 2.2 %collective-permute-done.2.rest_1_ = f32[8,512]{1,0:T(8,128)S(1)} collective-permute-done((f32[8,512]{1,0:T(8,128)S(1)}, f32[8,512]{1,0:T(8,128)S(1)}, u32[]{:S(2)}, u32[]{:S(2)}) %collective-permute-start.2) | collective-permute-done | bytes 16416 | tf_op jit(solution)/shard_map/ppermute | solution.py:38
  29.6 0.8 %shard_map.59._.rest_4_ = f32[4,64,512]{2,1,0:T(8,128)S(1)} custom-call(s32[64,128]{1,0:T(8,128)S(1)} %get-tuple-element.25.base, bf16[64,512]{1,0:T(8,128)(2,1)S(1)} %get-tuple-element.31.rest_0_), custom_call_target="tpu_custom_call" | custom-call | flops 7864320 | bytes 524288 | tf_op jit(solution)/shard_map/pallas_call | solution.py:458
  30.9 1.5 %collective-permute-start.7 = (bf16[32,512]{1,0:T(8,128)(2,1)S(1)}, bf16[32,512]{1,0:T(8,128)(2,1)S(1)}, u32[]{:S(2)}, u32[]{:S(2)}) collective-permute-start(bf16[32,512]{1,0:T(8,128)(2,1)S(1)} %get-tuple-element.33.rest_0_), channel_id=1, source_target_pairs={{0,24},{4,28},{8,16},{12,20},{16,8},{20,12},{24,0},{28,4},{1,25},{... | collective-permute-start | bytes 98312 | tf_op jit(solution)/shard_map/ppermute | solution.py:38
  32.5 0.6 %collective-permute-start.6 = (bf16[32,512]{1,0:T(8,128)(2,1)S(1)}, bf16[32,512]{1,0:T(8,128)(2,1)S(1)}, u32[]{:S(2)}, u32[]{:S(2)}) collective-permute-start(bf16[32,512]{1,0:T(8,128)(2,1)S(1)} %get-tuple-element.33.rest_0_), channel_id=1, source_target_pairs={{0,16},{4,20},{8,24},{12,28},{16,0},{20,4},{24,8},{28,12},{1,17},{... | collective-permute-start | bytes 98312 | tf_op jit(solution)/shard_map/ppermute | solution.py:38
  33.1 2.3 %collective-permute-start.5 = (bf16[32,512]{1,0:T(8,128)(2,1)S(1)}, bf16[32,512]{1,0:T(8,128)(2,1)S(1)}, u32[]{:S(2)}, u32[]{:S(2)}) collective-permute-start(bf16[32,512]{1,0:T(8,128)(2,1)S(1)} %get-tuple-element.33.rest_0_), channel_id=1, source_target_pairs={{0,8},{4,12},{8,0},{12,4},{16,24},{20,28},{24,16},{28,20},{1,9},{5... | collective-permute-start | bytes 98312 | tf_op jit(solution)/shard_map/ppermute | solution.py:38
  35.4 0.8 %shard_map.61.rest_3_.rest_5_ = f32[4,64,512]{2,1,0:T(8,128)S(1)} custom-call(s32[64,128]{1,0:T(8,128)S(1)} %get-tuple-element.25.base, bf16[32,512]{1,0:T(8,128)(2,1)S(1)} %get-tuple-element.33.rest_0_), custom_call_target="tpu_custom_call" | custom-call | flops 7864320 | bytes 524288 | tf_op jit(solution)/shard_map/pallas_call | solution.py:458
  36.2 0.8 %collective-permute-done.7.rest_2_ = bf16[32,512]{1,0:T(8,128)(2,1)S(1)} collective-permute-done((bf16[32,512]{1,0:T(8,128)(2,1)S(1)}, bf16[32,512]{1,0:T(8,128)(2,1)S(1)}, u32[]{:S(2)}, u32[]{:S(2)}) %collective-permute-start.7) | collective-permute-done | bytes 32800 | tf_op jit(solution)/shard_map/ppermute | solution.py:38
  37.8 0.8 %shard_map.63._.rest_6_ = f32[4,64,512]{2,1,0:T(8,128)S(1)} custom-call(s32[64,128]{1,0:T(8,128)S(1)} %get-tuple-element.25.base, bf16[32,512]{1,0:T(8,128)(2,1)S(1)} %get-tuple-element.35.rest_0_), custom_call_target="tpu_custom_call" | custom-call | flops 7864320 | bytes 524288 | tf_op jit(solution)/shard_map/pallas_call | solution.py:458
  39.0 1.5 %collective-permute-start.15 = (bf16[80,512]{1,0:T(8,128)(2,1)S(1)}, bf16[80,512]{1,0:T(8,128)(2,1)S(1)}, u32[]{:S(2)}, u32[]{:S(2)}) collective-permute-start(bf16[80,512]{1,0:T(8,128)(2,1)S(1)} %shard_map.64.message.rest_0_), channel_id=1, source_target_pairs={{0,3},{1,2},{2,1},{3,0},{4,7},{5,6},{6,5},{7,4},{8,11},{9,10},{10,... | collective-permute-start | bytes 245768 | tf_op jit(solution)/shard_map/ppermute | solution.py:38
  40.5 1.5 %collective-permute-start.14 = (bf16[80,512]{1,0:T(8,128)(2,1)S(1)}, bf16[80,512]{1,0:T(8,128)(2,1)S(1)}, u32[]{:S(2)}, u32[]{:S(2)}) collective-permute-start(bf16[80,512]{1,0:T(8,128)(2,1)S(1)} %shard_map.64.message.rest_0_), channel_id=1, source_target_pairs={{0,2},{1,3},{2,0},{3,1},{4,6},{5,7},{6,4},{7,5},{8,10},{9,11},{10,... | collective-permute-start | bytes 245768 | tf_op jit(solution)/shard_map/ppermute | solution.py:38
  42.0 0.5 %collective-permute-start.13 = (bf16[80,512]{1,0:T(8,128)(2,1)S(1)}, bf16[80,512]{1,0:T(8,128)(2,1)S(1)}, u32[]{:S(2)}, u32[]{:S(2)}) collective-permute-start(bf16[80,512]{1,0:T(8,128)(2,1)S(1)} %shard_map.64.message.rest_0_), channel_id=1, source_target_pairs={{0,1},{1,0},{2,3},{3,2},{4,5},{5,4},{6,7},{7,6},{8,9},{9,8},{10,11... | collective-permute-start | bytes 245768 | tf_op jit(solution)/shard_map/ppermute | solution.py:38
  42.6 0.8 %shard_map.66.rest_0_.rest_7_ = f32[4,64,512]{2,1,0:T(8,128)S(1)} custom-call(s32[64,128]{1,0:T(8,128)S(1)} %get-tuple-element.25.base, bf16[80,512]{1,0:T(8,128)(2,1)S(1)} %shard_map.64.message.rest_0_), custom_call_target="tpu_custom_call" | custom-call | flops 7864320 | bytes 524288 | tf_op jit(solution)/shard_map/pallas_call | solution.py:458
  43.4 1.7 %shard_map.67 = (f32[4,64,512]{2,1,0:T(8,128)S(1)}, f32[4,64,512]{2,1,0:T(8,128)S(1)}) custom-call(s32[64,128]{1,0:T(8,128)S(1)} %get-tuple-element.25.base, f32[4,64,512]{2,1,0:T(8,128)S(1)} %shard_map.66.rest_0_.rest_7_), custom_call_target="tpu_custom_call" | custom-call | flops 15728640 | bytes 1048576 | tf_op jit(solution)/shard_map/pallas_call | solution.py:458
  45.1 0.7 %shard_map.65.partial = f32[512,512]{1,0:T(8,128)S(1)} custom-call(f32[8,512]{1,0:T(8,128)S(1)} %get-tuple-element.23.coup, f32[1,512]{1,0:T(1,128)S(1)} %get-tuple-element.24.spec, bf16[2048,512]{1,0:T(8,128)(2,1)S(1)} %copy-done, f32[8,64,512]{2,1,0:T(8,128)S(1)} %shard_map.57.noise, bf16[80,512]{1,0:T(8,128)(2,1)S(1)} %shard_map.64.message.rest_0_), custom_call_target="tpu_custom_call" | custom-call | flops 268435456 | bytes 1048576 | tf_op jit(solution)/shard_map/pallas_call | solution.py:516
  46.5 2.8 %shard_map.68 = f32[512,512]{1,0:T(8,128)} custom-call(f32[512,512]{1,0:T(8,128)S(1)} %shard_map.65.partial, bf16[320,512]{1,0:T(8,128)(2,1)S(1)} %collective-permute-done.9.rest_0_, bf16[576,512]{1,0:T(8,128)(2,1)S(1)} %collective-permute-done.10.rest_1_, bf16[320,512]{1,0:T(8,128)(2,1)S(1)} %collective-permute-done.11.rest_2_, ...), custom_call_target="tpu_custom_call" | custom-call | flops 805306368 | bytes 3145728 | tf_op jit(solution)/shard_map/pallas_call | solution.py:532
  (24 shorter events, 2.9 us)
Async XLA Ops:
  0.0 1.7 %collective-permute-start = (f32[8,512]{1,0:T(8,128)}, f32[8,512]{1,0:T(8,128)S(1)}, u32[]{:S(2)}, u32[]{:S(2)}) collective-permute-start(f32[8,512]{1,0:T(8,128)} %coup.1), channel_id=1, source_target_pairs={{0,4},{4,0},{8,12},{12,8},{16,20},{20,16},{24,28},{28,24},{1,5},{5... | collective-permute-start | bytes 49160 | tf_op jit(solution)/shard_map/ppermute | solution.py:38
  2.0 14.0 %collective-permute-start.10 = (bf16[576,512]{1,0:T(8,128)(2,1)S(1)}, bf16[576,512]{1,0:T(8,128)(2,1)S(1)}, u32[]{:S(2)}, u32[]{:S(2)}) collective-permute-start(bf16[576,512]{1,0:T(8,128)(2,1)S(1)} %get-tuple-element.38), channel_id=1, source_target_pairs={{0,1},{1,0},{2,3},{3,2},{4,6},{5,7},{6,4},{7,5},{8,9},{9,8},{10,11... | collective-permute-start | bytes 1769480 | tf_op jit(solution)/shard_map/ppermute | solution.py:33
  4.7 16.4 %collective-permute-start.9 = (bf16[320,512]{1,0:T(8,128)(2,1)S(1)}, bf16[320,512]{1,0:T(8,128)(2,1)S(1)}, u32[]{:S(2)}, u32[]{:S(2)}) collective-permute-start(bf16[320,512]{1,0:T(8,128)(2,1)S(1)} %get-tuple-element.37), channel_id=1, source_target_pairs={{0,3},{1,2},{2,1},{3,0},{4,7},{5,6},{6,5},{7,4},{8,11},{9,10},{10,... | collective-permute-start | bytes 983048 | tf_op jit(solution)/shard_map/ppermute | solution.py:33
  16.0 30.4 %collective-permute-start.12 = (bf16[576,512]{1,0:T(8,128)(2,1)S(1)}, bf16[576,512]{1,0:T(8,128)(2,1)S(1)}, u32[]{:S(2)}, u32[]{:S(2)}) collective-permute-start(bf16[576,512]{1,0:T(8,128)(2,1)S(1)} %collective-permute-done.10.rest_1_), channel_id=1, source_target_pairs={{0,4},{4,0},{8,12},{12,8},{16,20},{20,16},{24,28},{28,24},{1,5},{5... | collective-permute-start | bytes 1769480 | tf_op jit(solution)/shard_map/ppermute | solution.py:38
  21.0 25.4 %collective-permute-start.11 = (bf16[320,512]{1,0:T(8,128)(2,1)S(1)}, bf16[320,512]{1,0:T(8,128)(2,1)S(1)}, u32[]{:S(2)}, u32[]{:S(2)}) collective-permute-start(bf16[320,512]{1,0:T(8,128)(2,1)S(1)} %collective-permute-done.9.rest_0_), channel_id=1, source_target_pairs={{0,4},{4,0},{8,12},{12,8},{16,20},{20,16},{24,28},{28,24},{1,5},{5... | collective-permute-start | bytes 983048 | tf_op jit(solution)/shard_map/ppermute | solution.py:38
  21.0 6.0 %collective-permute-start.3 = (f32[8,512]{1,0:T(8,128)S(1)}, f32[8,512]{1,0:T(8,128)S(1)}, u32[]{:S(2)}, u32[]{:S(2)}) collective-permute-start(f32[8,512]{1,0:T(8,128)S(1)} %get-tuple-element.28.rest_0_.table), channel_id=1, source_target_pairs={{0,24},{4,28},{8,16},{12,20},{16,8},{20,12},{24,0},{28,4},{1,25},{... | collective-permute-start | bytes 49160 | tf_op jit(solution)/shard_map/ppermute | solution.py:38
  24.6 4.6 %collective-permute-start.2 = (f32[8,512]{1,0:T(8,128)S(1)}, f32[8,512]{1,0:T(8,128)S(1)}, u32[]{:S(2)}, u32[]{:S(2)}) collective-permute-start(f32[8,512]{1,0:T(8,128)S(1)} %get-tuple-element.28.rest_0_.table), channel_id=1, source_target_pairs={{0,16},{4,20},{8,24},{12,28},{16,0},{20,4},{24,8},{28,12},{1,17},{... | collective-permute-start | bytes 49160 | tf_op jit(solution)/shard_map/ppermute | solution.py:38
  24.6 4.6 %collective-permute-start.1 = (f32[8,512]{1,0:T(8,128)S(1)}, f32[8,512]{1,0:T(8,128)S(1)}, u32[]{:S(2)}, u32[]{:S(2)}) collective-permute-start(f32[8,512]{1,0:T(8,128)S(1)} %get-tuple-element.28.rest_0_.table), channel_id=1, source_target_pairs={{0,8},{4,12},{8,0},{12,4},{16,24},{20,28},{24,16},{28,20},{1,9},{5... | collective-permute-start | bytes 49160 | tf_op jit(solution)/shard_map/ppermute | solution.py:38
  29.6 1.3 %collective-permute-start.4 = (bf16[64,512]{1,0:T(8,128)(2,1)S(1)}, bf16[64,512]{1,0:T(8,128)(2,1)S(1)}, u32[]{:S(2)}, u32[]{:S(2)}) collective-permute-start(bf16[64,512]{1,0:T(8,128)(2,1)S(1)} %get-tuple-element.31.rest_0_), channel_id=1, source_target_pairs={{0,4},{4,0},{8,12},{12,8},{16,20},{20,16},{24,28},{28,24},{1,5},{5... | collective-permute-start | bytes 196616 | tf_op jit(solution)/shard_map/ppermute | solution.py:38
  30.9 14.2 %copy-start = (bf16[2048,512]{1,0:T(8,128)(2,1)S(1)}, bf16[2048,512]{1,0:T(8,128)(2,1)}, u32[]{:S(2)}) copy-start(bf16[2048,512]{1,0:T(8,128)(2,1)} %basis.3) | copy-start | bytes 6291460
  30.9 6.1 %collective-permute-start.7 = (bf16[32,512]{1,0:T(8,128)(2,1)S(1)}, bf16[32,512]{1,0:T(8,128)(2,1)S(1)}, u32[]{:S(2)}, u32[]{:S(2)}) collective-permute-start(bf16[32,512]{1,0:T(8,128)(2,1)S(1)} %get-tuple-element.33.rest_0_), channel_id=1, source_target_pairs={{0,24},{4,28},{8,16},{12,20},{16,8},{20,12},{24,0},{28,4},{1,25},{... | collective-permute-start | bytes 98312 | tf_op jit(solution)/shard_map/ppermute | solution.py:38
  32.5 5.0 %collective-permute-start.6 = (bf16[32,512]{1,0:T(8,128)(2,1)S(1)}, bf16[32,512]{1,0:T(8,128)(2,1)S(1)}, u32[]{:S(2)}, u32[]{:S(2)}) collective-permute-start(bf16[32,512]{1,0:T(8,128)(2,1)S(1)} %get-tuple-element.33.rest_0_), channel_id=1, source_target_pairs={{0,16},{4,20},{8,24},{12,28},{16,0},{20,4},{24,8},{28,12},{1,17},{... | collective-permute-start | bytes 98312 | tf_op jit(solution)/shard_map/ppermute | solution.py:38
  33.1 4.6 %collective-permute-start.5 = (bf16[32,512]{1,0:T(8,128)(2,1)S(1)}, bf16[32,512]{1,0:T(8,128)(2,1)S(1)}, u32[]{:S(2)}, u32[]{:S(2)}) collective-permute-start(bf16[32,512]{1,0:T(8,128)(2,1)S(1)} %get-tuple-element.33.rest_0_), channel_id=1, source_target_pairs={{0,8},{4,12},{8,0},{12,4},{16,24},{20,28},{24,16},{28,20},{1,9},{5... | collective-permute-start | bytes 98312 | tf_op jit(solution)/shard_map/ppermute | solution.py:38
  37.7 1.3 %collective-permute-start.8 = (bf16[32,512]{1,0:T(8,128)(2,1)S(1)}, bf16[32,512]{1,0:T(8,128)(2,1)S(1)}, u32[]{:S(2)}, u32[]{:S(2)}) collective-permute-start(bf16[32,512]{1,0:T(8,128)(2,1)S(1)} %get-tuple-element.35.rest_0_), channel_id=1, source_target_pairs={{0,4},{4,0},{8,12},{12,8},{16,20},{20,16},{24,28},{28,24},{1,5},{5... | collective-permute-start | bytes 98312 | tf_op jit(solution)/shard_map/ppermute | solution.py:38
  39.0 6.7 %collective-permute-start.15 = (bf16[80,512]{1,0:T(8,128)(2,1)S(1)}, bf16[80,512]{1,0:T(8,128)(2,1)S(1)}, u32[]{:S(2)}, u32[]{:S(2)}) collective-permute-start(bf16[80,512]{1,0:T(8,128)(2,1)S(1)} %shard_map.64.message.rest_0_), channel_id=1, source_target_pairs={{0,3},{1,2},{2,1},{3,0},{4,7},{5,6},{6,5},{7,4},{8,11},{9,10},{10,... | collective-permute-start | bytes 245768 | tf_op jit(solution)/shard_map/ppermute | solution.py:38
  40.5 5.7 %collective-permute-start.14 = (bf16[80,512]{1,0:T(8,128)(2,1)S(1)}, bf16[80,512]{1,0:T(8,128)(2,1)S(1)}, u32[]{:S(2)}, u32[]{:S(2)}) collective-permute-start(bf16[80,512]{1,0:T(8,128)(2,1)S(1)} %shard_map.64.message.rest_0_), channel_id=1, source_target_pairs={{0,2},{1,3},{2,0},{3,1},{4,6},{5,7},{6,4},{7,5},{8,10},{9,11},{10,... | collective-permute-start | bytes 245768 | tf_op jit(solution)/shard_map/ppermute | solution.py:38
  42.0 4.4 %collective-permute-start.13 = (bf16[80,512]{1,0:T(8,128)(2,1)S(1)}, bf16[80,512]{1,0:T(8,128)(2,1)S(1)}, u32[]{:S(2)}, u32[]{:S(2)}) collective-permute-start(bf16[80,512]{1,0:T(8,128)(2,1)S(1)} %shard_map.64.message.rest_0_), channel_id=1, source_target_pairs={{0,1},{1,0},{2,3},{3,2},{4,5},{5,4},{6,7},{7,6},{8,9},{9,8},{10,11... | collective-permute-start | bytes 245768 | tf_op jit(solution)/shard_map/ppermute | solution.py:38

commit v5 on v4

--- a/solution.py
+++ b/solution.py
@@ -257,7 +257,7 @@
     lax.fori_loop(0, vecs // 16, tile, 0)
 
 
-def combine_kernel(tm_axis, own, other, df, _, out, late):
+def combine_kernel(tm_axis, own, other, df, out, late):
     core = lax.rem(lax.axis_index(tm_axis), 2)
     first = core == 0
     half = out.shape[0]
@@ -286,7 +286,7 @@
         carry = jnp.where(core == j, mine[...], theirs[...].astype(F32))
         out[at, :] = jnp.where(core == 0, late[at, :] + gain * carry, carry).astype(BF16)
     parts = split3(df[pl.ds(0, 1), :]) + split3(df[pl.ds(1, 1), :])
-    out[pl.ds(2 * half, 16), :] = table_rows((16, modes), parts).astype(BF16)
+    out[pl.ds(2 * half, 8), :] = table_rows((8, modes), parts).astype(BF16)
 
 
 def sums_of(block):
@@ -329,7 +329,7 @@
     start = pl.multiple_of(lax.axis_index(sp_axis) * rows, rows)
     copy = pltpu.make_async_copy(basis.at[pl.ds(start, rows), :], lhs, sem)
     copy.start()
-    set_coefs(coefs, coup[...], spec[...], sums_of(message[pl.ds(vecs, 16), :].astype(F32)))
+    set_coefs(coefs, coup[...], spec[...], sums_of(message[pl.ds(vecs, 8), :].astype(F32)))
     late, early = halves_of(steps)
     width = vecs * len(late)
     values((noise,), lambda at: message[at, :].astype(F32), coefs, state, rhs.at[0], late)
@@ -381,7 +381,7 @@
         before = x[0][0:8] + x[0][8:16] + x[1][0:8]
         behind = x[1][8:16] + x[2][0:8] + x[2][8:16]
         lam = x[3][0:1] + x[3][1:2] + x[3][2:3]
-        set_coefs(coefs.at[n], jnp.where(first, before, behind), lam, sums_of(message(pl.ds(vecs, 16))))
+        set_coefs(coefs.at[n], jnp.where(first, before, behind), lam, sums_of(message(pl.ds(vecs, 8))))
     late, early = halves_of(steps)
     width = vecs * len(late)
     work = [(h, n) for h in range(2) for n in range(count)]
@@ -476,39 +476,38 @@
         scratch_shapes=[pltpu.VMEM((chips, 8, modes), F32)] + [pltpu.VMEM((steps, modes), F32)] * 2,
         **fast,
     )(own, coup, spec, table, *tables)
-    alone_0 = half_of(alone, 0, (sent,))
     total, late = kernel_call(
         functools.partial(combine_kernel, "tm"),
         out_shape=[bf16(vecs // 2, modes), f32(vecs, modes)],
-        in_specs=[VMEM] * 3 + [ANY],
+        in_specs=[VMEM] * 3,
         out_specs=[VMEM] * 2,
         **fast,
-    )(state, swap(sent, "tm", 1), sums, alone_0[0])
+    )(state, swap(sent, "tm", 1), sums)
     later = [swap(total, "tm", 2 * e) for e in range(1, chips)]
-    alone_1 = half_of(alone, 1, (total,))
+    whole = lambda routes: [(r, n * span) for r in routes for n in range(2)]
+    noise = list(noise_of(whole(alone), span, (total,)))
+    near_0 = half_of(pairs, 0, (noise[-1],)) if pairs else noise
     mine, sent = kernel_call(
         functools.partial(half_kernel, "tm"),
         out_shape=[f32(vecs // 2, modes), bf16(vecs // 2, modes)],
         in_specs=[VMEM] * (1 + len(later)) + [ANY],
         out_specs=[VMEM] * 2,
         **fast,
-    )(weights, *later, alone_1[0])
+    )(weights, *later, near_0[-1])
     theirs = swap(sent, "tm", 1)
-    near_0 = half_of(pairs, 0, (sent,)) if pairs else [sent]
+    near_1 = half_of(pairs, 1, (sent,)) if pairs else [sent]
     carry = kernel_call(
         functools.partial(carry_kernel, "tm"),
-        out_shape=bf16(vecs + 16, modes),
+        out_shape=bf16(vecs + 8, modes),
         in_specs=[VMEM] * 4 + [ANY],
         out_specs=VMEM,
         **fast,
-    )(mine, theirs, late, sums, near_0[0])
+    )(mine, theirs, late, sums, near_1[0])
     carries = [swap(carry, "space", d) for d in range(1, space)]
     swapped = [swap(m, "tm", 1) for m in direct]
-    noise = [x for both in zip(alone_0, alone_1) for x in both]
     if pairs:
-        near_1 = half_of(pairs, 1, (carry,))
-        far = noise_of([(r[::-1], n * span) for r in pairs for n in range(2)], span, (near_1[-1],))
-        noise += [x for both in zip(near_0, near_1) for x in both] + list(far)
+        noise += [x for both in zip(near_0, near_1) for x in both]
+        noise += noise_of(whole([r[::-1] for r in pairs]), span, (carry,))
 
     flops = 2 * nodes_here * modes * steps * vecs
     half_cols = steps // 2 * vecs

time: 49.4 us -> 49.6 us (level)
    pallas_call x6 -> x5, Pallas kernels: 6.66 us -> 6.64 us  [noise_of(): kernel_call(functools.partial(noise_kernel, 'tm', 'space', parts, steps,...]
  transfers between devices with their start and end apart: 16 -> 16, of which waited for: 10 -> 7; matrix products, arithmetic and copies ran while one was open for 0% -> 0% of each run, Pallas kernels for 18% -> 18%
where the time goes in v5:
time: 49.6 us; the launch traced here: 49.4 us
  waiting for transfers between devices  20.1 us (41%)
  starting transfers between devices  17.2 us (35%)
  Pallas kernels  11.9 us (24%)
    ppermute x2, waiting for transfers between devices, exchange(): return lax.ppermute(x, ('tm', 'space'), moves)  14.9 us
    ppermute x14, starting transfers between devices, swap(): return lax.ppermute(x, axis, [(i, i ^ offset) for i in range(count)])  13 us
    pallas_call x5, Pallas kernels, noise_of(): kernel_call(functools.partial(noise_kernel, 'tm', 'space', parts, steps,...  6.64 us
    ppermute x14, waiting for transfers between devices, swap(): return lax.ppermute(x, axis, [(i, i ^ offset) for i in range(count)])  5.27 us
    ppermute x2, starting transfers between devices, exchange(): return lax.ppermute(x, ('tm', 'space'), moves)  4.16 us
    pallas_call x1, Pallas kernels, local(): kernel_call(functools.partial(final_kernel, 'tm', pairs, single), out_sha...  2.78 us
    pallas_call x1, Pallas kernels, local(): kernel_call(functools.partial(pack_kernel, 'tm', 'space', routes), out_sh...  1.24 us
  transfers between devices with their start and end apart: 16, of which 7 were waited for; matrix products, arithmetic and copies ran while one was open for 0% of the time, Pallas kernels for 18%

profile of v5, /device:TPU:0, one launch (start us, length us, event | category | flops | bytes accessed | tf_op | source)
XLA Modules:
  0.0 49.4 jit_solution(2820378208779717720)
XLA Ops:
  0.5 1.2 %shard_map.55 = (bf16[320,512]{1,0:T(8,128)(2,1)S(1)}, bf16[576,512]{1,0:T(8,128)(2,1)S(1)}, f32[8,512]{1,0:T(8,128)S(1)}, f32[1,512]{1,0:T(1,128)S(1)}, s32[64,128]{1,0:T(8,128)S(1)}) custom-call(f32[8,512]{1,0:T(8,128)} %coup.1, f32[1,512]{1,0:T(1,128)} %bitcast.3, bf16[2048,512]{1,0:T(8,128)(2,1)} %basis.3, s32[1,64]{1,0:T(1,128)} %bitcast.4, s32[1,64]{1,0:T(1,128)} %bitcast.5), custom_call_target="tpu_custom_call" | custom-call | tf_op jit(solution)/shard_map/pallas_call | solution.py:435
  2.0 2.7 %collective-permute-start.10 = (bf16[576,512]{1,0:T(8,128)(2,1)S(1)}, bf16[576,512]{1,0:T(8,128)(2,1)S(1)}, u32[]{:S(2)}, u32[]{:S(2)}) collective-permute-start(bf16[576,512]{1,0:T(8,128)(2,1)S(1)} %get-tuple-element.41), channel_id=1, source_target_pairs={{0,1},{1,0},{2,3},{3,2},{4,6},{5,7},{6,4},{7,5},{8,9},{9,8},{10,11... | collective-permute-start | bytes 1769480 | tf_op jit(solution)/shard_map/ppermute | solution.py:33
  4.7 1.5 %collective-permute-start.9 = (bf16[320,512]{1,0:T(8,128)(2,1)S(1)}, bf16[320,512]{1,0:T(8,128)(2,1)S(1)}, u32[]{:S(2)}, u32[]{:S(2)}) collective-permute-start(bf16[320,512]{1,0:T(8,128)(2,1)S(1)} %get-tuple-element.40), channel_id=1, source_target_pairs={{0,3},{1,2},{2,1},{3,0},{4,7},{5,6},{6,5},{7,4},{8,11},{9,10},{10,... | collective-permute-start | bytes 983048 | tf_op jit(solution)/shard_map/ppermute | solution.py:33
  6.2 9.9 %collective-permute-done.10.rest_1_ = bf16[576,512]{1,0:T(8,128)(2,1)S(1)} collective-permute-done((bf16[576,512]{1,0:T(8,128)(2,1)S(1)}, bf16[576,512]{1,0:T(8,128)(2,1)S(1)}, u32[]{:S(2)}, u32[]{:S(2)}) %collective-permute-start.10) | collective-permute-done | bytes 589856 | tf_op jit(solution)/shard_map/ppermute | solution.py:33
  16.0 5.0 %collective-permute-done.9.rest_0_ = bf16[320,512]{1,0:T(8,128)(2,1)S(1)} collective-permute-done((bf16[320,512]{1,0:T(8,128)(2,1)S(1)}, bf16[320,512]{1,0:T(8,128)(2,1)S(1)}, u32[]{:S(2)}, u32[]{:S(2)}) %collective-permute-start.9) | collective-permute-done | bytes 327712 | tf_op jit(solution)/shard_map/ppermute | solution.py:33
  21.0 3.6 %collective-permute-start.3 = (f32[8,512]{1,0:T(8,128)S(1)}, f32[8,512]{1,0:T(8,128)S(1)}, u32[]{:S(2)}, u32[]{:S(2)}) collective-permute-start(f32[8,512]{1,0:T(8,128)S(1)} %get-tuple-element.30.rest_0_.table), channel_id=1, source_target_pairs={{0,24},{4,28},{8,16},{12,20},{16,8},{20,12},{24,0},{28,4},{1,25},{... | collective-permute-start | bytes 49160 | tf_op jit(solution)/shard_map/ppermute | solution.py:38
  24.6 0.8 %collective-permute-start.1 = (f32[8,512]{1,0:T(8,128)S(1)}, f32[8,512]{1,0:T(8,128)S(1)}, u32[]{:S(2)}, u32[]{:S(2)}) collective-permute-start(f32[8,512]{1,0:T(8,128)S(1)} %get-tuple-element.30.rest_0_.table), channel_id=1, source_target_pairs={{0,8},{4,12},{8,0},{12,4},{16,24},{20,28},{24,16},{28,20},{1,9},{5... | collective-permute-start | bytes 49160 | tf_op jit(solution)/shard_map/ppermute | solution.py:38
  25.4 1.7 %shard_map.57.noise = f32[8,64,512]{2,1,0:T(8,128)S(1)} custom-call(s32[64,128]{1,0:T(8,128)S(1)} %get-tuple-element.27.base, f32[8,512]{1,0:T(8,128)S(1)} %get-tuple-element.30.rest_0_.table), custom_call_target="tpu_custom_call" | custom-call | flops 15728640 | bytes 1048576 | tf_op jit(solution)/shard_map/pallas_call | solution.py:458
  27.1 2.2 %collective-permute-done.2.rest_1_ = f32[8,512]{1,0:T(8,128)S(1)} collective-permute-done((f32[8,512]{1,0:T(8,128)S(1)}, f32[8,512]{1,0:T(8,128)S(1)}, u32[]{:S(2)}, u32[]{:S(2)}) %collective-permute-start.2) | collective-permute-done | bytes 16416 | tf_op jit(solution)/shard_map/ppermute | solution.py:38
  29.6 1.2 %collective-permute-done.4.other = bf16[64,512]{1,0:T(8,128)(2,1)S(1)} collective-permute-done((bf16[64,512]{1,0:T(8,128)(2,1)S(1)}, bf16[64,512]{1,0:T(8,128)(2,1)S(1)}, u32[]{:S(2)}, u32[]{:S(2)}) %collective-permute-start.4) | collective-permute-done | bytes 65568 | tf_op jit(solution)/shard_map/ppermute | solution.py:38
  30.9 1.5 %collective-permute-start.7 = (bf16[32,512]{1,0:T(8,128)(2,1)S(1)}, bf16[32,512]{1,0:T(8,128)(2,1)S(1)}, u32[]{:S(2)}, u32[]{:S(2)}) collective-permute-start(bf16[32,512]{1,0:T(8,128)(2,1)S(1)} %get-tuple-element.35.rest_0_), channel_id=1, source_target_pairs={{0,24},{4,28},{8,16},{12,20},{16,8},{20,12},{24,0},{28,4},{1,25},{... | collective-permute-start | bytes 98312 | tf_op jit(solution)/shard_map/ppermute | solution.py:38
  32.4 0.6 %collective-permute-start.6 = (bf16[32,512]{1,0:T(8,128)(2,1)S(1)}, bf16[32,512]{1,0:T(8,128)(2,1)S(1)}, u32[]{:S(2)}, u32[]{:S(2)}) collective-permute-start(bf16[32,512]{1,0:T(8,128)(2,1)S(1)} %get-tuple-element.35.rest_0_), channel_id=1, source_target_pairs={{0,16},{4,20},{8,24},{12,28},{16,0},{20,4},{24,8},{28,12},{1,17},{... | collective-permute-start | bytes 98312 | tf_op jit(solution)/shard_map/ppermute | solution.py:38
  33.1 2.3 %collective-permute-start.5 = (bf16[32,512]{1,0:T(8,128)(2,1)S(1)}, bf16[32,512]{1,0:T(8,128)(2,1)S(1)}, u32[]{:S(2)}, u32[]{:S(2)}) collective-permute-start(bf16[32,512]{1,0:T(8,128)(2,1)S(1)} %get-tuple-element.35.rest_0_), channel_id=1, source_target_pairs={{0,8},{4,12},{8,0},{12,4},{16,24},{20,28},{24,16},{28,20},{1,9},{5... | collective-permute-start | bytes 98312 | tf_op jit(solution)/shard_map/ppermute | solution.py:38
  35.4 1.7 %shard_map.60 = (f32[4,64,512]{2,1,0:T(8,128)S(1)}, f32[4,64,512]{2,1,0:T(8,128)S(1)}) custom-call(s32[64,128]{1,0:T(8,128)S(1)} %get-tuple-element.27.base, bf16[32,512]{1,0:T(8,128)(2,1)S(1)} %get-tuple-element.35.rest_0_), custom_call_target="tpu_custom_call" | custom-call | flops 15728640 | bytes 1048576 | tf_op jit(solution)/shard_map/pallas_call | solution.py:458
  37.0 0.8 %shard_map.61.rest_3_.rest_6_ = f32[4,64,512]{2,1,0:T(8,128)S(1)} custom-call(s32[64,128]{1,0:T(8,128)S(1)} %get-tuple-element.27.base, f32[4,64,512]{2,1,0:T(8,128)S(1)} %get-tuple-element.36.rest_0_.rest_5_), custom_call_target="tpu_custom_call" | custom-call | flops 7864320 | bytes 524288 | tf_op jit(solution)/shard_map/pallas_call | solution.py:458
  38.0 0.8 %shard_map.63._.rest_7_ = f32[4,64,512]{2,1,0:T(8,128)S(1)} custom-call(s32[64,128]{1,0:T(8,128)S(1)} %get-tuple-element.27.base, bf16[32,512]{1,0:T(8,128)(2,1)S(1)} %get-tuple-element.38.rest_0_), custom_call_target="tpu_custom_call" | custom-call | flops 7864320 | bytes 524288 | tf_op jit(solution)/shard_map/pallas_call | solution.py:458
  39.3 1.5 %collective-permute-start.15 = (bf16[72,512]{1,0:T(8,128)(2,1)S(1)}, bf16[72,512]{1,0:T(8,128)(2,1)S(1)}, u32[]{:S(2)}, u32[]{:S(2)}) collective-permute-start(bf16[72,512]{1,0:T(8,128)(2,1)S(1)} %shard_map.64.message.rest_0_), channel_id=1, source_target_pairs={{0,3},{1,2},{2,1},{3,0},{4,7},{5,6},{6,5},{7,4},{8,11},{9,10},{10,... | collective-permute-start | bytes 221192 | tf_op jit(solution)/shard_map/ppermute | solution.py:38
  40.8 1.5 %collective-permute-start.14 = (bf16[72,512]{1,0:T(8,128)(2,1)S(1)}, bf16[72,512]{1,0:T(8,128)(2,1)S(1)}, u32[]{:S(2)}, u32[]{:S(2)}) collective-permute-start(bf16[72,512]{1,0:T(8,128)(2,1)S(1)} %shard_map.64.message.rest_0_), channel_id=1, source_target_pairs={{0,2},{1,3},{2,0},{3,1},{4,6},{5,7},{6,4},{7,5},{8,10},{9,11},{10,... | collective-permute-start | bytes 221192 | tf_op jit(solution)/shard_map/ppermute | solution.py:38
  42.3 0.5 %collective-permute-start.13 = (bf16[72,512]{1,0:T(8,128)(2,1)S(1)}, bf16[72,512]{1,0:T(8,128)(2,1)S(1)}, u32[]{:S(2)}, u32[]{:S(2)}) collective-permute-start(bf16[72,512]{1,0:T(8,128)(2,1)S(1)} %shard_map.64.message.rest_0_), channel_id=1, source_target_pairs={{0,1},{1,0},{2,3},{3,2},{4,5},{5,4},{6,7},{7,6},{8,9},{9,8},{10,11... | collective-permute-start | bytes 221192 | tf_op jit(solution)/shard_map/ppermute | solution.py:38
  42.8 1.7 %shard_map.66 = (f32[4,64,512]{2,1,0:T(8,128)S(1)}, f32[4,64,512]{2,1,0:T(8,128)S(1)}) custom-call(s32[64,128]{1,0:T(8,128)S(1)} %get-tuple-element.27.base, bf16[72,512]{1,0:T(8,128)(2,1)S(1)} %shard_map.64.message.rest_0_), custom_call_target="tpu_custom_call" | custom-call | flops 15728640 | bytes 1048576 | tf_op jit(solution)/shard_map/pallas_call | solution.py:458
  44.5 0.7 %shard_map.65.partial = f32[512,512]{1,0:T(8,128)S(1)} custom-call(f32[8,512]{1,0:T(8,128)S(1)} %get-tuple-element.25.coup, f32[1,512]{1,0:T(1,128)S(1)} %get-tuple-element.26.spec, bf16[2048,512]{1,0:T(8,128)(2,1)S(1)} %copy-done, f32[8,64,512]{2,1,0:T(8,128)S(1)} %shard_map.57.noise, bf16[72,512]{1,0:T(8,128)(2,1)S(1)} %shard_map.64.message.rest_0_), custom_call_target="tpu_custom_call" | custom-call | flops 268435456 | bytes 1048576 | tf_op jit(solution)/shard_map/pallas_call | solution.py:515
  45.2 1.0 %collective-permute-done.14.rest_11_ = bf16[72,512]{1,0:T(8,128)(2,1)S(1)} collective-permute-done((bf16[72,512]{1,0:T(8,128)(2,1)S(1)}, bf16[72,512]{1,0:T(8,128)(2,1)S(1)}, u32[]{:S(2)}, u32[]{:S(2)}) %collective-permute-start.14) | collective-permute-done | bytes 73760 | tf_op jit(solution)/shard_map/ppermute | solution.py:38
  46.1 0.5 collective-permute-done.13.rest_10_
  46.6 2.8 %shard_map.67 = f32[512,512]{1,0:T(8,128)} custom-call(f32[512,512]{1,0:T(8,128)S(1)} %shard_map.65.partial, bf16[320,512]{1,0:T(8,128)(2,1)S(1)} %collective-permute-done.9.rest_0_, bf16[576,512]{1,0:T(8,128)(2,1)S(1)} %collective-permute-done.10.rest_1_, bf16[320,512]{1,0:T(8,128)(2,1)S(1)} %collective-permute-done.11.rest_2_, ...), custom_call_target="tpu_custom_call" | custom-call | flops 805306368 | bytes 3145728 | tf_op jit(solution)/shard_map/pallas_call | solution.py:531
  (23 shorter events, 1.6 us)
Async XLA Ops:
  0.0 1.7 %collective-permute-start = (f32[8,512]{1,0:T(8,128)}, f32[8,512]{1,0:T(8,128)S(1)}, u32[]{:S(2)}, u32[]{:S(2)}) collective-permute-start(f32[8,512]{1,0:T(8,128)} %coup.1), channel_id=1, source_target_pairs={{0,4},{4,0},{8,12},{12,8},{16,20},{20,16},{24,28},{28,24},{1,5},{5... | collective-permute-start | bytes 49160 | tf_op jit(solution)/shard_map/ppermute | solution.py:38
  2.0 14.0 %collective-permute-start.10 = (bf16[576,512]{1,0:T(8,128)(2,1)S(1)}, bf16[576,512]{1,0:T(8,128)(2,1)S(1)}, u32[]{:S(2)}, u32[]{:S(2)}) collective-permute-start(bf16[576,512]{1,0:T(8,128)(2,1)S(1)} %get-tuple-element.41), channel_id=1, source_target_pairs={{0,1},{1,0},{2,3},{3,2},{4,6},{5,7},{6,4},{7,5},{8,9},{9,8},{10,11... | collective-permute-start | bytes 1769480 | tf_op jit(solution)/shard_map/ppermute | solution.py:33
  4.7 16.4 %collective-permute-start.9 = (bf16[320,512]{1,0:T(8,128)(2,1)S(1)}, bf16[320,512]{1,0:T(8,128)(2,1)S(1)}, u32[]{:S(2)}, u32[]{:S(2)}) collective-permute-start(bf16[320,512]{1,0:T(8,128)(2,1)S(1)} %get-tuple-element.40), channel_id=1, source_target_pairs={{0,3},{1,2},{2,1},{3,0},{4,7},{5,6},{6,5},{7,4},{8,11},{9,10},{10,... | collective-permute-start | bytes 983048 | tf_op jit(solution)/shard_map/ppermute | solution.py:33
  16.0 30.6 %collective-permute-start.12 = (bf16[576,512]{1,0:T(8,128)(2,1)S(1)}, bf16[576,512]{1,0:T(8,128)(2,1)S(1)}, u32[]{:S(2)}, u32[]{:S(2)}) collective-permute-start(bf16[576,512]{1,0:T(8,128)(2,1)S(1)} %collective-permute-done.10.rest_1_), channel_id=1, source_target_pairs={{0,4},{4,0},{8,12},{12,8},{16,20},{20,16},{24,28},{28,24},{1,5},{5... | collective-permute-start | bytes 1769480 | tf_op jit(solution)/shard_map/ppermute | solution.py:38
  21.0 25.6 %collective-permute-start.11 = (bf16[320,512]{1,0:T(8,128)(2,1)S(1)}, bf16[320,512]{1,0:T(8,128)(2,1)S(1)}, u32[]{:S(2)}, u32[]{:S(2)}) collective-permute-start(bf16[320,512]{1,0:T(8,128)(2,1)S(1)} %collective-permute-done.9.rest_0_), channel_id=1, source_target_pairs={{0,4},{4,0},{8,12},{12,8},{16,20},{20,16},{24,28},{28,24},{1,5},{5... | collective-permute-start | bytes 983048 | tf_op jit(solution)/shard_map/ppermute | solution.py:38
  21.0 6.0 %collective-permute-start.3 = (f32[8,512]{1,0:T(8,128)S(1)}, f32[8,512]{1,0:T(8,128)S(1)}, u32[]{:S(2)}, u32[]{:S(2)}) collective-permute-start(f32[8,512]{1,0:T(8,128)S(1)} %get-tuple-element.30.rest_0_.table), channel_id=1, source_target_pairs={{0,24},{4,28},{8,16},{12,20},{16,8},{20,12},{24,0},{28,4},{1,25},{... | collective-permute-start | bytes 49160 | tf_op jit(solution)/shard_map/ppermute | solution.py:38
  24.6 4.6 %collective-permute-start.2 = (f32[8,512]{1,0:T(8,128)S(1)}, f32[8,512]{1,0:T(8,128)S(1)}, u32[]{:S(2)}, u32[]{:S(2)}) collective-permute-start(f32[8,512]{1,0:T(8,128)S(1)} %get-tuple-element.30.rest_0_.table), channel_id=1, source_target_pairs={{0,16},{4,20},{8,24},{12,28},{16,0},{20,4},{24,8},{28,12},{1,17},{... | collective-permute-start | bytes 49160 | tf_op jit(solution)/shard_map/ppermute | solution.py:38
  24.6 4.6 %collective-permute-start.1 = (f32[8,512]{1,0:T(8,128)S(1)}, f32[8,512]{1,0:T(8,128)S(1)}, u32[]{:S(2)}, u32[]{:S(2)}) collective-permute-start(f32[8,512]{1,0:T(8,128)S(1)} %get-tuple-element.30.rest_0_.table), channel_id=1, source_target_pairs={{0,8},{4,12},{8,0},{12,4},{16,24},{20,28},{24,16},{28,20},{1,9},{5... | collective-permute-start | bytes 49160 | tf_op jit(solution)/shard_map/ppermute | solution.py:38
  29.5 1.3 %collective-permute-start.4 = (bf16[64,512]{1,0:T(8,128)(2,1)S(1)}, bf16[64,512]{1,0:T(8,128)(2,1)S(1)}, u32[]{:S(2)}, u32[]{:S(2)}) collective-permute-start(bf16[64,512]{1,0:T(8,128)(2,1)S(1)} %get-tuple-element.33), channel_id=1, source_target_pairs={{0,4},{4,0},{8,12},{12,8},{16,20},{20,16},{24,28},{28,24},{1,5},{5... | collective-permute-start | bytes 196616 | tf_op jit(solution)/shard_map/ppermute | solution.py:38
  30.9 7.0 %collective-permute-start.7 = (bf16[32,512]{1,0:T(8,128)(2,1)S(1)}, bf16[32,512]{1,0:T(8,128)(2,1)S(1)}, u32[]{:S(2)}, u32[]{:S(2)}) collective-permute-start(bf16[32,512]{1,0:T(8,128)(2,1)S(1)} %get-tuple-element.35.rest_0_), channel_id=1, source_target_pairs={{0,24},{4,28},{8,16},{12,20},{16,8},{20,12},{24,0},{28,4},{1,25},{... | collective-permute-start | bytes 98312 | tf_op jit(solution)/shard_map/ppermute | solution.py:38
  32.4 5.4 %collective-permute-start.6 = (bf16[32,512]{1,0:T(8,128)(2,1)S(1)}, bf16[32,512]{1,0:T(8,128)(2,1)S(1)}, u32[]{:S(2)}, u32[]{:S(2)}) collective-permute-start(bf16[32,512]{1,0:T(8,128)(2,1)S(1)} %get-tuple-element.35.rest_0_), channel_id=1, source_target_pairs={{0,16},{4,20},{8,24},{12,28},{16,0},{20,4},{24,8},{28,12},{1,17},{... | collective-permute-start | bytes 98312 | tf_op jit(solution)/shard_map/ppermute | solution.py:38
  33.1 4.8 %collective-permute-start.5 = (bf16[32,512]{1,0:T(8,128)(2,1)S(1)}, bf16[32,512]{1,0:T(8,128)(2,1)S(1)}, u32[]{:S(2)}, u32[]{:S(2)}) collective-permute-start(bf16[32,512]{1,0:T(8,128)(2,1)S(1)} %get-tuple-element.35.rest_0_), channel_id=1, source_target_pairs={{0,8},{4,12},{8,0},{12,4},{16,24},{20,28},{24,16},{28,20},{1,9},{5... | collective-permute-start | bytes 98312 | tf_op jit(solution)/shard_map/ppermute | solution.py:38
  37.0 7.5 %copy-start = (bf16[2048,512]{1,0:T(8,128)(2,1)S(1)}, bf16[2048,512]{1,0:T(8,128)(2,1)}, u32[]{:S(2)}) copy-start(bf16[2048,512]{1,0:T(8,128)(2,1)} %basis.3) | copy-start | bytes 6291460
  37.9 1.3 %collective-permute-start.8 = (bf16[32,512]{1,0:T(8,128)(2,1)S(1)}, bf16[32,512]{1,0:T(8,128)(2,1)S(1)}, u32[]{:S(2)}, u32[]{:S(2)}) collective-permute-start(bf16[32,512]{1,0:T(8,128)(2,1)S(1)} %get-tuple-element.38.rest_0_), channel_id=1, source_target_pairs={{0,4},{4,0},{8,12},{12,8},{16,20},{20,16},{24,28},{28,24},{1,5},{5... | collective-permute-start | bytes 98312 | tf_op jit(solution)/shard_map/ppermute | solution.py:38
  39.3 5.9 %collective-permute-start.15 = (bf16[72,512]{1,0:T(8,128)(2,1)S(1)}, bf16[72,512]{1,0:T(8,128)(2,1)S(1)}, u32[]{:S(2)}, u32[]{:S(2)}) collective-permute-start(bf16[72,512]{1,0:T(8,128)(2,1)S(1)} %shard_map.64.message.rest_0_), channel_id=1, source_target_pairs={{0,3},{1,2},{2,1},{3,0},{4,7},{5,6},{6,5},{7,4},{8,11},{9,10},{10,... | collective-permute-start | bytes 221192 | tf_op jit(solution)/shard_map/ppermute | solution.py:38
  40.8 5.4 %collective-permute-start.14 = (bf16[72,512]{1,0:T(8,128)(2,1)S(1)}, bf16[72,512]{1,0:T(8,128)(2,1)S(1)}, u32[]{:S(2)}, u32[]{:S(2)}) collective-permute-start(bf16[72,512]{1,0:T(8,128)(2,1)S(1)} %shard_map.64.message.rest_0_), channel_id=1, source_target_pairs={{0,2},{1,3},{2,0},{3,1},{4,6},{5,7},{6,4},{7,5},{8,10},{9,11},{10,... | collective-permute-start | bytes 221192 | tf_op jit(solution)/shard_map/ppermute | solution.py:38
  42.3 4.4 %collective-permute-start.13 = (bf16[72,512]{1,0:T(8,128)(2,1)S(1)}, bf16[72,512]{1,0:T(8,128)(2,1)S(1)}, u32[]{:S(2)}, u32[]{:S(2)}) collective-permute-start(bf16[72,512]{1,0:T(8,128)(2,1)S(1)} %shard_map.64.message.rest_0_), channel_id=1, source_target_pairs={{0,1},{1,0},{2,3},{3,2},{4,5},{5,4},{6,7},{7,6},{8,9},{9,8},{10,11... | collective-permute-start | bytes 221192 | tf_op jit(solution)/shard_map/ppermute | solution.py:38

commit v6 on v5

--- a/solution.py
+++ b/solution.py
@@ -76,7 +76,7 @@
 
 
 def pack_kernel(tm_axis, sp_axis, offsets, coup, spec, basis, keys, counters, *rest):
-    *outs, coup_out, spec_out, base, key_row, counter_row, sems = rest
+    *outs, coup_out, spec_out, base, early, key_row, counter_row, sems = rest
     me, sp = lax.axis_index(tm_axis), lax.axis_index(sp_axis)
     core = lax.rem(me, 2)
     copies = [
@@ -101,6 +101,7 @@
     for copy in rows_in:
         copy.wait()
     base_columns(key_row, counter_row, base)
+    fill_noise(early, base, mode_ids(sp, early.shape[2]), me * coup.shape[0], 0)
     for copy in copies:
         copy.wait()
 
@@ -166,24 +167,40 @@
     base[...] = jnp.broadcast_to(start, base.shape)
 
 
+def fill_noise(out, base, ids, first_step, begin):
+    steps, vecs, modes = out.shape
+    lane = ids * jnp.int32(-1640531535)
+    group = 8
+
+    def step(t, _):
+        shifted = lane + (first_step + t) * jnp.int32(374761393)
+        for v in range(vecs // group):
+            seeded = jnp.tile(base[pl.ds(v * group, group), :], (1, modes // 128)) + shifted
+            out[t, pl.ds(v * group, group), :] = gaussian(seeded)
+        return 0
+
+    lax.fori_loop(begin, steps, step, 0)
+
+
+def mode_ids(block, modes):
+    return block * modes + lax.broadcasted_iota(jnp.int32, (1, modes), 1)
+
+
 def noise_kernel(tm_axis, sp_axis, parts, total_steps, extras, base, *rest):
     outs = rest[extras:]
     me, sp = lax.axis_index(tm_axis), lax.axis_index(sp_axis)
-    group = 8
     for out, (offset, begin) in zip(outs, parts):
-        steps, vecs, modes = out.shape
-        ids = (sp ^ pick(lax.rem(me, 2), offset)) * modes + lax.broadcasted_iota(jnp.int32, (1, modes), 1)
-        lane = ids * jnp.int32(-1640531535)
-        first_step = me * total_steps + begin
-
-        def step(t, _):
-            shifted = lane + (first_step + t) * jnp.int32(374761393)
-            for v in range(vecs // group):
-                seeded = jnp.tile(base[pl.ds(v * group, group), :], (1, modes // 128)) + shifted
-                out[t, pl.ds(v * group, group), :] = gaussian(seeded)
-            return 0
-
-        lax.fori_loop(0, steps, step, 0)
+        ids = mode_ids(sp ^ pick(lax.rem(me, 2), offset), out.shape[2])
+        fill_noise(out, base, ids, me * total_steps + begin, 0)
+
+
+def chip_kernel(tm_axis, sp_axis, base, early, _, out):
+    steps, _, modes = out.shape
+    made = early.shape[0]
+    for t in range(made):
+        out[t] = early[t]
+    me, sp = lax.axis_index(tm_axis), lax.axis_index(sp_axis)
+    fill_noise(out, base, mode_ids(sp, modes), me * steps, made)
 
 
 def running(x, combine, identity):
@@ -432,12 +449,13 @@
     routes = [(d, d) for d in single] + pairs
     sizes = [half + TAIL] * len(single) + [nodes_here + TAIL] * len(pairs)
     other = swap(coupling, "tm", 1)
-    *messages, coup, spec, base = kernel_call(
+    *messages, coup, spec, base, early = kernel_call(
         functools.partial(pack_kernel, "tm", "space", routes),
         out_shape=[bf16(n, modes) for n in sizes]
-        + [f32(steps, modes), f32(1, modes), jax.ShapeDtypeStruct((vecs, 128), jnp.int32)],
+        + [f32(steps, modes), f32(1, modes), jax.ShapeDtypeStruct((vecs, 128), jnp.int32)]
+        + [f32(steps // 4, vecs, modes)],
         in_specs=[HBM] * 5,
-        out_specs=[VMEM] * (len(sizes) + 3),
+        out_specs=[VMEM] * (len(sizes) + 4),
         scratch_shapes=[pltpu.VMEM((1, vecs), jnp.int32)] * 2 + [pltpu.SemaphoreType.DMA((len(sizes) + 4,))],
         **fast,
     )(*in_hbm)
@@ -467,7 +485,13 @@
     span = steps // 2
     alone = [(d, d) for d in single]
     half_of = lambda routes, part, after: noise_of([(r, part * span) for r in routes], span, after)
-    (own,) = noise_of([((0, 0), 0)], steps, (table,))
+    own = kernel_call(
+        functools.partial(chip_kernel, "tm", "space"),
+        out_shape=f32(steps, vecs, modes),
+        in_specs=[VMEM] * 2 + [ANY],
+        out_specs=VMEM,
+        **fast,
+    )(base, early, table)
     state, sent, weights, sums = kernel_call(
         functools.partial(offset_kernel, "tm"),
         out_shape=[f32(vecs, modes), bf16(vecs, modes), f32(chips, 8, modes), f32(8, modes)],

time: 49.6 us -> 49.6 us (level)
    pallas_call x5 -> x4, Pallas kernels: 6.64 us -> 4.99 us  [noise_of(): kernel_call(functools.partial(noise_kernel, 'tm', 'space', parts, steps,...]
    pallas_call x0 -> x1, Pallas kernels: none -> 1.25 us  [local(): kernel_call(functools.partial(chip_kernel, 'tm', 'space'), out_shape=f32(...]
  transfers between devices with their start and end apart: 16 -> 16, of which waited for: 7 -> 7; matrix products, arithmetic and copies ran while one was open for 0% -> 0% of each run, Pallas kernels for 18% -> 17%
where the time goes in v6:
time: 49.6 us; the launch traced here: 49.4 us
  waiting for transfers between devices  20.5 us (41%)
  starting transfers between devices  17.2 us (35%)
  Pallas kernels  11.5 us (23%)
    ppermute x2, waiting for transfers between devices, exchange(): return lax.ppermute(x, ('tm', 'space'), moves)  14.9 us
    ppermute x14, starting transfers between devices, swap(): return lax.ppermute(x, axis, [(i, i ^ offset) for i in range(count)])  13 us
    ppermute x14, waiting for transfers between devices, swap(): return lax.ppermute(x, axis, [(i, i ^ offset) for i in range(count)])  5.66 us
    pallas_call x4, Pallas kernels, noise_of(): kernel_call(functools.partial(noise_kernel, 'tm', 'space', parts, steps,...  4.99 us
    ppermute x2, starting transfers between devices, exchange(): return lax.ppermute(x, ('tm', 'space'), moves)  4.16 us
    pallas_call x1, Pallas kernels, local(): kernel_call(functools.partial(final_kernel, 'tm', pairs, single), out_sha...  2.78 us
    pallas_call x1, Pallas kernels, local(): kernel_call(functools.partial(chip_kernel, 'tm', 'space'), out_shape=f32(...  1.25 us
    pallas_call x1, Pallas kernels, local(): kernel_call(functools.partial(pack_kernel, 'tm', 'space', routes), out_sh...  1.24 us
  transfers between devices with their start and end apart: 16, of which 7 were waited for; matrix products, arithmetic and copies ran while one was open for 0% of the time, Pallas kernels for 17%

profile of v6, /device:TPU:0, one launch (start us, length us, event | category | flops | bytes accessed | tf_op | source)
XLA Modules:
  0.0 49.4 jit_solution(11111708645901103434)
XLA Ops:
  0.5 1.2 %shard_map.55 = (bf16[320,512]{1,0:T(8,128)(2,1)S(1)}, bf16[576,512]{1,0:T(8,128)(2,1)S(1)}, f32[8,512]{1,0:T(8,128)S(1)}, f32[1,512]{1,0:T(1,128)S(1)}, s32[64,...) custom-call(f32[8,512]{1,0:T(8,128)} %coup.1, f32[1,512]{1,0:T(1,128)} %bitcast.3, bf16[2048,512]{1,0:T(8,128)(2,1)} %basis.3, ...), custom_call_target="tpu_custom_call" | custom-call | tf_op jit(solution)/shard_map/pallas_call | solution.py:452
  2.0 2.7 %collective-permute-start.10 = (bf16[576,512]{1,0:T(8,128)(2,1)S(1)}, bf16[576,512]{1,0:T(8,128)(2,1)S(1)}, u32[]{:S(2)}, u32[]{:S(2)}) collective-permute-start(bf16[576,512]{1,0:T(8,128)(2,1)S(1)} %get-tuple-element.43), channel_id=1, source_target_pairs={{0,1},{1,0},{2,3},{3,2},{4,6},{5,7},{6,4},{7,5},{8,9},{9,8},{10,11... | collective-permute-start | bytes 1769480 | tf_op jit(solution)/shard_map/ppermute | solution.py:33
  4.7 1.5 %collective-permute-start.9 = (bf16[320,512]{1,0:T(8,128)(2,1)S(1)}, bf16[320,512]{1,0:T(8,128)(2,1)S(1)}, u32[]{:S(2)}, u32[]{:S(2)}) collective-permute-start(bf16[320,512]{1,0:T(8,128)(2,1)S(1)} %get-tuple-element.42), channel_id=1, source_target_pairs={{0,3},{1,2},{2,1},{3,0},{4,7},{5,6},{6,5},{7,4},{8,11},{9,10},{10,... | collective-permute-start | bytes 983048 | tf_op jit(solution)/shard_map/ppermute | solution.py:33
  6.2 9.9 %collective-permute-done.10.rest_1_ = bf16[576,512]{1,0:T(8,128)(2,1)S(1)} collective-permute-done((bf16[576,512]{1,0:T(8,128)(2,1)S(1)}, bf16[576,512]{1,0:T(8,128)(2,1)S(1)}, u32[]{:S(2)}, u32[]{:S(2)}) %collective-permute-start.10) | collective-permute-done | bytes 589856 | tf_op jit(solution)/shard_map/ppermute | solution.py:33
  16.0 5.0 %collective-permute-done.9.rest_0_ = bf16[320,512]{1,0:T(8,128)(2,1)S(1)} collective-permute-done((bf16[320,512]{1,0:T(8,128)(2,1)S(1)}, bf16[320,512]{1,0:T(8,128)(2,1)S(1)}, u32[]{:S(2)}, u32[]{:S(2)}) %collective-permute-start.9) | collective-permute-done | bytes 327712 | tf_op jit(solution)/shard_map/ppermute | solution.py:33
  21.0 3.6 %collective-permute-start.3 = (f32[8,512]{1,0:T(8,128)S(1)}, f32[8,512]{1,0:T(8,128)S(1)}, u32[]{:S(2)}, u32[]{:S(2)}) collective-permute-start(f32[8,512]{1,0:T(8,128)S(1)} %get-tuple-element.32._.table), channel_id=1, source_target_pairs={{0,24},{4,28},{8,16},{12,20},{16,8},{20,12},{24,0},{28,4},{1,25},{... | collective-permute-start | bytes 49160 | tf_op jit(solution)/shard_map/ppermute | solution.py:38
  24.6 0.8 %collective-permute-start.1 = (f32[8,512]{1,0:T(8,128)S(1)}, f32[8,512]{1,0:T(8,128)S(1)}, u32[]{:S(2)}, u32[]{:S(2)}) collective-permute-start(f32[8,512]{1,0:T(8,128)S(1)} %get-tuple-element.32._.table), channel_id=1, source_target_pairs={{0,8},{4,12},{8,0},{12,4},{16,24},{20,28},{24,16},{28,20},{1,9},{5... | collective-permute-start | bytes 49160 | tf_op jit(solution)/shard_map/ppermute | solution.py:38
  25.4 1.3 %shard_map.57.noise = f32[8,64,512]{2,1,0:T(8,128)S(1)} custom-call(s32[64,128]{1,0:T(8,128)S(1)} %get-tuple-element.28.base, f32[2,64,512]{2,1,0:T(8,128)S(1)} %get-tuple-element.29.early, f32[8,512]{1,0:T(8,128)S(1)} %get-tuple-element.32._.table), custom_call_target="tpu_custom_call" | custom-call | tf_op jit(solution)/shard_map/pallas_call | solution.py:488
  26.7 2.6 %collective-permute-done.2.rest_1_ = f32[8,512]{1,0:T(8,128)S(1)} collective-permute-done((f32[8,512]{1,0:T(8,128)S(1)}, f32[8,512]{1,0:T(8,128)S(1)}, u32[]{:S(2)}, u32[]{:S(2)}) %collective-permute-start.2) | collective-permute-done | bytes 16416 | tf_op jit(solution)/shard_map/ppermute | solution.py:38
  29.6 1.2 %collective-permute-done.4.other = bf16[64,512]{1,0:T(8,128)(2,1)S(1)} collective-permute-done((bf16[64,512]{1,0:T(8,128)(2,1)S(1)}, bf16[64,512]{1,0:T(8,128)(2,1)S(1)}, u32[]{:S(2)}, u32[]{:S(2)}) %collective-permute-start.4) | collective-permute-done | bytes 65568 | tf_op jit(solution)/shard_map/ppermute | solution.py:38
  30.9 1.5 %collective-permute-start.7 = (bf16[32,512]{1,0:T(8,128)(2,1)S(1)}, bf16[32,512]{1,0:T(8,128)(2,1)S(1)}, u32[]{:S(2)}, u32[]{:S(2)}) collective-permute-start(bf16[32,512]{1,0:T(8,128)(2,1)S(1)} %get-tuple-element.37.rest_0_), channel_id=1, source_target_pairs={{0,24},{4,28},{8,16},{12,20},{16,8},{20,12},{24,0},{28,4},{1,25},{... | collective-permute-start | bytes 98312 | tf_op jit(solution)/shard_map/ppermute | solution.py:38
  32.4 0.6 %collective-permute-start.6 = (bf16[32,512]{1,0:T(8,128)(2,1)S(1)}, bf16[32,512]{1,0:T(8,128)(2,1)S(1)}, u32[]{:S(2)}, u32[]{:S(2)}) collective-permute-start(bf16[32,512]{1,0:T(8,128)(2,1)S(1)} %get-tuple-element.37.rest_0_), channel_id=1, source_target_pairs={{0,16},{4,20},{8,24},{12,28},{16,0},{20,4},{24,8},{28,12},{1,17},{... | collective-permute-start | bytes 98312 | tf_op jit(solution)/shard_map/ppermute | solution.py:38
  33.1 2.3 %collective-permute-start.5 = (bf16[32,512]{1,0:T(8,128)(2,1)S(1)}, bf16[32,512]{1,0:T(8,128)(2,1)S(1)}, u32[]{:S(2)}, u32[]{:S(2)}) collective-permute-start(bf16[32,512]{1,0:T(8,128)(2,1)S(1)} %get-tuple-element.37.rest_0_), channel_id=1, source_target_pairs={{0,8},{4,12},{8,0},{12,4},{16,24},{20,28},{24,16},{28,20},{1,9},{5... | collective-permute-start | bytes 98312 | tf_op jit(solution)/shard_map/ppermute | solution.py:38
  35.4 1.7 %shard_map.60 = (f32[4,64,512]{2,1,0:T(8,128)S(1)}, f32[4,64,512]{2,1,0:T(8,128)S(1)}) custom-call(s32[64,128]{1,0:T(8,128)S(1)} %get-tuple-element.28.base, bf16[32,512]{1,0:T(8,128)(2,1)S(1)} %get-tuple-element.37.rest_0_), custom_call_target="tpu_custom_call" | custom-call | flops 15728640 | bytes 1048576 | tf_op jit(solution)/shard_map/pallas_call | solution.py:476
  37.0 0.8 %shard_map.61.rest_3_.rest_6_ = f32[4,64,512]{2,1,0:T(8,128)S(1)} custom-call(s32[64,128]{1,0:T(8,128)S(1)} %get-tuple-element.28.base, f32[4,64,512]{2,1,0:T(8,128)S(1)} %get-tuple-element.38.rest_0_.rest_5_), custom_call_target="tpu_custom_call" | custom-call | flops 7864320 | bytes 524288 | tf_op jit(solution)/shard_map/pallas_call | solution.py:476
  38.0 0.8 %shard_map.63._.rest_7_ = f32[4,64,512]{2,1,0:T(8,128)S(1)} custom-call(s32[64,128]{1,0:T(8,128)S(1)} %get-tuple-element.28.base, bf16[32,512]{1,0:T(8,128)(2,1)S(1)} %get-tuple-element.40.rest_0_), custom_call_target="tpu_custom_call" | custom-call | flops 7864320 | bytes 524288 | tf_op jit(solution)/shard_map/pallas_call | solution.py:476
  39.3 1.5 %collective-permute-start.15 = (bf16[72,512]{1,0:T(8,128)(2,1)S(1)}, bf16[72,512]{1,0:T(8,128)(2,1)S(1)}, u32[]{:S(2)}, u32[]{:S(2)}) collective-permute-start(bf16[72,512]{1,0:T(8,128)(2,1)S(1)} %shard_map.64.message.rest_0_), channel_id=1, source_target_pairs={{0,3},{1,2},{2,1},{3,0},{4,7},{5,6},{6,5},{7,4},{8,11},{9,10},{10,... | collective-permute-start | bytes 221192 | tf_op jit(solution)/shard_map/ppermute | solution.py:38
  40.8 1.5 %collective-permute-start.14 = (bf16[72,512]{1,0:T(8,128)(2,1)S(1)}, bf16[72,512]{1,0:T(8,128)(2,1)S(1)}, u32[]{:S(2)}, u32[]{:S(2)}) collective-permute-start(bf16[72,512]{1,0:T(8,128)(2,1)S(1)} %shard_map.64.message.rest_0_), channel_id=1, source_target_pairs={{0,2},{1,3},{2,0},{3,1},{4,6},{5,7},{6,4},{7,5},{8,10},{9,11},{10,... | collective-permute-start | bytes 221192 | tf_op jit(solution)/shard_map/ppermute | solution.py:38
  42.3 0.5 %collective-permute-start.13 = (bf16[72,512]{1,0:T(8,128)(2,1)S(1)}, bf16[72,512]{1,0:T(8,128)(2,1)S(1)}, u32[]{:S(2)}, u32[]{:S(2)}) collective-permute-start(bf16[72,512]{1,0:T(8,128)(2,1)S(1)} %shard_map.64.message.rest_0_), channel_id=1, source_target_pairs={{0,1},{1,0},{2,3},{3,2},{4,5},{5,4},{6,7},{7,6},{8,9},{9,8},{10,11... | collective-permute-start | bytes 221192 | tf_op jit(solution)/shard_map/ppermute | solution.py:38
  42.8 1.7 %shard_map.66 = (f32[4,64,512]{2,1,0:T(8,128)S(1)}, f32[4,64,512]{2,1,0:T(8,128)S(1)}) custom-call(s32[64,128]{1,0:T(8,128)S(1)} %get-tuple-element.28.base, bf16[72,512]{1,0:T(8,128)(2,1)S(1)} %shard_map.64.message.rest_0_), custom_call_target="tpu_custom_call" | custom-call | flops 15728640 | bytes 1048576 | tf_op jit(solution)/shard_map/pallas_call | solution.py:476
  44.5 0.7 %shard_map.65.partial = f32[512,512]{1,0:T(8,128)S(1)} custom-call(f32[8,512]{1,0:T(8,128)S(1)} %get-tuple-element.26.coup, f32[1,512]{1,0:T(1,128)S(1)} %get-tuple-element.27.spec, bf16[2048,512]{1,0:T(8,128)(2,1)S(1)} %copy-done, f32[8,64,512]{2,1,0:T(8,128)S(1)} %shard_map.57.noise, bf16[72,512]{1,0:T(8,128)(2,1)S(1)} %shard_map.64.message.rest_0_), custom_call_target="tpu_custom_call" | custom-call | flops 268435456 | bytes 1048576 | tf_op jit(solution)/shard_map/pallas_call | solution.py:539
  45.2 1.0 %collective-permute-done.14.rest_11_ = bf16[72,512]{1,0:T(8,128)(2,1)S(1)} collective-permute-done((bf16[72,512]{1,0:T(8,128)(2,1)S(1)}, bf16[72,512]{1,0:T(8,128)(2,1)S(1)}, u32[]{:S(2)}, u32[]{:S(2)}) %collective-permute-start.14) | collective-permute-done | bytes 73760 | tf_op jit(solution)/shard_map/ppermute | solution.py:38
  46.1 0.5 collective-permute-done.13.rest_10_
  46.6 2.8 %shard_map.67 = f32[512,512]{1,0:T(8,128)} custom-call(f32[512,512]{1,0:T(8,128)S(1)} %shard_map.65.partial, bf16[320,512]{1,0:T(8,128)(2,1)S(1)} %collective-permute-done.9.rest_0_, bf16[576,512]{1,0:T(8,128)(2,1)S(1)} %collective-permute-done.10.rest_1_, bf16[320,512]{1,0:T(8,128)(2,1)S(1)} %collective-permute-done.11.rest_2_, ...), custom_call_target="tpu_custom_call" | custom-call | flops 805306368 | bytes 3145728 | tf_op jit(solution)/shard_map/pallas_call | solution.py:555
  (23 shorter events, 1.6 us)
Async XLA Ops:
  0.0 1.7 %collective-permute-start = (f32[8,512]{1,0:T(8,128)}, f32[8,512]{1,0:T(8,128)S(1)}, u32[]{:S(2)}, u32[]{:S(2)}) collective-permute-start(f32[8,512]{1,0:T(8,128)} %coup.1), channel_id=1, source_target_pairs={{0,4},{4,0},{8,12},{12,8},{16,20},{20,16},{24,28},{28,24},{1,5},{5... | collective-permute-start | bytes 49160 | tf_op jit(solution)/shard_map/ppermute | solution.py:38
  2.0 14.0 %collective-permute-start.10 = (bf16[576,512]{1,0:T(8,128)(2,1)S(1)}, bf16[576,512]{1,0:T(8,128)(2,1)S(1)}, u32[]{:S(2)}, u32[]{:S(2)}) collective-permute-start(bf16[576,512]{1,0:T(8,128)(2,1)S(1)} %get-tuple-element.43), channel_id=1, source_target_pairs={{0,1},{1,0},{2,3},{3,2},{4,6},{5,7},{6,4},{7,5},{8,9},{9,8},{10,11... | collective-permute-start | bytes 1769480 | tf_op jit(solution)/shard_map/ppermute | solution.py:33
  4.7 16.4 %collective-permute-start.9 = (bf16[320,512]{1,0:T(8,128)(2,1)S(1)}, bf16[320,512]{1,0:T(8,128)(2,1)S(1)}, u32[]{:S(2)}, u32[]{:S(2)}) collective-permute-start(bf16[320,512]{1,0:T(8,128)(2,1)S(1)} %get-tuple-element.42), channel_id=1, source_target_pairs={{0,3},{1,2},{2,1},{3,0},{4,7},{5,6},{6,5},{7,4},{8,11},{9,10},{10,... | collective-permute-start | bytes 983048 | tf_op jit(solution)/shard_map/ppermute | solution.py:33
  16.0 30.6 %collective-permute-start.12 = (bf16[576,512]{1,0:T(8,128)(2,1)S(1)}, bf16[576,512]{1,0:T(8,128)(2,1)S(1)}, u32[]{:S(2)}, u32[]{:S(2)}) collective-permute-start(bf16[576,512]{1,0:T(8,128)(2,1)S(1)} %collective-permute-done.10.rest_1_), channel_id=1, source_target_pairs={{0,4},{4,0},{8,12},{12,8},{16,20},{20,16},{24,28},{28,24},{1,5},{5... | collective-permute-start | bytes 1769480 | tf_op jit(solution)/shard_map/ppermute | solution.py:38
  21.0 25.6 %collective-permute-start.11 = (bf16[320,512]{1,0:T(8,128)(2,1)S(1)}, bf16[320,512]{1,0:T(8,128)(2,1)S(1)}, u32[]{:S(2)}, u32[]{:S(2)}) collective-permute-start(bf16[320,512]{1,0:T(8,128)(2,1)S(1)} %collective-permute-done.9.rest_0_), channel_id=1, source_target_pairs={{0,4},{4,0},{8,12},{12,8},{16,20},{20,16},{24,28},{28,24},{1,5},{5... | collective-permute-start | bytes 983048 | tf_op jit(solution)/shard_map/ppermute | solution.py:38
  21.0 5.6 %collective-permute-start.3 = (f32[8,512]{1,0:T(8,128)S(1)}, f32[8,512]{1,0:T(8,128)S(1)}, u32[]{:S(2)}, u32[]{:S(2)}) collective-permute-start(f32[8,512]{1,0:T(8,128)S(1)} %get-tuple-element.32._.table), channel_id=1, source_target_pairs={{0,24},{4,28},{8,16},{12,20},{16,8},{20,12},{24,0},{28,4},{1,25},{... | collective-permute-start | bytes 49160 | tf_op jit(solution)/shard_map/ppermute | solution.py:38
  24.6 4.6 %collective-permute-start.2 = (f32[8,512]{1,0:T(8,128)S(1)}, f32[8,512]{1,0:T(8,128)S(1)}, u32[]{:S(2)}, u32[]{:S(2)}) collective-permute-start(f32[8,512]{1,0:T(8,128)S(1)} %get-tuple-element.32._.table), channel_id=1, source_target_pairs={{0,16},{4,20},{8,24},{12,28},{16,0},{20,4},{24,8},{28,12},{1,17},{... | collective-permute-start | bytes 49160 | tf_op jit(solution)/shard_map/ppermute | solution.py:38
  24.6 4.6 %collective-permute-start.1 = (f32[8,512]{1,0:T(8,128)S(1)}, f32[8,512]{1,0:T(8,128)S(1)}, u32[]{:S(2)}, u32[]{:S(2)}) collective-permute-start(f32[8,512]{1,0:T(8,128)S(1)} %get-tuple-element.32._.table), channel_id=1, source_target_pairs={{0,8},{4,12},{8,0},{12,4},{16,24},{20,28},{24,16},{28,20},{1,9},{5... | collective-permute-start | bytes 49160 | tf_op jit(solution)/shard_map/ppermute | solution.py:38
  29.5 1.3 %collective-permute-start.4 = (bf16[64,512]{1,0:T(8,128)(2,1)S(1)}, bf16[64,512]{1,0:T(8,128)(2,1)S(1)}, u32[]{:S(2)}, u32[]{:S(2)}) collective-permute-start(bf16[64,512]{1,0:T(8,128)(2,1)S(1)} %get-tuple-element.35), channel_id=1, source_target_pairs={{0,4},{4,0},{8,12},{12,8},{16,20},{20,16},{24,28},{28,24},{1,5},{5... | collective-permute-start | bytes 196616 | tf_op jit(solution)/shard_map/ppermute | solution.py:38
  30.9 7.0 %collective-permute-start.7 = (bf16[32,512]{1,0:T(8,128)(2,1)S(1)}, bf16[32,512]{1,0:T(8,128)(2,1)S(1)}, u32[]{:S(2)}, u32[]{:S(2)}) collective-permute-start(bf16[32,512]{1,0:T(8,128)(2,1)S(1)} %get-tuple-element.37.rest_0_), channel_id=1, source_target_pairs={{0,24},{4,28},{8,16},{12,20},{16,8},{20,12},{24,0},{28,4},{1,25},{... | collective-permute-start | bytes 98312 | tf_op jit(solution)/shard_map/ppermute | solution.py:38
  32.4 5.4 %collective-permute-start.6 = (bf16[32,512]{1,0:T(8,128)(2,1)S(1)}, bf16[32,512]{1,0:T(8,128)(2,1)S(1)}, u32[]{:S(2)}, u32[]{:S(2)}) collective-permute-start(bf16[32,512]{1,0:T(8,128)(2,1)S(1)} %get-tuple-element.37.rest_0_), channel_id=1, source_target_pairs={{0,16},{4,20},{8,24},{12,28},{16,0},{20,4},{24,8},{28,12},{1,17},{... | collective-permute-start | bytes 98312 | tf_op jit(solution)/shard_map/ppermute | solution.py:38
  33.1 4.8 %collective-permute-start.5 = (bf16[32,512]{1,0:T(8,128)(2,1)S(1)}, bf16[32,512]{1,0:T(8,128)(2,1)S(1)}, u32[]{:S(2)}, u32[]{:S(2)}) collective-permute-start(bf16[32,512]{1,0:T(8,128)(2,1)S(1)} %get-tuple-element.37.rest_0_), channel_id=1, source_target_pairs={{0,8},{4,12},{8,0},{12,4},{16,24},{20,28},{24,16},{28,20},{1,9},{5... | collective-permute-start | bytes 98312 | tf_op jit(solution)/shard_map/ppermute | solution.py:38
  37.0 7.5 %copy-start = (bf16[2048,512]{1,0:T(8,128)(2,1)S(1)}, bf16[2048,512]{1,0:T(8,128)(2,1)}, u32[]{:S(2)}) copy-start(bf16[2048,512]{1,0:T(8,128)(2,1)} %basis.3) | copy-start | bytes 6291460
  37.9 1.3 %collective-permute-start.8 = (bf16[32,512]{1,0:T(8,128)(2,1)S(1)}, bf16[32,512]{1,0:T(8,128)(2,1)S(1)}, u32[]{:S(2)}, u32[]{:S(2)}) collective-permute-start(bf16[32,512]{1,0:T(8,128)(2,1)S(1)} %get-tuple-element.40.rest_0_), channel_id=1, source_target_pairs={{0,4},{4,0},{8,12},{12,8},{16,20},{20,16},{24,28},{28,24},{1,5},{5... | collective-permute-start | bytes 98312 | tf_op jit(solution)/shard_map/ppermute | solution.py:38
  39.3 5.9 %collective-permute-start.15 = (bf16[72,512]{1,0:T(8,128)(2,1)S(1)}, bf16[72,512]{1,0:T(8,128)(2,1)S(1)}, u32[]{:S(2)}, u32[]{:S(2)}) collective-permute-start(bf16[72,512]{1,0:T(8,128)(2,1)S(1)} %shard_map.64.message.rest_0_), channel_id=1, source_target_pairs={{0,3},{1,2},{2,1},{3,0},{4,7},{5,6},{6,5},{7,4},{8,11},{9,10},{10,... | collective-permute-start | bytes 221192 | tf_op jit(solution)/shard_map/ppermute | solution.py:38
  40.8 5.4 %collective-permute-start.14 = (bf16[72,512]{1,0:T(8,128)(2,1)S(1)}, bf16[72,512]{1,0:T(8,128)(2,1)S(1)}, u32[]{:S(2)}, u32[]{:S(2)}) collective-permute-start(bf16[72,512]{1,0:T(8,128)(2,1)S(1)} %shard_map.64.message.rest_0_), channel_id=1, source_target_pairs={{0,2},{1,3},{2,0},{3,1},{4,6},{5,7},{6,4},{7,5},{8,10},{9,11},{10,... | collective-permute-start | bytes 221192 | tf_op jit(solution)/shard_map/ppermute | solution.py:38
  42.3 4.4 %collective-permute-start.13 = (bf16[72,512]{1,0:T(8,128)(2,1)S(1)}, bf16[72,512]{1,0:T(8,128)(2,1)S(1)}, u32[]{:S(2)}, u32[]{:S(2)}) collective-permute-start(bf16[72,512]{1,0:T(8,128)(2,1)S(1)} %shard_map.64.message.rest_0_), channel_id=1, source_target_pairs={{0,1},{1,0},{2,3},{3,2},{4,5},{5,4},{6,7},{7,6},{8,9},{9,8},{10,11... | collective-permute-start | bytes 221192 | tf_op jit(solution)/shard_map/ppermute | solution.py:38

commit v7 on v6

--- a/solution.py
+++ b/solution.py
@@ -386,12 +386,12 @@
     for j, (x, y) in enumerate(pairs):
         i = len(single) + j
         rows = direct[i].shape[0] - TAIL
-        near = lambda i=i, rows=rows: direct[i][pl.ds(0, rows), :]
-        far = lambda i=i, rows=rows: swapped[i][pl.ds(0, rows), :]
+        near = lambda at=pl.ds(0, rows), i=i: direct[i][at, :]
+        far = lambda at=pl.ds(0, rows), i=i: swapped[i][at, :]
         items.append((near, direct[i], noise[len(single) + j], chosen(x - 1, y - 1)))
         items.append((far, swapped[i], noise[len(single) + len(pairs) + j], chosen(y - 1, x - 1)))
     for i, d in enumerate(single):
-        items.append((lambda i=i: lhs[i], direct[i], noise[i], chosen(d - 1, d - 1)))
+        items.append((lambda at=slice(None), i=i: lhs[i, at, :], direct[i], noise[i], chosen(d - 1, d - 1)))
     for n, (_, source, _, message) in enumerate(items):
         rows = source.shape[0] - TAIL
         x = [source[pl.ds(rows + 16 * j, 16), :].astype(F32) for j in range(4)]
@@ -415,12 +415,17 @@
         if h == 0 and n == count - len(single):
             for copy in copies:
                 copy.wait()
-        term = product(items[n][0](), rhs[h, n])
         at = pl.ds((1 - h) * width, width)
-        result[h] = (partial[:, at] if n == 0 else result[h]) + term
-        if n == count - 1:
-            outs.append(pltpu.make_async_copy(result.at[h], out.at[:, at], sems.at[2 * len(single) + h]))
-            outs[-1].start()
+        rows = result.shape[1]
+        ends = n == count - 1 and h == 1
+        for part in range(2 if ends else 1):
+            take = pl.ds(part * (rows // 2), rows // 2) if ends else pl.ds(0, rows)
+            term = product(items[n][0](take), rhs[h, n])
+            result[h, take, :] = (partial[take, at] if n == 0 else result[h, take, :]) + term
+            if n == count - 1:
+                slot = 2 * len(single) + h + part
+                outs.append(pltpu.make_async_copy(result.at[h, take, :], out.at[take, at], sems.at[slot]))
+                outs[-1].start()
     for copy in outs:
         copy.wait()
 
@@ -563,7 +568,7 @@
             pltpu.VMEM((count, vecs, modes), F32),
             pltpu.VMEM((count, 2, steps, modes), F32),
             pltpu.VMEM((2, nodes_here, half_cols), F32),
-            pltpu.SemaphoreType.DMA((2 * len(single) + 2,)),
+            pltpu.SemaphoreType.DMA((2 * len(single) + 3,)),
         ],
         cost_estimate=pl.CostEstimate(
             flops=flops * count, transcendentals=0, bytes_accessed=4 * steps * vecs * modes * count

time: 49.6 us -> 49.5 us (level)
  no operation moved by 1% of the time
where the time goes in v7:
time: 49.5 us; the launch traced here: 49.4 us
  waiting for transfers between devices  20.5 us (41%)
  starting transfers between devices  17.2 us (35%)
  Pallas kernels  11.5 us (23%)
    ppermute x2, waiting for transfers between devices, exchange(): return lax.ppermute(x, ('tm', 'space'), moves)  14.9 us
    ppermute x14, starting transfers between devices, swap(): return lax.ppermute(x, axis, [(i, i ^ offset) for i in range(count)])  13 us
    ppermute x14, waiting for transfers between devices, swap(): return lax.ppermute(x, axis, [(i, i ^ offset) for i in range(count)])  5.66 us
    pallas_call x4, Pallas kernels, noise_of(): kernel_call(functools.partial(noise_kernel, 'tm', 'space', parts, steps,...  4.99 us
    ppermute x2, starting transfers between devices, exchange(): return lax.ppermute(x, ('tm', 'space'), moves)  4.16 us
    pallas_call x1, Pallas kernels, local(): kernel_call(functools.partial(final_kernel, 'tm', pairs, single), out_sha...  2.71 us
    pallas_call x1, Pallas kernels, local(): kernel_call(functools.partial(chip_kernel, 'tm', 'space'), out_shape=f32(...  1.25 us
    pallas_call x1, Pallas kernels, local(): kernel_call(functools.partial(pack_kernel, 'tm', 'space', routes), out_sh...  1.24 us
  transfers between devices with their start and end apart: 16, of which 7 were waited for; matrix products, arithmetic and copies ran while one was open for 0% of the time, Pallas kernels for 17%

profile of v7, /device:TPU:0, one launch (start us, length us, event | category | flops | bytes accessed | tf_op | source)
XLA Modules:
  0.0 49.4 jit_solution(5286983357207591560)
XLA Ops:
  0.5 1.2 %shard_map.55 = (bf16[320,512]{1,0:T(8,128)(2,1)S(1)}, bf16[576,512]{1,0:T(8,128)(2,1)S(1)}, f32[8,512]{1,0:T(8,128)S(1)}, f32[1,512]{1,0:T(1,128)S(1)}, s32[64,...) custom-call(f32[8,512]{1,0:T(8,128)} %coup.1, f32[1,512]{1,0:T(1,128)} %bitcast.3, bf16[2048,512]{1,0:T(8,128)(2,1)} %basis.3, ...), custom_call_target="tpu_custom_call" | custom-call | tf_op jit(solution)/shard_map/pallas_call | solution.py:457
  2.0 2.7 %collective-permute-start.10 = (bf16[576,512]{1,0:T(8,128)(2,1)S(1)}, bf16[576,512]{1,0:T(8,128)(2,1)S(1)}, u32[]{:S(2)}, u32[]{:S(2)}) collective-permute-start(bf16[576,512]{1,0:T(8,128)(2,1)S(1)} %get-tuple-element.43), channel_id=1, source_target_pairs={{0,1},{1,0},{2,3},{3,2},{4,6},{5,7},{6,4},{7,5},{8,9},{9,8},{10,11... | collective-permute-start | bytes 1769480 | tf_op jit(solution)/shard_map/ppermute | solution.py:33
  4.7 1.5 %collective-permute-start.9 = (bf16[320,512]{1,0:T(8,128)(2,1)S(1)}, bf16[320,512]{1,0:T(8,128)(2,1)S(1)}, u32[]{:S(2)}, u32[]{:S(2)}) collective-permute-start(bf16[320,512]{1,0:T(8,128)(2,1)S(1)} %get-tuple-element.42), channel_id=1, source_target_pairs={{0,3},{1,2},{2,1},{3,0},{4,7},{5,6},{6,5},{7,4},{8,11},{9,10},{10,... | collective-permute-start | bytes 983048 | tf_op jit(solution)/shard_map/ppermute | solution.py:33
  6.2 9.9 %collective-permute-done.10.rest_1_ = bf16[576,512]{1,0:T(8,128)(2,1)S(1)} collective-permute-done((bf16[576,512]{1,0:T(8,128)(2,1)S(1)}, bf16[576,512]{1,0:T(8,128)(2,1)S(1)}, u32[]{:S(2)}, u32[]{:S(2)}) %collective-permute-start.10) | collective-permute-done | bytes 589856 | tf_op jit(solution)/shard_map/ppermute | solution.py:33
  16.0 5.0 %collective-permute-done.9.rest_0_ = bf16[320,512]{1,0:T(8,128)(2,1)S(1)} collective-permute-done((bf16[320,512]{1,0:T(8,128)(2,1)S(1)}, bf16[320,512]{1,0:T(8,128)(2,1)S(1)}, u32[]{:S(2)}, u32[]{:S(2)}) %collective-permute-start.9) | collective-permute-done | bytes 327712 | tf_op jit(solution)/shard_map/ppermute | solution.py:33
  21.0 3.6 %collective-permute-start.3 = (f32[8,512]{1,0:T(8,128)S(1)}, f32[8,512]{1,0:T(8,128)S(1)}, u32[]{:S(2)}, u32[]{:S(2)}) collective-permute-start(f32[8,512]{1,0:T(8,128)S(1)} %get-tuple-element.32._.table), channel_id=1, source_target_pairs={{0,24},{4,28},{8,16},{12,20},{16,8},{20,12},{24,0},{28,4},{1,25},{... | collective-permute-start | bytes 49160 | tf_op jit(solution)/shard_map/ppermute | solution.py:38
  24.6 0.8 %collective-permute-start.1 = (f32[8,512]{1,0:T(8,128)S(1)}, f32[8,512]{1,0:T(8,128)S(1)}, u32[]{:S(2)}, u32[]{:S(2)}) collective-permute-start(f32[8,512]{1,0:T(8,128)S(1)} %get-tuple-element.32._.table), channel_id=1, source_target_pairs={{0,8},{4,12},{8,0},{12,4},{16,24},{20,28},{24,16},{28,20},{1,9},{5... | collective-permute-start | bytes 49160 | tf_op jit(solution)/shard_map/ppermute | solution.py:38
  25.4 1.3 %shard_map.57.noise = f32[8,64,512]{2,1,0:T(8,128)S(1)} custom-call(s32[64,128]{1,0:T(8,128)S(1)} %get-tuple-element.28.base, f32[2,64,512]{2,1,0:T(8,128)S(1)} %get-tuple-element.29.early, f32[8,512]{1,0:T(8,128)S(1)} %get-tuple-element.32._.table), custom_call_target="tpu_custom_call" | custom-call | tf_op jit(solution)/shard_map/pallas_call | solution.py:493
  26.7 2.6 %collective-permute-done.2.rest_1_ = f32[8,512]{1,0:T(8,128)S(1)} collective-permute-done((f32[8,512]{1,0:T(8,128)S(1)}, f32[8,512]{1,0:T(8,128)S(1)}, u32[]{:S(2)}, u32[]{:S(2)}) %collective-permute-start.2) | collective-permute-done | bytes 16416 | tf_op jit(solution)/shard_map/ppermute | solution.py:38
  29.6 1.2 %collective-permute-done.4.other = bf16[64,512]{1,0:T(8,128)(2,1)S(1)} collective-permute-done((bf16[64,512]{1,0:T(8,128)(2,1)S(1)}, bf16[64,512]{1,0:T(8,128)(2,1)S(1)}, u32[]{:S(2)}, u32[]{:S(2)}) %collective-permute-start.4) | collective-permute-done | bytes 65568 | tf_op jit(solution)/shard_map/ppermute | solution.py:38
  30.9 1.5 %collective-permute-start.7 = (bf16[32,512]{1,0:T(8,128)(2,1)S(1)}, bf16[32,512]{1,0:T(8,128)(2,1)S(1)}, u32[]{:S(2)}, u32[]{:S(2)}) collective-permute-start(bf16[32,512]{1,0:T(8,128)(2,1)S(1)} %get-tuple-element.37.rest_0_), channel_id=1, source_target_pairs={{0,24},{4,28},{8,16},{12,20},{16,8},{20,12},{24,0},{28,4},{1,25},{... | collective-permute-start | bytes 98312 | tf_op jit(solution)/shard_map/ppermute | solution.py:38
  32.4 0.6 %collective-permute-start.6 = (bf16[32,512]{1,0:T(8,128)(2,1)S(1)}, bf16[32,512]{1,0:T(8,128)(2,1)S(1)}, u32[]{:S(2)}, u32[]{:S(2)}) collective-permute-start(bf16[32,512]{1,0:T(8,128)(2,1)S(1)} %get-tuple-element.37.rest_0_), channel_id=1, source_target_pairs={{0,16},{4,20},{8,24},{12,28},{16,0},{20,4},{24,8},{28,12},{1,17},{... | collective-permute-start | bytes 98312 | tf_op jit(solution)/shard_map/ppermute | solution.py:38
  33.1 2.3 %collective-permute-start.5 = (bf16[32,512]{1,0:T(8,128)(2,1)S(1)}, bf16[32,512]{1,0:T(8,128)(2,1)S(1)}, u32[]{:S(2)}, u32[]{:S(2)}) collective-permute-start(bf16[32,512]{1,0:T(8,128)(2,1)S(1)} %get-tuple-element.37.rest_0_), channel_id=1, source_target_pairs={{0,8},{4,12},{8,0},{12,4},{16,24},{20,28},{24,16},{28,20},{1,9},{5... | collective-permute-start | bytes 98312 | tf_op jit(solution)/shard_map/ppermute | solution.py:38
  35.4 1.7 %shard_map.60 = (f32[4,64,512]{2,1,0:T(8,128)S(1)}, f32[4,64,512]{2,1,0:T(8,128)S(1)}) custom-call(s32[64,128]{1,0:T(8,128)S(1)} %get-tuple-element.28.base, bf16[32,512]{1,0:T(8,128)(2,1)S(1)} %get-tuple-element.37.rest_0_), custom_call_target="tpu_custom_call" | custom-call | flops 15728640 | bytes 1048576 | tf_op jit(solution)/shard_map/pallas_call | solution.py:481
  37.0 0.8 %shard_map.61.rest_3_.rest_6_ = f32[4,64,512]{2,1,0:T(8,128)S(1)} custom-call(s32[64,128]{1,0:T(8,128)S(1)} %get-tuple-element.28.base, f32[4,64,512]{2,1,0:T(8,128)S(1)} %get-tuple-element.38.rest_0_.rest_5_), custom_call_target="tpu_custom_call" | custom-call | flops 7864320 | bytes 524288 | tf_op jit(solution)/shard_map/pallas_call | solution.py:481
  38.0 0.8 %shard_map.63._.rest_7_ = f32[4,64,512]{2,1,0:T(8,128)S(1)} custom-call(s32[64,128]{1,0:T(8,128)S(1)} %get-tuple-element.28.base, bf16[32,512]{1,0:T(8,128)(2,1)S(1)} %get-tuple-element.40.rest_0_), custom_call_target="tpu_custom_call" | custom-call | flops 7864320 | bytes 524288 | tf_op jit(solution)/shard_map/pallas_call | solution.py:481
  39.3 1.5 %collective-permute-start.15 = (bf16[72,512]{1,0:T(8,128)(2,1)S(1)}, bf16[72,512]{1,0:T(8,128)(2,1)S(1)}, u32[]{:S(2)}, u32[]{:S(2)}) collective-permute-start(bf16[72,512]{1,0:T(8,128)(2,1)S(1)} %shard_map.64.message.rest_0_), channel_id=1, source_target_pairs={{0,3},{1,2},{2,1},{3,0},{4,7},{5,6},{6,5},{7,4},{8,11},{9,10},{10,... | collective-permute-start | bytes 221192 | tf_op jit(solution)/shard_map/ppermute | solution.py:38
  40.8 1.5 %collective-permute-start.14 = (bf16[72,512]{1,0:T(8,128)(2,1)S(1)}, bf16[72,512]{1,0:T(8,128)(2,1)S(1)}, u32[]{:S(2)}, u32[]{:S(2)}) collective-permute-start(bf16[72,512]{1,0:T(8,128)(2,1)S(1)} %shard_map.64.message.rest_0_), channel_id=1, source_target_pairs={{0,2},{1,3},{2,0},{3,1},{4,6},{5,7},{6,4},{7,5},{8,10},{9,11},{10,... | collective-permute-start | bytes 221192 | tf_op jit(solution)/shard_map/ppermute | solution.py:38
  42.3 0.5 %collective-permute-start.13 = (bf16[72,512]{1,0:T(8,128)(2,1)S(1)}, bf16[72,512]{1,0:T(8,128)(2,1)S(1)}, u32[]{:S(2)}, u32[]{:S(2)}) collective-permute-start(bf16[72,512]{1,0:T(8,128)(2,1)S(1)} %shard_map.64.message.rest_0_), channel_id=1, source_target_pairs={{0,1},{1,0},{2,3},{3,2},{4,5},{5,4},{6,7},{7,6},{8,9},{9,8},{10,11... | collective-permute-start | bytes 221192 | tf_op jit(solution)/shard_map/ppermute | solution.py:38
  42.8 1.7 %shard_map.66 = (f32[4,64,512]{2,1,0:T(8,128)S(1)}, f32[4,64,512]{2,1,0:T(8,128)S(1)}) custom-call(s32[64,128]{1,0:T(8,128)S(1)} %get-tuple-element.28.base, bf16[72,512]{1,0:T(8,128)(2,1)S(1)} %shard_map.64.message.rest_0_), custom_call_target="tpu_custom_call" | custom-call | flops 15728640 | bytes 1048576 | tf_op jit(solution)/shard_map/pallas_call | solution.py:481
  44.5 0.7 %shard_map.65.partial = f32[512,512]{1,0:T(8,128)S(1)} custom-call(f32[8,512]{1,0:T(8,128)S(1)} %get-tuple-element.26.coup, f32[1,512]{1,0:T(1,128)S(1)} %get-tuple-element.27.spec, bf16[2048,512]{1,0:T(8,128)(2,1)S(1)} %copy-done, f32[8,64,512]{2,1,0:T(8,128)S(1)} %shard_map.57.noise, bf16[72,512]{1,0:T(8,128)(2,1)S(1)} %shard_map.64.message.rest_0_), custom_call_target="tpu_custom_call" | custom-call | flops 268435456 | bytes 1048576 | tf_op jit(solution)/shard_map/pallas_call | solution.py:544
  45.2 1.0 %collective-permute-done.14.rest_11_ = bf16[72,512]{1,0:T(8,128)(2,1)S(1)} collective-permute-done((bf16[72,512]{1,0:T(8,128)(2,1)S(1)}, bf16[72,512]{1,0:T(8,128)(2,1)S(1)}, u32[]{:S(2)}, u32[]{:S(2)}) %collective-permute-start.14) | collective-permute-done | bytes 73760 | tf_op jit(solution)/shard_map/ppermute | solution.py:38
  46.1 0.5 collective-permute-done.13.rest_10_
  46.6 2.7 %shard_map.67 = f32[512,512]{1,0:T(8,128)} custom-call(f32[512,512]{1,0:T(8,128)S(1)} %shard_map.65.partial, bf16[320,512]{1,0:T(8,128)(2,1)S(1)} %collective-permute-done.9.rest_0_, bf16[576,512]{1,0:T(8,128)(2,1)S(1)} %collective-permute-done.10.rest_1_, bf16[320,512]{1,0:T(8,128)(2,1)S(1)} %collective-permute-done.11.rest_2_, ...), custom_call_target="tpu_custom_call" | custom-call | flops 805306368 | bytes 3145728 | tf_op jit(solution)/shard_map/pallas_call | solution.py:560
  (23 shorter events, 1.6 us)
Async XLA Ops:
  0.0 1.7 %collective-permute-start = (f32[8,512]{1,0:T(8,128)}, f32[8,512]{1,0:T(8,128)S(1)}, u32[]{:S(2)}, u32[]{:S(2)}) collective-permute-start(f32[8,512]{1,0:T(8,128)} %coup.1), channel_id=1, source_target_pairs={{0,4},{4,0},{8,12},{12,8},{16,20},{20,16},{24,28},{28,24},{1,5},{5... | collective-permute-start | bytes 49160 | tf_op jit(solution)/shard_map/ppermute | solution.py:38
  2.0 14.0 %collective-permute-start.10 = (bf16[576,512]{1,0:T(8,128)(2,1)S(1)}, bf16[576,512]{1,0:T(8,128)(2,1)S(1)}, u32[]{:S(2)}, u32[]{:S(2)}) collective-permute-start(bf16[576,512]{1,0:T(8,128)(2,1)S(1)} %get-tuple-element.43), channel_id=1, source_target_pairs={{0,1},{1,0},{2,3},{3,2},{4,6},{5,7},{6,4},{7,5},{8,9},{9,8},{10,11... | collective-permute-start | bytes 1769480 | tf_op jit(solution)/shard_map/ppermute | solution.py:33
  4.7 16.4 %collective-permute-start.9 = (bf16[320,512]{1,0:T(8,128)(2,1)S(1)}, bf16[320,512]{1,0:T(8,128)(2,1)S(1)}, u32[]{:S(2)}, u32[]{:S(2)}) collective-permute-start(bf16[320,512]{1,0:T(8,128)(2,1)S(1)} %get-tuple-element.42), channel_id=1, source_target_pairs={{0,3},{1,2},{2,1},{3,0},{4,7},{5,6},{6,5},{7,4},{8,11},{9,10},{10,... | collective-permute-start | bytes 983048 | tf_op jit(solution)/shard_map/ppermute | solution.py:33
  16.0 30.6 %collective-permute-start.12 = (bf16[576,512]{1,0:T(8,128)(2,1)S(1)}, bf16[576,512]{1,0:T(8,128)(2,1)S(1)}, u32[]{:S(2)}, u32[]{:S(2)}) collective-permute-start(bf16[576,512]{1,0:T(8,128)(2,1)S(1)} %collective-permute-done.10.rest_1_), channel_id=1, source_target_pairs={{0,4},{4,0},{8,12},{12,8},{16,20},{20,16},{24,28},{28,24},{1,5},{5... | collective-permute-start | bytes 1769480 | tf_op jit(solution)/shard_map/ppermute | solution.py:38
  21.0 25.6 %collective-permute-start.11 = (bf16[320,512]{1,0:T(8,128)(2,1)S(1)}, bf16[320,512]{1,0:T(8,128)(2,1)S(1)}, u32[]{:S(2)}, u32[]{:S(2)}) collective-permute-start(bf16[320,512]{1,0:T(8,128)(2,1)S(1)} %collective-permute-done.9.rest_0_), channel_id=1, source_target_pairs={{0,4},{4,0},{8,12},{12,8},{16,20},{20,16},{24,28},{28,24},{1,5},{5... | collective-permute-start | bytes 983048 | tf_op jit(solution)/shard_map/ppermute | solution.py:38
  21.0 5.6 %collective-permute-start.3 = (f32[8,512]{1,0:T(8,128)S(1)}, f32[8,512]{1,0:T(8,128)S(1)}, u32[]{:S(2)}, u32[]{:S(2)}) collective-permute-start(f32[8,512]{1,0:T(8,128)S(1)} %get-tuple-element.32._.table), channel_id=1, source_target_pairs={{0,24},{4,28},{8,16},{12,20},{16,8},{20,12},{24,0},{28,4},{1,25},{... | collective-permute-start | bytes 49160 | tf_op jit(solution)/shard_map/ppermute | solution.py:38
  24.6 4.6 %collective-permute-start.2 = (f32[8,512]{1,0:T(8,128)S(1)}, f32[8,512]{1,0:T(8,128)S(1)}, u32[]{:S(2)}, u32[]{:S(2)}) collective-permute-start(f32[8,512]{1,0:T(8,128)S(1)} %get-tuple-element.32._.table), channel_id=1, source_target_pairs={{0,16},{4,20},{8,24},{12,28},{16,0},{20,4},{24,8},{28,12},{1,17},{... | collective-permute-start | bytes 49160 | tf_op jit(solution)/shard_map/ppermute | solution.py:38
  24.6 4.6 %collective-permute-start.1 = (f32[8,512]{1,0:T(8,128)S(1)}, f32[8,512]{1,0:T(8,128)S(1)}, u32[]{:S(2)}, u32[]{:S(2)}) collective-permute-start(f32[8,512]{1,0:T(8,128)S(1)} %get-tuple-element.32._.table), channel_id=1, source_target_pairs={{0,8},{4,12},{8,0},{12,4},{16,24},{20,28},{24,16},{28,20},{1,9},{5... | collective-permute-start | bytes 49160 | tf_op jit(solution)/shard_map/ppermute | solution.py:38
  29.5 1.3 %collective-permute-start.4 = (bf16[64,512]{1,0:T(8,128)(2,1)S(1)}, bf16[64,512]{1,0:T(8,128)(2,1)S(1)}, u32[]{:S(2)}, u32[]{:S(2)}) collective-permute-start(bf16[64,512]{1,0:T(8,128)(2,1)S(1)} %get-tuple-element.35), channel_id=1, source_target_pairs={{0,4},{4,0},{8,12},{12,8},{16,20},{20,16},{24,28},{28,24},{1,5},{5... | collective-permute-start | bytes 196616 | tf_op jit(solution)/shard_map/ppermute | solution.py:38
  30.9 7.0 %collective-permute-start.7 = (bf16[32,512]{1,0:T(8,128)(2,1)S(1)}, bf16[32,512]{1,0:T(8,128)(2,1)S(1)}, u32[]{:S(2)}, u32[]{:S(2)}) collective-permute-start(bf16[32,512]{1,0:T(8,128)(2,1)S(1)} %get-tuple-element.37.rest_0_), channel_id=1, source_target_pairs={{0,24},{4,28},{8,16},{12,20},{16,8},{20,12},{24,0},{28,4},{1,25},{... | collective-permute-start | bytes 98312 | tf_op jit(solution)/shard_map/ppermute | solution.py:38
  32.4 5.4 %collective-permute-start.6 = (bf16[32,512]{1,0:T(8,128)(2,1)S(1)}, bf16[32,512]{1,0:T(8,128)(2,1)S(1)}, u32[]{:S(2)}, u32[]{:S(2)}) collective-permute-start(bf16[32,512]{1,0:T(8,128)(2,1)S(1)} %get-tuple-element.37.rest_0_), channel_id=1, source_target_pairs={{0,16},{4,20},{8,24},{12,28},{16,0},{20,4},{24,8},{28,12},{1,17},{... | collective-permute-start | bytes 98312 | tf_op jit(solution)/shard_map/ppermute | solution.py:38
  33.1 4.8 %collective-permute-start.5 = (bf16[32,512]{1,0:T(8,128)(2,1)S(1)}, bf16[32,512]{1,0:T(8,128)(2,1)S(1)}, u32[]{:S(2)}, u32[]{:S(2)}) collective-permute-start(bf16[32,512]{1,0:T(8,128)(2,1)S(1)} %get-tuple-element.37.rest_0_), channel_id=1, source_target_pairs={{0,8},{4,12},{8,0},{12,4},{16,24},{20,28},{24,16},{28,20},{1,9},{5... | collective-permute-start | bytes 98312 | tf_op jit(solution)/shard_map/ppermute | solution.py:38
  37.0 7.5 %copy-start = (bf16[2048,512]{1,0:T(8,128)(2,1)S(1)}, bf16[2048,512]{1,0:T(8,128)(2,1)}, u32[]{:S(2)}) copy-start(bf16[2048,512]{1,0:T(8,128)(2,1)} %basis.3) | copy-start | bytes 6291460
  37.9 1.3 %collective-permute-start.8 = (bf16[32,512]{1,0:T(8,128)(2,1)S(1)}, bf16[32,512]{1,0:T(8,128)(2,1)S(1)}, u32[]{:S(2)}, u32[]{:S(2)}) collective-permute-start(bf16[32,512]{1,0:T(8,128)(2,1)S(1)} %get-tuple-element.40.rest_0_), channel_id=1, source_target_pairs={{0,4},{4,0},{8,12},{12,8},{16,20},{20,16},{24,28},{28,24},{1,5},{5... | collective-permute-start | bytes 98312 | tf_op jit(solution)/shard_map/ppermute | solution.py:38
  39.3 5.9 %collective-permute-start.15 = (bf16[72,512]{1,0:T(8,128)(2,1)S(1)}, bf16[72,512]{1,0:T(8,128)(2,1)S(1)}, u32[]{:S(2)}, u32[]{:S(2)}) collective-permute-start(bf16[72,512]{1,0:T(8,128)(2,1)S(1)} %shard_map.64.message.rest_0_), channel_id=1, source_target_pairs={{0,3},{1,2},{2,1},{3,0},{4,7},{5,6},{6,5},{7,4},{8,11},{9,10},{10,... | collective-permute-start | bytes 221192 | tf_op jit(solution)/shard_map/ppermute | solution.py:38
  40.8 5.4 %collective-permute-start.14 = (bf16[72,512]{1,0:T(8,128)(2,1)S(1)}, bf16[72,512]{1,0:T(8,128)(2,1)S(1)}, u32[]{:S(2)}, u32[]{:S(2)}) collective-permute-start(bf16[72,512]{1,0:T(8,128)(2,1)S(1)} %shard_map.64.message.rest_0_), channel_id=1, source_target_pairs={{0,2},{1,3},{2,0},{3,1},{4,6},{5,7},{6,4},{7,5},{8,10},{9,11},{10,... | collective-permute-start | bytes 221192 | tf_op jit(solution)/shard_map/ppermute | solution.py:38
  42.3 4.4 %collective-permute-start.13 = (bf16[72,512]{1,0:T(8,128)(2,1)S(1)}, bf16[72,512]{1,0:T(8,128)(2,1)S(1)}, u32[]{:S(2)}, u32[]{:S(2)}) collective-permute-start(bf16[72,512]{1,0:T(8,128)(2,1)S(1)} %shard_map.64.message.rest_0_), channel_id=1, source_target_pairs={{0,1},{1,0},{2,3},{3,2},{4,5},{5,4},{6,7},{7,6},{8,9},{9,8},{10,11... | collective-permute-start | bytes 221192 | tf_op jit(solution)/shard_map/ppermute | solution.py:38
